TPU v7x, 128 devices: a whole 4x4x4 slice. The times are simulated.
128 devices in a mesh: bond: 32 (over y, x, core), mpo: 4 (over z).
Axes of the slice: x: 4, y: 4, z: 4, core: 2. Of those that a mesh axis runs over, the one named last changes fastest.
Arguments:
- carried: bfloat16 [198, 8192], P(None, 'bond'), may hold values from -6 to 6
- site_tensors: bfloat16 [2, 8192, 4, 8192], P(None, 'bond', 'mpo'), may hold values from -0.125 to 0.125
- operator_tensors: bfloat16 [2, 4, 66, 264], replicated, may hold values from -0.375 to 0.375
- rotation: bfloat16 [2, 8192, 4, 8192], P(None, 'bond', 'mpo'), may hold values from -0.125 to 0.125
- kept_columns: int32 [2, 8192], replicated, may hold values from 0 to 32767, as said below
Outputs:
- rotated_state: bfloat16 [198, 8192], P(None, 'bond')
- truncation_gram: float32 [2, 198, 198], replicated
Inputs may be any that keep to these rules, and one draw needn't show every extreme that they name: `kept_columns`: each row holds 8192 distinct values; value r * 4 + t names right-bond index r and physical index t.
All inputs are finite; a program needn't handle non-finite values.
Results may differ from a plain program's by a relative error of at most 0.035.
Values may be sent and summed in bfloat16 or wider, within the bound.
No kernel may reach another device: no remote copies, remote signals or barrier semaphores. Data moves between devices by JAX's collectives and lax.ppermute only.
A program may use at most 128 MiB of HBM per device.

v0:
```python
import jax
import jax.numpy as jnp
from jax import lax
from jax.sharding import Mesh
from jax.sharding import PartitionSpec as P

BOND_DIM = 8192
PHYSICAL = 4
MPO_BOND = 66
LEFT_ROWS = 3
SITE_COUNT = 2
BOND = ("bond_0", "bond_1", "bond_2")


def cut_along(array, dim, count):
    dims = array.shape
    parts = array.reshape(*dims[:dim], count, dims[dim] // count, *dims[dim + 1 :])
    return jnp.moveaxis(parts, dim, 0)


def sent_and_summed(array, axis, dim):
    count = lax.axis_size(axis)
    parts = lax.all_to_all(cut_along(array, dim, count), axis, 0, 0, tiled=True)
    return jnp.sum(parts.astype(jnp.float32), axis=0)


def summed_rows(array, axes, dim):
    far, near = axes
    parts = cut_along(array, dim, lax.axis_size(far))
    nearer = sent_and_summed(parts, near, dim + 1)
    arrived = lax.all_to_all(
        nearer.astype(jnp.bfloat16), far, split_axis=0, concat_axis=0, tiled=True
    )
    return arrived.astype(jnp.float32).sum(axis=0)


def rows_for(lines, count):
    spare = -len(lines) % count
    return jnp.pad(lines, [(0, spare)] + [(0, 0)] * (lines.ndim - 1))


def from_everyone(array, axis):
    count = lax.axis_size(axis)
    return lax.all_to_all(
        jnp.broadcast_to(array[None], (count, *array.shape)), axis, 0, 0, tiled=True
    )


def laid_out(parts, dim):
    parts = jnp.moveaxis(parts, 0, dim)
    dims = parts.shape
    return parts.reshape(*dims[:dim], dims[dim] * dims[dim + 1], *dims[dim + 2 :])


def gathered_by_axis(array, axes, dim):
    far, near = axes
    initial = from_everyone(array, far)
    parts = jnp.swapaxes(from_everyone(initial, near), 0, 1)
    return laid_out(parts.reshape(-1, *array.shape), dim)


def sent_and_summed_2(array, axis, dim):
    parts = cut_along(array, dim, lax.axis_size(axis))
    arrived = lax.all_to_all(parts, axis, split_axis=0, concat_axis=0, tiled=True)
    return arrived.sum(axis=0)


def sum_in_two_steps(array, axes, dim):
    far, near = axes
    own = sent_and_summed_2(cut_along(array, dim, lax.axis_size(far)), near, dim + 1)
    return jnp.sum(lax.all_to_all(own, far, 0, 0, tiled=True), axis=0)


def total_of(array, axes):
    lines = array.reshape(-1)
    padded = rows_for(lines, lax.axis_size(axes[0]) * lax.axis_size(axes[1]))
    whole = gathered_by_axis(sum_in_two_steps(padded, axes, 0), axes, 0)
    return lax.slice_in_dim(whole, 0, len(lines)).reshape(array.shape)


def of_everyone(array, axis):
    everything = from_everyone(array, axis)
    return jnp.sum(everything.astype(jnp.float32), axis=0)


def on_device(carried, site_tensors, operator_tensors, rotation, kept_columns):
    row_count = carried.shape[0]
    bond_block = carried.shape[1]
    phys_local = site_tensors.shape[2]
    state = carried
    gram_list = []
    for position in range(SITE_COUNT):
        tensor = site_tensors[position].reshape(bond_block, phys_local * BOND_DIM)
        partial_sum = jnp.dot(state, tensor, preferred_element_type=jnp.float32)
        partial_sum = partial_sum.reshape(row_count, phys_local, BOND_DIM)
        summed = summed_rows(partial_sum.astype(jnp.bfloat16), (("bond_0", "bond_1"), "bond_2"), 2)
        contracted = summed.astype(jnp.bfloat16).reshape(
            LEFT_ROWS, MPO_BOND, phys_local, bond_block
        )
        weights = lax.dynamic_slice_in_dim(
            operator_tensors[position], lax.axis_index("mpo") * phys_local, phys_local, 0
        )
        mixed_rows = jnp.einsum(
            "lasr,sac->lcr", contracted, weights, preferred_element_type=jnp.float32
        )
        mixed_rows = mixed_rows.reshape(LEFT_ROWS, PHYSICAL, MPO_BOND, bond_block)
        mixed_rows = sent_and_summed(mixed_rows.astype(jnp.bfloat16), "mpo", 1)
        out_local = mixed_rows.shape[1]
        chosen = jnp.zeros((PHYSICAL * BOND_DIM,), jnp.float32).at[kept_columns[position]].set(1.0)
        chosen = chosen.reshape(BOND_DIM, PHYSICAL)
        chosen = lax.dynamic_slice(
            chosen,
            (lax.axis_index(BOND) * bond_block, lax.axis_index("mpo") * out_local),
            (bond_block, out_local),
        )
        kept_rows = (mixed_rows * chosen.T[None, :, None, :]).astype(jnp.bfloat16)
        gram_matrix = jnp.einsum(
            "ltar,mtbr->lamb", kept_rows, kept_rows, preferred_element_type=jnp.float32
        )
        gram_matrix = gram_matrix.reshape(row_count, row_count) / BOND_DIM
        gram_list.append(total_of(gram_matrix, (("bond_0", "bond_1"), ("bond_2", "mpo"))))
        rotated = jnp.einsum(
            "ltbr,rtq->lbq", kept_rows, rotation[position], preferred_element_type=jnp.float32
        )
        rotated = rotated.reshape(row_count, BOND_DIM)
        rotated_part = summed_rows(
            rotated.astype(jnp.bfloat16), (("bond_0", "bond_1"), "bond_2"), 1
        )
        rotated_part = of_everyone(rotated_part.astype(jnp.bfloat16), "mpo").astype(jnp.float32)
        state = rotated_part.astype(jnp.bfloat16)
    return (state, jnp.stack(gram_list))


def solution(mesh):
    finer = Mesh(
        mesh.devices.reshape(4, 4, 2, mesh.shape["mpo"]), ("bond_0", "bond_1", "bond_2", "mpo")
    )
    placed = (P(None, BOND), P(None, BOND, "mpo", None), P(), P(None, BOND, "mpo", None), P())
    return jax.shard_map(
        on_device, mesh=finer, in_specs=placed, out_specs=(P(None, BOND), P()), check_vma=False
    )
```

profile of v0, /device:TPU:1, one launch (start us, length us, event | category | flops | bytes accessed | tf_op | source)
XLA Modules:
  0.0 399.6 jit_solution(7494521204436369601)
XLA Ops:
  11.9 7.3 %all_to_all.110 = bf16[2,16,198,1,256]{4,1,2,3,0:T(8,128)(2,1)S(1)} all-to-all(bf16[2,16,198,1,256]{4,1,2,3,0:T(8,128)(2,1)S(1)} %copy.86), channel_id=1, replica_groups=mesh['bond_0'=4,'bond_1'=4,'bond_2'=2,'mpo'=4] {'bond_2'}, dimensions={0} | all-to-all | bytes 6488064 | tf_op jit(solution)/shard_map/all_to_all | solution.py:23
  24.7 6.9 %all-to-all-start.1 = ((bf16[16,198,1,256]{3,1,2,0:T(8,128)(2,1)}), bf16[16,198,1,256]{3,1,2,0:T(8,128)(2,1)S(1)}, u32[]{:S(2)}, u32[]{:S(2)}) async-start(bf16[16,198,1,256]{3,1,2,0:T(8,128)(2,1)} %copy.88), calls=%async_computation.1 | async-start | bytes 3276800 | tf_op jit(solution)/shard_map/all_to_all | solution.py:31
  32.6 24.2 %all-to-all-done.1 = bf16[16,198,1,256]{3,1,2,0:T(8,128)(2,1)S(1)} async-done(((bf16[16,198,1,256]{3,1,2,0:T(8,128)(2,1)}), bf16[16,198,1,256]{3,1,2,0:T(8,128)(2,1)S(1)}, u32[]{:S(2)}, u32[]{:S(2)}) %all-to-all-start.1) | async-done | bytes 1622048 | tf_op jit(solution)/shard_map/all_to_all | solution.py:31
  58.3 5.0 %all-to-all-start.2 = ((bf16[4,3,1,66,256]{4,3,1,2,0:T(8,128)(2,1)}), bf16[4,3,1,66,256]{4,3,1,2,0:T(8,128)(2,1)S(1)}, u32[]{:S(2)}, u32[]{:S(2)}) async-start(bf16[4,3,1,66,256]{4,3,1,2,0:T(8,128)(2,1)} %copy.89), calls=%async_computation.2 | async-start | bytes 884736 | tf_op jit(solution)/shard_map/all_to_all | solution.py:23
  64.0 30.7 %scatter_custom_fusion = f32[32768]{0:T(1024)S(1)} fusion(s32[8192]{0:T(1024)S(1)} %bitcast.124, f32[8192]{0:T(1024)S(1)} %broadcast.186, f32[]{:T(128)} %constant.43.clone.1), kind=kCustom, calls=%fused_computation.35 | custom fusion | bytes 131076 | tf_op jit(solution)/shard_map/scatter | solution.py:109
  94.7 5.6 %reshape.387 = f32[8192,4]{1,0:T(8,128)} reshape(f32[32768]{0:T(1024)S(1)} %scatter_custom_fusion) | data formatting | bytes 262144 | tf_op jit(solution)/shard_map/reshape | solution.py:110
  112.0 7.7 %all_to_all.111 = bf16[2,16,198,256]{3,1,2,0:T(8,128)(2,1)S(1)} all-to-all(bf16[2,16,198,256]{3,1,2,0:T(8,128)(2,1)S(1)} %copy.90), channel_id=1, replica_groups=mesh['bond_0'=4,'bond_1'=4,'bond_2'=2,'mpo'=4] {'bond_2'}, dimensions={0} | all-to-all | bytes 6488064 | tf_op jit(solution)/shard_map/all_to_all | solution.py:23
  123.9 25.3 %all_to_all.112 = bf16[16,198,256]{2,1,0:T(8,128)(2,1)S(1)} all-to-all(bf16[16,198,256]{2,1,0:T(8,128)(2,1)S(1)} %copy.92), channel_id=1, replica_groups=mesh['bond_0'=4,'bond_1'=4,'bond_2'=2,'mpo'=4] {'bond_0','bond_1'}, dimensions={0} | all-to-all | bytes 3244032 | tf_op jit(solution)/shard_map/all_to_all | solution.py:31
  156.2 4.8 %all-to-all-done.5 = bf16[4,198,256]{2,1,0:T(8,128)(2,1)S(1)} async-done(((bf16[4,198,256]{2,1,0:T(8,128)(2,1)}), bf16[4,198,256]{2,1,0:T(8,128)(2,1)S(1)}, u32[]{:S(2)}, u32[]{:S(2)}) %all-to-all-start.5) | async-done | bytes 405536 | tf_op jit(solution)/shard_map/all_to_all | solution.py:44
  171.5 9.1 %all_to_all.113 = bf16[2,16,198,1,256]{4,1,2,3,0:T(8,128)(2,1)S(1)} all-to-all(bf16[2,16,198,1,256]{4,1,2,3,0:T(8,128)(2,1)S(1)} %copy.94), channel_id=1, replica_groups=mesh['bond_0'=4,'bond_1'=4,'bond_2'=2,'mpo'=4] {'bond_2'}, dimensions={0} | all-to-all | bytes 6488064 | tf_op jit(solution)/shard_map/all_to_all | solution.py:23
  194.9 25.1 %all-to-all-done.7 = bf16[16,198,1,256]{3,1,2,0:T(8,128)(2,1)S(1)} async-done(((bf16[16,198,1,256]{3,1,2,0:T(8,128)(2,1)}), bf16[16,198,1,256]{3,1,2,0:T(8,128)(2,1)S(1)}, u32[]{:S(2)}, u32[]{:S(2)}) %all-to-all-start.7) | async-done | bytes 1622048 | tf_op jit(solution)/shard_map/all_to_all | solution.py:31
  225.0 4.9 %all-to-all-done.13 = f32[16,1,307]{2,1,0:T(1,128)S(1)} async-done(((f32[16,1,307]{2,1,0:T(1,128)}), f32[16,1,307]{2,1,0:T(1,128)S(1)}, u32[]{:S(2)}, u32[]{:S(2)}) %all-to-all-start.13) | async-done | bytes 19680 | tf_op jit(solution)/shard_map/all_to_all | solution.py:71
  233.8 30.6 %scatter_custom_fusion.1 = f32[32768]{0:T(1024)S(1)} fusion(s32[8192]{0:T(1024)} %bitcast.123, f32[8192]{0:T(1024)} %copy-done.5, f32[]{:T(128)} %constant.43.clone.1), kind=kCustom, calls=%fused_computation.33 | custom fusion | bytes 131584 | tf_op jit(solution)/shard_map/scatter | solution.py:109
  264.4 5.6 %reshape.394 = f32[8192,4]{1,0:T(8,128)} reshape(f32[32768]{0:T(1024)S(1)} %scatter_custom_fusion.1) | data formatting | bytes 262144 | tf_op jit(solution)/shard_map/reshape | solution.py:110
  276.9 4.7 %all-to-all-done.14 = f32[16,1,307]{2,1,0:T(1,128)S(1)} async-done(((f32[16,1,307]{2,1,0:T(1,128)}), f32[16,1,307]{2,1,0:T(1,128)S(1)}, u32[]{:S(2)}, u32[]{:S(2)}) %all-to-all-start.14) | async-done | bytes 19680 | tf_op jit(solution)/shard_map/all_to_all | solution.py:44
  281.7 8.6 %all-to-all-start.16 = ((f32[8,16,307]{2,1,0:T(8,128)}), f32[8,16,307]{2,1,0:T(8,128)S(1)}, u32[]{:S(2)}, u32[]{:S(2)}) async-start(f32[8,16,307]{2,1,0:T(8,128)} %copy.104), calls=%async_computation.16 | async-start | bytes 393216 | tf_op jit(solution)/shard_map/all_to_all | solution.py:64
  290.3 5.8 %all-to-all-done.16 = f32[8,16,307]{2,1,0:T(8,128)S(1)} async-done(((f32[8,16,307]{2,1,0:T(8,128)}), f32[8,16,307]{2,1,0:T(8,128)S(1)}, u32[]{:S(2)}, u32[]{:S(2)}) %all-to-all-start.16) | async-done | bytes 157216 | tf_op jit(solution)/shard_map/all_to_all | solution.py:64
  307.3 5.4 %all-to-all-start.15 = ((f32[8,16,307]{2,1,0:T(8,128)}), f32[8,16,307]{2,1,0:T(8,128)}, u32[]{:S(2)}, u32[]{:S(2)}) async-start(f32[8,16,307]{2,1,0:T(8,128)} %broadcast_in_dim.20), calls=%async_computation.15 | async-start | bytes 393216 | tf_op jit(solution)/shard_map/all_to_all | solution.py:44
  314.8 7.6 %reshape.397 = bf16[16,198,2,256]{3,2,0,1:T(2,128)(2,1)} reshape(bf16[16,198,512]{2,0,1:T(8,128)(2,1)} %slice_bitcast_fusion) | data formatting | bytes 6488064 | tf_op jit(solution)/shard_map/reshape | solution.py:17
  324.8 7.1 %all_to_all.114 = bf16[2,16,198,256]{3,1,2,0:T(8,128)(2,1)} all-to-all(bf16[2,16,198,256]{3,1,2,0:T(8,128)(2,1)S(1)} %copy.98), channel_id=1, replica_groups=mesh['bond_0'=4,'bond_1'=4,'bond_2'=2,'mpo'=4] {'bond_2'}, dimensions={0} | all-to-all | bytes 6488064 | tf_op jit(solution)/shard_map/all_to_all | solution.py:23
  343.2 5.7 %all-to-all-start.10 = ((bf16[16,198,256]{2,1,0:T(8,128)(2,1)}), bf16[16,198,256]{2,1,0:T(8,128)(2,1)S(1)}, u32[]{:S(2)}, u32[]{:S(2)}) async-start(bf16[16,198,256]{2,1,0:T(8,128)(2,1)} %copy.100), calls=%async_computation.10 | async-start | bytes 3276800 | tf_op jit(solution)/shard_map/all_to_all | solution.py:31
  348.9 23.2 %all-to-all-done.10 = bf16[16,198,256]{2,1,0:T(8,128)(2,1)S(1)} async-done(((bf16[16,198,256]{2,1,0:T(8,128)(2,1)}), bf16[16,198,256]{2,1,0:T(8,128)(2,1)S(1)}, u32[]{:S(2)}, u32[]{:S(2)}) %all-to-all-start.10) | async-done | bytes 1622048 | tf_op jit(solution)/shard_map/all_to_all | solution.py:31
  372.8 7.6 %all-to-all-start.19 = ((f32[8,16,307]{2,1,0:T(8,128)}), f32[8,16,307]{2,1,0:T(8,128)S(1)}, u32[]{:S(2)}, u32[]{:S(2)}) async-start(f32[8,16,307]{2,1,0:T(8,128)} %broadcast_in_dim.23), calls=%async_computation.19 | async-start | bytes 393216 | tf_op jit(solution)/shard_map/all_to_all | solution.py:44
  380.7 5.6 %all-to-all-done.19 = f32[8,16,307]{2,1,0:T(8,128)S(1)} async-done(((f32[8,16,307]{2,1,0:T(8,128)}), f32[8,16,307]{2,1,0:T(8,128)S(1)}, u32[]{:S(2)}, u32[]{:S(2)}) %all-to-all-start.19) | async-done | bytes 157216 | tf_op jit(solution)/shard_map/all_to_all | solution.py:44
  (114 shorter events, 123.7 us)
Async XLA Ops:
  0.6 0.9 copy-start
  21.5 10.1 %copy-start.3 = (bf16[2,4,66,264]{3,1,2,0:T(4,128)(2,1)S(1)}, bf16[2,4,66,264]{3,1,2,0:T(4,128)(2,1)}, u32[]{:S(2)}) copy-start(bf16[2,4,66,264]{3,1,2,0:T(4,128)(2,1)} %param.7) | copy-start | bytes 836356
  24.7 32.1 %all-to-all-start.1 = ((bf16[16,198,1,256]{3,1,2,0:T(8,128)(2,1)}), bf16[16,198,1,256]{3,1,2,0:T(8,128)(2,1)S(1)}, u32[]{:S(2)}, u32[]{:S(2)}) async-start(bf16[16,198,1,256]{3,1,2,0:T(8,128)(2,1)} %copy.88), calls=%async_computation.1 | async-start | bytes 3276800 | tf_op jit(solution)/shard_map/all_to_all | solution.py:31
  31.6 31.7 %copy-start.4 = (s32[2,8192]{1,0:T(2,128)S(1)}, s32[2,8192]{1,0:T(2,128)}, u32[]{:S(2)}) copy-start(s32[2,8192]{1,0:T(2,128)} %param.9) | copy-start | bytes 196612
  58.3 43.1 %all-to-all-start.2 = ((bf16[4,3,1,66,256]{4,3,1,2,0:T(8,128)(2,1)}), bf16[4,3,1,66,256]{4,3,1,2,0:T(8,128)(2,1)S(1)}, u32[]{:S(2)}, u32[]{:S(2)}) async-start(bf16[4,3,1,66,256]{4,3,1,2,0:T(8,128)(2,1)} %copy.89), calls=%async_computation.2 | async-start | bytes 884736 | tf_op jit(solution)/shard_map/all_to_all | solution.py:23
  64.0 37.5 %copy-start.5 = (f32[8192]{0:T(1024)}, f32[8192]{0:T(1024)S(1)}, u32[]{:S(2)}) copy-start(f32[8192]{0:T(1024)S(1)} %broadcast.186) | copy-start | bytes 98308
  150.2 10.8 %all-to-all-start.5 = ((bf16[4,198,256]{2,1,0:T(8,128)(2,1)}), bf16[4,198,256]{2,1,0:T(8,128)(2,1)S(1)}, u32[]{:S(2)}, u32[]{:S(2)}) async-start(bf16[4,198,256]{2,1,0:T(8,128)(2,1)} %broadcast_in_dim.16), calls=%async_computation.5 | async-start | bytes 819200 | tf_op jit(solution)/shard_map/all_to_all | solution.py:44
  180.6 9.8 %all-to-all-start.12 = ((f32[8,16,307]{2,1,0:T(8,128)}), f32[8,16,307]{2,1,0:T(8,128)S(1)}, u32[]{:S(2)}, u32[]{:S(2)}) async-start(f32[8,16,307]{2,1,0:T(8,128)} %copy.102), calls=%async_computation.12 | async-start | bytes 393216 | tf_op jit(solution)/shard_map/all_to_all | solution.py:64
  186.8 7.3 %copy-start.2 = (bf16[1,4,66,264]{3,1,2,0:T(4,128)(2,1)S(1)}, bf16[1,4,66,264]{3,1,2,0:T(4,128)(2,1)}, u32[]{:S(2)}) copy-start(bf16[1,4,66,264]{3,1,2,0:T(4,128)(2,1)} %get-tuple-element.14) | copy-start | bytes 418180
  190.4 29.6 %all-to-all-start.7 = ((bf16[16,198,1,256]{3,1,2,0:T(8,128)(2,1)}), bf16[16,198,1,256]{3,1,2,0:T(8,128)(2,1)S(1)}, u32[]{:S(2)}, u32[]{:S(2)}) async-start(bf16[16,198,1,256]{3,1,2,0:T(8,128)(2,1)} %copy.96), calls=%async_computation.7 | async-start | bytes 3276800 | tf_op jit(solution)/shard_map/all_to_all | solution.py:31
  220.0 9.9 %all-to-all-start.13 = ((f32[16,1,307]{2,1,0:T(1,128)}), f32[16,1,307]{2,1,0:T(1,128)S(1)}, u32[]{:S(2)}, u32[]{:S(2)}) async-start(f32[16,1,307]{2,1,0:T(1,128)} %all_to_all.81), calls=%async_computation.13 | async-start | bytes 49152 | tf_op jit(solution)/shard_map/all_to_all | solution.py:71
  229.9 41.3 %all-to-all-start.8 = ((bf16[4,3,1,66,256]{4,3,1,2,0:T(8,128)(2,1)}), bf16[4,3,1,66,256]{4,3,1,2,0:T(8,128)(2,1)S(1)}, u32[]{:S(2)}, u32[]{:S(2)}) async-start(bf16[4,3,1,66,256]{4,3,1,2,0:T(8,128)(2,1)} %copy.97), calls=%async_computation.8 | async-start | bytes 884736 | tf_op jit(solution)/shard_map/all_to_all | solution.py:23
  271.8 9.9 %all-to-all-start.14 = ((f32[16,1,307]{2,1,0:T(1,128)}), f32[16,1,307]{2,1,0:T(1,128)S(1)}, u32[]{:S(2)}, u32[]{:S(2)}) async-start(f32[16,1,307]{2,1,0:T(1,128)} %broadcast_in_dim.18), calls=%async_computation.14 | async-start | bytes 49152 | tf_op jit(solution)/shard_map/all_to_all | solution.py:44
  281.7 14.4 %all-to-all-start.16 = ((f32[8,16,307]{2,1,0:T(8,128)}), f32[8,16,307]{2,1,0:T(8,128)S(1)}, u32[]{:S(2)}, u32[]{:S(2)}) async-start(f32[8,16,307]{2,1,0:T(8,128)} %copy.104), calls=%async_computation.16 | async-start | bytes 393216 | tf_op jit(solution)/shard_map/all_to_all | solution.py:64
  296.8 9.9 %all-to-all-start.17 = ((f32[16,1,307]{2,1,0:T(1,128)}), f32[16,1,307]{2,1,0:T(1,128)S(1)}, u32[]{:S(2)}, u32[]{:S(2)}) async-start(f32[16,1,307]{2,1,0:T(1,128)} %all_to_all.86), calls=%async_computation.17 | async-start | bytes 49152 | tf_op jit(solution)/shard_map/all_to_all | solution.py:71
  307.3 17.5 %all-to-all-start.15 = ((f32[8,16,307]{2,1,0:T(8,128)}), f32[8,16,307]{2,1,0:T(8,128)}, u32[]{:S(2)}, u32[]{:S(2)}) async-start(f32[8,16,307]{2,1,0:T(8,128)} %broadcast_in_dim.20), calls=%async_computation.15 | async-start | bytes 393216 | tf_op jit(solution)/shard_map/all_to_all | solution.py:44
  332.5 10.7 %all-to-all-start.18 = ((f32[16,1,307]{2,1,0:T(1,128)}), f32[16,1,307]{2,1,0:T(1,128)S(1)}, u32[]{:S(2)}, u32[]{:S(2)}) async-start(f32[16,1,307]{2,1,0:T(1,128)} %broadcast_in_dim.21), calls=%async_computation.18 | async-start | bytes 49152 | tf_op jit(solution)/shard_map/all_to_all | solution.py:44
  343.2 28.9 %all-to-all-start.10 = ((bf16[16,198,256]{2,1,0:T(8,128)(2,1)}), bf16[16,198,256]{2,1,0:T(8,128)(2,1)S(1)}, u32[]{:S(2)}, u32[]{:S(2)}) async-start(bf16[16,198,256]{2,1,0:T(8,128)(2,1)} %copy.100), calls=%async_computation.10 | async-start | bytes 3276800 | tf_op jit(solution)/shard_map/all_to_all | solution.py:31
  372.8 13.5 %all-to-all-start.19 = ((f32[8,16,307]{2,1,0:T(8,128)}), f32[8,16,307]{2,1,0:T(8,128)S(1)}, u32[]{:S(2)}, u32[]{:S(2)}) async-start(f32[8,16,307]{2,1,0:T(8,128)} %broadcast_in_dim.23), calls=%async_computation.19 | async-start | bytes 393216 | tf_op jit(solution)/shard_map/all_to_all | solution.py:44
  380.5 18.7 %copy-start.1 = (bf16[198,256]{1,0:T(8,128)(2,1)S(1)}, bf16[198,256]{1,0:T(8,128)(2,1)}, u32[]{:S(2)}) copy-start(bf16[198,256]{1,0:T(8,128)(2,1)} %param.5) | copy-start | bytes 304132
  387.0 11.4 %all-to-all-start.11 = ((bf16[4,198,256]{2,1,0:T(8,128)(2,1)}), bf16[4,198,256]{2,1,0:T(8,128)(2,1)S(1)}, u32[]{:S(2)}, u32[]{:S(2)}) async-start(bf16[4,198,256]{2,1,0:T(8,128)(2,1)} %broadcast_in_dim.17), calls=%async_computation.11 | async-start | bytes 819200 | tf_op jit(solution)/shard_map/all_to_all | solution.py:44
where the time goes:
time: 407 us; the launch traced here: 400 us
  local copies, waits for them, and re-layouts  135 us (33%)
  waiting for transfers between devices  106 us (26%)
  starting transfers between devices  73.5 us (18%)
  blocking collectives  56.5 us (14%)
  matrix products  13.8 us (3%)
  other arithmetic  13 us (3%)
    all_to_all x3, waiting for transfers between devices, summed_rows(): lax.all_to_all(nearer.astype(jnp.bfloat16), far, split_axis=0, concat_axi...  72.6 us
    scatter x2, local copies, waits for them, and re-layouts, on_device(): jnp.zeros((PHYSICAL * BOND_DIM,), jnp.float32).at[kept_columns[position]]  61.3 us
    all_to_all x4, blocking collectives, sent_and_summed(): parts = lax.all_to_all(cut_along(array, dim, count), axis, 0, 0, tiled=True)  31.2 us
    all_to_all x6, starting transfers between devices, from_everyone(): lax.all_to_all(jnp.broadcast_to(array[None], (count, *array.shape)), axis...  28.8 us
    all_to_all x1, blocking collectives, summed_rows(): lax.all_to_all(nearer.astype(jnp.bfloat16), far, split_axis=0, concat_axi...  25.3 us
    all_to_all x6, waiting for transfers between devices, from_everyone(): lax.all_to_all(jnp.broadcast_to(array[None], (count, *array.shape)), axis...  20.9 us
    reshape x4, local copies, waits for them, and re-layouts, cut_along(): array.reshape(*dims[:dim], count, dims[dim] // count, *dims[dim + 1:])  16.7 us
    all_to_all x3, starting transfers between devices, summed_rows(): lax.all_to_all(nearer.astype(jnp.bfloat16), far, split_axis=0, concat_axi...  16.3 us
  transfers between devices with their start and end apart: 15, of which 12 were waited for; matrix products, arithmetic and copies ran while one was open for 28% of the time, Pallas kernels for 0%

commit v1 on v0

v1 whole, which is shorter than its diff:
```python
import functools

import jax
import jax.numpy as jnp
from jax import lax
from jax.experimental import pallas as pl
from jax.experimental.pallas import tpu as pltpu
from jax.sharding import Mesh
from jax.sharding import PartitionSpec as P

BOND_DIM = 8192
PHYSICAL = 4
MPO_BOND = 66
LEFT_ROWS = 3
SITE_COUNT = 2
ROWS = LEFT_ROWS * MPO_BOND
BOND = ("y", "x", "core")
RING = 4
BLOCK = 256
F32 = jnp.float32
BF16 = jnp.bfloat16


def summed(terms):
    total = terms[0].astype(F32)
    for term in terms[1:]:
        total = total + term.astype(F32)
    return total


def chip_device(y, x, core):
    return (y % RING * RING + x % RING) * 2 + core


def shifts(step, x_core):
    pairs = []
    for y in range(RING):
        for x in range(RING):
            pairs.append((chip_device(y, x, x_core), chip_device(y, x + step, x_core)))
            other = 1 - x_core
            pairs.append((chip_device(y, x, other), chip_device(y + step, x, other)))
    return pairs


def ring_shift(step):
    return [(i, (i + step) % RING) for i in range(RING)]


def swap_cores(array):
    return lax.ppermute(array, "core", [(0, 1), (1, 0)])


def block_order(core):
    y, x = lax.axis_index("y"), lax.axis_index("x")
    far = jnp.repeat(jnp.arange(RING), RING)
    near = jnp.tile(jnp.arange(RING), RING)
    dy = jnp.where(core == 0, near, far)
    dx = jnp.where(core == 0, far, near)
    return (((y + dy) % RING * RING + (x + dx) % RING) * 2 + core).astype(jnp.int32)


def column_copy(site, order, weights, tiles, sems, i):
    first = pl.multiple_of(order[i] * BLOCK, BLOCK)
    source = weights.at[pl.ds(site * BLOCK, BLOCK), pl.ds(first, BLOCK)]
    return pltpu.make_async_copy(source, tiles.at[i], sems.at[i])


def start_columns(site, order, weights, tiles, sems):
    @pl.loop(0, RING * RING)
    def _(i):
        column_copy(site, order, weights, tiles, sems, i).start()

    return functools.partial(column_copy, site, order, weights, tiles, sems)


def multiply_columns(left, copies, tiles, outs):
    for d, out in enumerate(outs):

        @pl.loop(0, RING)
        def _(e, d=d, out=out):
            i = d * RING + e
            copies(i).wait()
            product = jnp.dot(left[...], tiles[i], preferred_element_type=F32)
            out[e] = product.astype(BF16)


def plain_kernel(site, order, left, weights, *rest):
    outs, (tiles, sems) = rest[:RING], rest[RING:]
    copies = start_columns(site, order, weights, tiles, sems)
    multiply_columns(left, copies, tiles, outs)


def sum_kernel(site, order, a, b, c, d, weights, state, *rest):
    outs, (tiles, sems) = rest[:RING], rest[RING:]
    copies = start_columns(site, order, weights, tiles, sems)
    state[...] = summed([a[...], b[...], c[...], d[...]]).astype(BF16)
    multiply_columns(state, copies, tiles, outs)


def mix_kernel(site, order, a, b, c, d, mixing, chosen, weights, kept, *rest):
    outs, (tiles, sems) = rest[:RING], rest[RING:]
    copies = start_columns(site, order, weights, tiles, sems)
    mixed = jnp.zeros((ROWS, BLOCK), F32)
    for i, part in enumerate((a, b, c, d)):
        mixed = mixed + jnp.dot(mixing[i], part[...], preferred_element_type=F32)
    kept[...] = (mixed * chosen[...]).astype(BF16)
    multiply_columns(kept, copies, tiles, outs)


def gram_kernel(site, order, left, weights, *rest):
    outs, gram, (tiles, sems) = rest[:RING], rest[RING], rest[RING + 1 :]
    copies = start_columns(site, order, weights, tiles, sems)
    multiply_columns(left, copies, tiles, outs)
    kept = left[...]
    whole = lax.dot_general(kept, kept, (((1,), (1,)), ((), ())), preferred_element_type=F32)
    gram[...] = (whole * (1.0 / BOND_DIM)).astype(BF16)


VMEM = pl.BlockSpec(memory_space=pltpu.VMEM)
PIECES = [jax.ShapeDtypeStruct((RING, ROWS, BLOCK), BF16)] * RING
SQUARE = jax.ShapeDtypeStruct((ROWS, ROWS), BF16)
TALL = jax.ShapeDtypeStruct((ROWS, BLOCK), BF16)


def call(kernel, site, order, operands, weights, before=(), after=()):
    shapes = [*before, *PIECES, *after]
    flops = 2 * ROWS * BLOCK * BLOCK * RING * RING
    return pl.pallas_call(
        functools.partial(kernel, site),
        out_shape=shapes,
        in_specs=[pl.BlockSpec(memory_space=pltpu.SMEM)]
        + [VMEM] * len(operands)
        + [pl.BlockSpec(memory_space=pl.ANY)],
        out_specs=[VMEM] * len(shapes),
        scratch_shapes=[
            pltpu.VMEM((RING * RING, BLOCK, BLOCK), BF16),
            pltpu.SemaphoreType.DMA((RING * RING,)),
        ],
        compiler_params=pltpu.CompilerParams(vmem_limit_bytes=24 * 2**20),
        cost_estimate=pl.CostEstimate(
            flops=flops, bytes_accessed=4 * 2**20, transcendentals=0
        ),
    )(order, *operands, weights)


def scattered(theirs, ours):
    arrived = [swap_cores(theirs[d]) for d in (2, 1, 3, 0)]
    mine = {d: summed([ours[d], got]).astype(BF16) for d, got in zip((2, 1, 3, 0), arrived)}
    got = [lax.ppermute(mine[d], BOND, shifts(d, 0)) for d in (2, 1, 3)]
    near = summed([mine[0], *got]).astype(BF16)
    got = [lax.ppermute(near[e], BOND, shifts(e, 1)) for e in (2, 1, 3)]
    return summed([near[0], *got]).astype(BF16)


def along_z(array):
    return [array] + [lax.ppermute(array, "z", ring_shift(d)) for d in (1, 2, 3)]


def mixing_weights(operator_tensors):
    z = lax.axis_index("z")
    turned = jnp.stack(
        [
            lax.dynamic_index_in_dim(operator_tensors, (z - d) % RING, 1, keepdims=False)
            for d in range(RING)
        ],
        1,
    )
    row = jnp.arange(ROWS)
    pick = (z * MPO_BOND + row[:, None] % MPO_BOND == jnp.arange(PHYSICAL * MPO_BOND)).astype(BF16)
    spread = (jnp.arange(MPO_BOND)[:, None] == row[None] % MPO_BOND).astype(BF16)
    narrow = jnp.einsum("xc,kdac->kdxa", pick, turned, preferred_element_type=F32).astype(BF16)
    wide = jnp.einsum("kdxa,aw->kdxw", narrow, spread, preferred_element_type=F32)
    same = row[:, None] // MPO_BOND == row[None] // MPO_BOND
    return jnp.where(same, wide, 0.0).astype(BF16)


def chosen_columns(kept_columns):
    first = lax.axis_index(BOND) * BLOCK * PHYSICAL
    place = kept_columns - first
    here = (place >= 0) & (place < BLOCK * PHYSICAL) & (place % PHYSICAL == lax.axis_index("z"))
    column = place // PHYSICAL
    digits = jnp.arange(16)[None, :, None]
    high = ((column // 16)[:, None] == digits) & here[:, None]
    low = (column % 16)[:, None] == digits
    counts = jnp.einsum(
        "khn,kln->khl", high.astype(BF16), low.astype(BF16), preferred_element_type=F32
    )
    return (counts > 0.5).astype(F32).reshape(SITE_COUNT, 1, BLOCK)


def total_grams(grams):
    core = lax.axis_index("core")
    own = jnp.where(core == 0, grams[0], grams[1])
    total = summed([own, swap_cores(jnp.where(core == 0, grams[1], grams[0]))]).astype(BF16)
    for axis in ("z", "x", "y"):
        got = [lax.ppermute(total, axis, ring_shift(d)) for d in (1, 2, 3)]
        total = summed([total, *got])
        if axis != "y":
            total = total.astype(BF16)
    other = swap_cores(total)
    return jnp.stack([jnp.where(core == 0, total, other), jnp.where(core == 0, other, total)])


def on_device(carried, site_tensors, operator_tensors, rotation, kept_columns):
    core = lax.axis_index("core")
    their_order, our_order = block_order(1 - core), block_order(core)
    tensors = site_tensors.reshape(SITE_COUNT * BLOCK, BOND_DIM)
    turns = rotation.reshape(SITE_COUNT * BLOCK, BOND_DIM)
    mixing = mixing_weights(operator_tensors)
    chosen = chosen_columns(kept_columns)
    grams, parts = [], None
    for site in range(SITE_COUNT):
        if parts is None:
            state = carried
            theirs = call(plain_kernel, site, their_order, [state], tensors)
        else:
            state, *theirs = call(sum_kernel, site, their_order, parts, tensors, before=[TALL])
        ours = call(plain_kernel, site, our_order, [state], tensors)
        parts = along_z(scattered(theirs, ours))
        kept, *theirs = call(
            mix_kernel, site, their_order, [*parts, mixing[site], chosen[site]], turns, before=[TALL]
        )
        *ours, gram = call(gram_kernel, site, our_order, [kept], turns, after=[SQUARE])
        grams.append(gram)
        parts = along_z(scattered(theirs, ours))
    return summed(parts).astype(BF16), total_grams(grams)


def solution(mesh):
    finer = Mesh(mesh.devices.reshape(RING, RING, 2, mesh.shape["mpo"]), (*BOND, "z"))
    placed = (P(None, BOND), P(None, BOND, "z", None), P(), P(None, BOND, "z", None), P())
    return jax.shard_map(
        on_device, mesh=finer, in_specs=placed, out_specs=(P(None, BOND), P()), check_vma=False
    )
```

time: 407 us -> 227 us (0.56); the launches traced: 400 us -> 224 us
  local copies, waits for them, and re-layouts: 135 us -> 20.3 us
  blocking collectives: 56.5 us -> 0 us
  Pallas kernels: 0 us -> 33.8 us
  waiting for transfers between devices: 106 us -> 78.6 us
  matrix products: 13.8 us -> 2.49 us
    all_to_all x15 -> x0, waiting for transfers between devices: 106 us -> none  [the longest x3 72.6 us: summed_rows(): lax.all_to_all(nearer.astype(jnp.bfloat16), far, split_axis=0, concat_axi...]
    ppermute x0 -> x63, waiting for transfers between devices: none -> 78.6 us  [the longest x12 29.4 us: scattered(): got = [lax.ppermute(mine[d], BOND, shifts(d, 0)) for d in (2, 1, 3)]]
    ppermute x0 -> x63, starting transfers between devices: none -> 76 us  [the longest x18 24.7 us: swap_cores(): return lax.ppermute(array, 'core', [(0, 1), (1, 0)])]
    all_to_all x15 -> x0, starting transfers between devices: 73.5 us -> none  [the longest x6 28.8 us: from_everyone(): lax.all_to_all(jnp.broadcast_to(array[None], (count, *array.shape)), axis...]
    scatter x2 -> x0, local copies, waits for them, and re-layouts: 61.3 us -> none  [on_device(): jnp.zeros((PHYSICAL * BOND_DIM,), jnp.float32).at[kept_columns[position]]]
    all_to_all x5 -> x0, blocking collectives: 56.5 us -> none  [the longest x4 31.2 us: sent_and_summed(): parts = lax.all_to_all(cut_along(array, dim, count), axis, 0, 0, tiled=True)]
    pallas_call x0 -> x8, Pallas kernels: none -> 33.8 us  [call(): pl.pallas_call(functools.partial(kernel, site), out_shape=shapes, in_spec...]
    reshape x8 -> x0, local copies, waits for them, and re-layouts: 28.4 us -> none  [the longest x4 16.7 us: cut_along(): array.reshape(*dims[:dim], count, dims[dim] // count, *dims[dim + 1:])]
  transfers between devices with their start and end apart: 15 -> 63, of which waited for: 12 -> 32; matrix products, arithmetic and copies ran while one was open for 28% -> 6% of each run, Pallas kernels for 0% -> 6%
where the time goes in v1:
time: 227 us; the launch traced here: 224 us
  waiting for transfers between devices  78.6 us (35%)
  starting transfers between devices  76 us (33%)
  Pallas kernels  33.8 us (15%)
  local copies, waits for them, and re-layouts  20.3 us (9%)
  other arithmetic  11.6 us (5%)
  matrix products  2.49 us (1%)
    pallas_call x8, Pallas kernels, call(): pl.pallas_call(functools.partial(kernel, site), out_shape=shapes, in_spec...  33.8 us
    ppermute x12, waiting for transfers between devices, scattered(): got = [lax.ppermute(mine[d], BOND, shifts(d, 0)) for d in (2, 1, 3)]  29.4 us
    ppermute x18, starting transfers between devices, swap_cores(): return lax.ppermute(array, 'core', [(0, 1), (1, 0)])  24.7 us
    ppermute x9, waiting for transfers between devices, total_grams(): got = [lax.ppermute(total, axis, ring_shift(d)) for d in (1, 2, 3)]  19.5 us
    unnamed x23, local copies, waits for them, and re-layouts  18.8 us
    ppermute x12, waiting for transfers between devices, scattered(): got = [lax.ppermute(near[e], BOND, shifts(e, 1)) for e in (2, 1, 3)]  15.3 us
    ppermute x12, starting transfers between devices, along_z(): lax.ppermute(array, 'z', ring_shift(d))  14.1 us
    ppermute x12, starting transfers between devices, scattered(): got = [lax.ppermute(mine[d], BOND, shifts(d, 0)) for d in (2, 1, 3)]  13.5 us
  transfers between devices with their start and end apart: 63, of which 32 were waited for; matrix products, arithmetic and copies ran while one was open for 6% of the time, Pallas kernels for 6%

profile of v1, /device:TPU:1, one launch (start us, length us, event | category | flops | bytes accessed | tf_op | source)
XLA Modules:
  0.0 224.0 jit_solution(7215632970035200910)
XLA Ops:
  0.9 3.4 %copy-done = bf16[2,256,1,8192]{3,1,2,0:T(8,128)(2,1)S(1)} copy-done((bf16[2,256,1,8192]{3,1,2,0:T(8,128)(2,1)S(1)}, bf16[2,256,1,8192]{3,1,2,0:T(8,128)(2,1)}, u32[]{:S(2)}) %copy-start) | copy-done | bytes 8388632
  5.1 4.1 %shard_map.69 = (bf16[4,198,256]{2,1,0:T(8,128)(2,1)S(1)}, bf16[4,198,256]{2,1,0:T(8,128)(2,1)S(1)}, bf16[4,198,256]{2,1,0:T(8,128)(2,1)S(1)}, bf16[4,198,256]{2,1,0:T(8,128)(2,1)S(1)}) custom-call(s32[16]{0:T(128)S(1)} %multiply_add_fusion.order, bf16[198,256]{1,0:T(8,128)(2,1)S(1)} %copy-done.5, bf16[512,8192]{1,0:T(8,128)(2,1)S(1)} %bitcast.69), custom_call_target="tpu_custom_call" | custom-call | flops 415236096 | bytes 4194304 | tf_op jit(solution)/shard_map/pallas_call | solution.py:128
  13.2 3.4 %copy-done.1 = bf16[2,256,1,8192]{3,1,2,0:T(8,128)(2,1)S(1)} copy-done((bf16[2,256,1,8192]{3,1,2,0:T(8,128)(2,1)S(1)}, bf16[2,256,1,8192]{3,1,2,0:T(8,128)(2,1)}, u32[]{:S(2)}) %copy-start.1) | copy-done | bytes 8388632
  16.6 4.1 %shard_map.68 = (bf16[4,198,256]{2,1,0:T(8,128)(2,1)S(1)}, bf16[4,198,256]{2,1,0:T(8,128)(2,1)S(1)}, bf16[4,198,256]{2,1,0:T(8,128)(2,1)S(1)}, bf16[4,198,256]{2,1,0:T(8,128)(2,1)S(1)}) custom-call(s32[16]{0:T(128)S(1)} %multiply_add_fusion.1.order, bf16[198,256]{1,0:T(8,128)(2,1)S(1)} %copy-done.6, bf16[512,8192]{1,0:T(8,128)(2,1)S(1)} %bitcast.70), custom_call_target="tpu_custom_call" | custom-call | flops 415236096 | bytes 4194304 | tf_op jit(solution)/shard_map/pallas_call | solution.py:128
  33.7 7.4 %collective-permute-done.4 = bf16[4,198,256]{2,1,0:T(8,128)(2,1)} collective-permute-done((bf16[4,198,256]{2,1,0:T(8,128)(2,1)}, bf16[4,198,256]{2,1,0:T(8,128)(2,1)}, u32[]{:S(2)}, u32[]{:S(2)}) %collective-permute-start.4) | collective-permute-done | bytes 405536 | tf_op jit(solution)/shard_map/ppermute | solution.py:149
  47.0 3.6 %collective-permute-done.8 = bf16[198,256]{1,0:T(8,128)(2,1)S(1)} collective-permute-done((bf16[198,256]{1,0:T(8,128)(2,1)S(1)}, bf16[198,256]{1,0:T(8,128)(2,1)S(1)}, u32[]{:S(2)}, u32[]{:S(2)}) %collective-permute-start.8) | collective-permute-done | bytes 101408 | tf_op jit(solution)/shard_map/ppermute | solution.py:151
  59.5 3.4 %copy-done.2 = bf16[2,256,1,8192]{3,1,2,0:T(8,128)(2,1)S(1)} copy-done((bf16[2,256,1,8192]{3,1,2,0:T(8,128)(2,1)S(1)}, bf16[2,256,1,8192]{3,1,2,0:T(8,128)(2,1)}, u32[]{:S(2)}) %copy-start.2) | copy-done | bytes 8388632
  62.8 4.4 %shard_map.70 = (bf16[198,256]{1,0:T(8,128)(2,1)S(1)}, bf16[4,198,256]{2,1,0:T(8,128)(2,1)S(1)}, bf16[4,198,256]{2,1,0:T(8,128)(2,1)S(1)}, bf16[4,198,256]{2,1,0:T(8,128)(2,1)S(1)}, bf16[4,198,256]{2,1,0:T(8,128)(2,1)S(1)}) custom-call(s32[16]{0:T(128)S(1)} %multiply_add_fusion.order, bf16[198,256]{1,0:T(8,128)(2,1)S(1)} %fusion.23.a, ...), custom_call_target="tpu_custom_call" | custom-call | flops 415236096 | bytes 4194304 | tf_op jit(solution)/shard_map/pallas_call | solution.py:128
  67.2 4.7 %collective-permute-start.18 = (bf16[4,198,256]{2,1,0:T(8,128)(2,1)S(1)}, bf16[4,198,256]{2,1,0:T(8,128)(2,1)S(1)}, u32[]{:S(2)}, u32[]{:S(2)}) collective-permute-start(bf16[4,198,256]{2,1,0:T(8,128)(2,1)S(1)} %get-tuple-element.55), channel_id=1, source_target_pairs={{0,4},{4,0},{1,5},{5,1},{2,6},{6,2},{3,7},{7,3},{8,12},{12,8},{9,1... | collective-permute-start | bytes 1216520 | tf_op jit(solution)/shard_map/ppermute | solution.py:50
  72.6 3.4 %copy-done.3 = bf16[2,256,1,8192]{3,1,2,0:T(8,128)(2,1)S(1)} copy-done((bf16[2,256,1,8192]{3,1,2,0:T(8,128)(2,1)S(1)}, bf16[2,256,1,8192]{3,1,2,0:T(8,128)(2,1)}, u32[]{:S(2)}) %copy-start.3) | copy-done | bytes 8388632
  76.0 4.3 %shard_map.71 = (bf16[4,198,256]{2,1,0:T(8,128)(2,1)S(1)}, bf16[4,198,256]{2,1,0:T(8,128)(2,1)S(1)}, bf16[4,198,256]{2,1,0:T(8,128)(2,1)S(1)}, bf16[4,198,256]{2,1,0:T(8,128)(2,1)S(1)}, bf16[198,198]{1,0:T(8,128)(2,1)S(1)}) custom-call(s32[16]{0:T(128)S(1)} %multiply_add_fusion.1.order, bf16[198,256]{1,0:T(8,128)(2,1)S(1)} %get-tuple-element.47.left, ...), custom_call_target="tpu_custom_call" | custom-call | flops 415236096 | bytes 4194304 | tf_op jit(solution)/shard_map/pallas_call | solution.py:128
  84.4 7.7 %collective-permute-done.19 = bf16[4,198,256]{2,1,0:T(8,128)(2,1)S(1)} collective-permute-done((bf16[4,198,256]{2,1,0:T(8,128)(2,1)S(1)}, bf16[4,198,256]{2,1,0:T(8,128)(2,1)S(1)}, u32[]{:S(2)}, u32[]{:S(2)}) %collective-permute-start.19) | collective-permute-done | bytes 405536 | tf_op jit(solution)/shard_map/ppermute | solution.py:149
  92.1 3.3 %collective-permute-done.17 = bf16[4,198,256]{2,1,0:T(8,128)(2,1)S(1)} collective-permute-done((bf16[4,198,256]{2,1,0:T(8,128)(2,1)S(1)}, bf16[4,198,256]{2,1,0:T(8,128)(2,1)S(1)}, u32[]{:S(2)}, u32[]{:S(2)}) %collective-permute-start.17) | collective-permute-done | bytes 405536 | tf_op jit(solution)/shard_map/ppermute | solution.py:149
  109.1 4.2 %shard_map.72 = (bf16[198,256]{1,0:T(8,128)(2,1)S(1)}, bf16[4,198,256]{2,1,0:T(8,128)(2,1)S(1)}, bf16[4,198,256]{2,1,0:T(8,128)(2,1)S(1)}, bf16[4,198,256]{2,1,0:T(8,128)(2,1)S(1)}, bf16[4,198,256]{2,1,0:T(8,128)(2,1)S(1)}) custom-call(s32[16]{0:T(128)S(1)} %multiply_add_fusion.order, bf16[198,256]{1,0:T(8,128)(2,1)S(1)} %fusion.20.a, ...), custom_call_target="tpu_custom_call" | custom-call | flops 415236096 | bytes 4194304 | tf_op jit(solution)/shard_map/pallas_call | solution.py:128
  113.3 5.1 %collective-permute-start.31 = (bf16[4,198,256]{2,1,0:T(8,128)(2,1)S(1)}, bf16[4,198,256]{2,1,0:T(8,128)(2,1)S(1)}, u32[]{:S(2)}, u32[]{:S(2)}) collective-permute-start(bf16[4,198,256]{2,1,0:T(8,128)(2,1)S(1)} %get-tuple-element.64), channel_id=1, source_target_pairs={{0,4},{4,0},{1,5},{5,1},{2,6},{6,2},{3,7},{7,3},{8,12},{12,8},{9,1... | collective-permute-start | bytes 1216520 | tf_op jit(solution)/shard_map/ppermute | solution.py:50
  119.0 4.1 %shard_map.73 = (bf16[4,198,256]{2,1,0:T(8,128)(2,1)S(1)}, bf16[4,198,256]{2,1,0:T(8,128)(2,1)S(1)}, bf16[4,198,256]{2,1,0:T(8,128)(2,1)S(1)}, bf16[4,198,256]{2,1,0:T(8,128)(2,1)S(1)}) custom-call(s32[16]{0:T(128)S(1)} %multiply_add_fusion.1.order, bf16[198,256]{1,0:T(8,128)(2,1)S(1)} %get-tuple-element.56.left, bf16[512,8192]{1,0:T(8,128)(2,1)S(1)} %bitcast.74), custom_call_target="tpu_custom_call" | custom-call | flops 415236096 | bytes 4194304 | tf_op jit(solution)/shard_map/pallas_call | solution.py:128
  127.0 7.7 %collective-permute-done.32 = bf16[4,198,256]{2,1,0:T(8,128)(2,1)S(1)} collective-permute-done((bf16[4,198,256]{2,1,0:T(8,128)(2,1)S(1)}, bf16[4,198,256]{2,1,0:T(8,128)(2,1)S(1)}, u32[]{:S(2)}, u32[]{:S(2)}) %collective-permute-start.32) | collective-permute-done | bytes 405536 | tf_op jit(solution)/shard_map/ppermute | solution.py:149
  134.7 3.3 %collective-permute-done.30 = bf16[4,198,256]{2,1,0:T(8,128)(2,1)S(1)} collective-permute-done((bf16[4,198,256]{2,1,0:T(8,128)(2,1)S(1)}, bf16[4,198,256]{2,1,0:T(8,128)(2,1)S(1)}, u32[]{:S(2)}, u32[]{:S(2)}) %collective-permute-start.30) | collective-permute-done | bytes 405536 | tf_op jit(solution)/shard_map/ppermute | solution.py:149
  151.6 3.4 %copy-done.4 = bf16[2,256,1,8192]{3,1,2,0:T(8,128)(2,1)S(1)} copy-done((bf16[2,256,1,8192]{3,1,2,0:T(8,128)(2,1)S(1)}, bf16[2,256,1,8192]{3,1,2,0:T(8,128)(2,1)}, u32[]{:S(2)}) %copy-start.4) | copy-done | bytes 8388632
  154.9 4.4 %shard_map.74 = (bf16[198,256]{1,0:T(8,128)(2,1)S(1)}, bf16[4,198,256]{2,1,0:T(8,128)(2,1)S(1)}, bf16[4,198,256]{2,1,0:T(8,128)(2,1)S(1)}, bf16[4,198,256]{2,1,0:T(8,128)(2,1)S(1)}, bf16[4,198,256]{2,1,0:T(8,128)(2,1)S(1)}) custom-call(s32[16]{0:T(128)S(1)} %multiply_add_fusion.order, bf16[198,256]{1,0:T(8,128)(2,1)S(1)} %fusion.17.a, ...), custom_call_target="tpu_custom_call" | custom-call | flops 415236096 | bytes 4194304 | tf_op jit(solution)/shard_map/pallas_call | solution.py:128
  159.3 4.3 %shard_map.75 = (bf16[4,198,256]{2,1,0:T(8,128)(2,1)S(1)}, bf16[4,198,256]{2,1,0:T(8,128)(2,1)S(1)}, bf16[4,198,256]{2,1,0:T(8,128)(2,1)S(1)}, bf16[4,198,256]{2,1,0:T(8,128)(2,1)S(1)}, bf16[198,198]{1,0:T(8,128)(2,1)S(1)}) custom-call(s32[16]{0:T(128)S(1)} %multiply_add_fusion.1.order, bf16[198,256]{1,0:T(8,128)(2,1)S(1)} %get-tuple-element.65.left, ...), custom_call_target="tpu_custom_call" | custom-call | flops 415236096 | bytes 4194304 | tf_op jit(solution)/shard_map/pallas_call | solution.py:128
  163.7 4.4 %collective-permute-start.52 = (bf16[198,198]{1,0:T(8,128)(2,1)S(1)}, bf16[198,198]{1,0:T(8,128)(2,1)S(1)}, u32[]{:S(2)}, u32[]{:S(2)}) collective-permute-start(bf16[198,198]{1,0:T(8,128)(2,1)S(1)} %broadcast_select_fusion), channel_id=1, source_target_pairs={{0,4},{4,0},{1,5},{5,1},{2,6},{6,2},{3,7},{7,3},{8,12},{12,8},{9,1... | collective-permute-start | bytes 235232 | tf_op jit(solution)/shard_map/ppermute | solution.py:50
  195.4 8.8 %collective-permute-done.60 = bf16[198,198]{1,0:T(8,128)(2,1)S(1)} collective-permute-done((bf16[198,198]{1,0:T(8,128)(2,1)S(1)}, bf16[198,198]{1,0:T(8,128)(2,1)S(1)}, u32[]{:S(2)}, u32[]{:S(2)}) %collective-permute-start.60) | collective-permute-done | bytes 78440 | tf_op jit(solution)/shard_map/ppermute | solution.py:196
  205.2 4.2 %collective-permute-done.59 = bf16[198,198]{1,0:T(8,128)(2,1)S(1)} collective-permute-done((bf16[198,198]{1,0:T(8,128)(2,1)S(1)}, bf16[198,198]{1,0:T(8,128)(2,1)S(1)}, u32[]{:S(2)}, u32[]{:S(2)}) %collective-permute-start.59) | collective-permute-done | bytes 78440 | tf_op jit(solution)/shard_map/ppermute | solution.py:196
  (188 shorter events, 111.8 us)
Async XLA Ops:
  9.3 13.2 %collective-permute-start.5 = (bf16[4,198,256]{2,1,0:T(8,128)(2,1)S(1)}, bf16[4,198,256]{2,1,0:T(8,128)(2,1)S(1)}, u32[]{:S(2)}, u32[]{:S(2)}) collective-permute-start(bf16[4,198,256]{2,1,0:T(8,128)(2,1)S(1)} %get-tuple-element.46), channel_id=1, source_target_pairs={{0,4},{4,0},{1,5},{5,1},{2,6},{6,2},{3,7},{7,3},{8,12},{12,8},{9,1... | collective-permute-start | bytes 1216520 | tf_op jit(solution)/shard_map/ppermute | solution.py:50
  10.7 15.4 %collective-permute-start.3 = (bf16[4,198,256]{2,1,0:T(8,128)(2,1)S(1)}, bf16[4,198,256]{2,1,0:T(8,128)(2,1)}, u32[]{:S(2)}, u32[]{:S(2)}) collective-permute-start(bf16[4,198,256]{2,1,0:T(8,128)(2,1)S(1)} %get-tuple-element.44), channel_id=1, source_target_pairs={{0,4},{4,0},{1,5},{5,1},{2,6},{6,2},{3,7},{7,3},{8,12},{12,8},{9,1... | collective-permute-start | bytes 1216520 | tf_op jit(solution)/shard_map/ppermute | solution.py:50
  10.8 17.2 %collective-permute-start.1 = (bf16[4,198,256]{2,1,0:T(8,128)(2,1)S(1)}, bf16[4,198,256]{2,1,0:T(8,128)(2,1)}, u32[]{:S(2)}, u32[]{:S(2)}) collective-permute-start(bf16[4,198,256]{2,1,0:T(8,128)(2,1)S(1)} %get-tuple-element.42), channel_id=1, source_target_pairs={{0,4},{4,0},{1,5},{5,1},{2,6},{6,2},{3,7},{7,3},{8,12},{12,8},{9,1... | collective-permute-start | bytes 1216520 | tf_op jit(solution)/shard_map/ppermute | solution.py:50
  11.2 22.4 %collective-permute-start = (bf16[4,198,256]{2,1,0:T(8,128)(2,1)S(1)}, bf16[4,198,256]{2,1,0:T(8,128)(2,1)S(1)}, u32[]{:S(2)}, u32[]{:S(2)}) collective-permute-start(bf16[4,198,256]{2,1,0:T(8,128)(2,1)S(1)} %get-tuple-element.40), channel_id=1, source_target_pairs={{0,4},{4,0},{1,5},{5,1},{2,6},{6,2},{3,7},{7,3},{8,12},{12,8},{9,1... | collective-permute-start | bytes 1216520 | tf_op jit(solution)/shard_map/ppermute | solution.py:50
  23.3 10.4 %collective-permute-start.6 = (bf16[4,198,256]{2,1,0:T(8,128)(2,1)}, bf16[4,198,256]{2,1,0:T(8,128)(2,1)S(1)}, u32[]{:S(2)}, u32[]{:S(2)}) collective-permute-start(bf16[4,198,256]{2,1,0:T(8,128)(2,1)} %add_convert_fusion.16), channel_id=1, source_target_pairs={{0,24},{4,100},{8,0},{12,108},{16,8},{20,116},{24,16},{28,124},{32... | collective-permute-start | bytes 1216520 | tf_op jit(solution)/shard_map/ppermute | solution.py:149
  28.1 13.0 %collective-permute-start.4 = (bf16[4,198,256]{2,1,0:T(8,128)(2,1)}, bf16[4,198,256]{2,1,0:T(8,128)(2,1)}, u32[]{:S(2)}, u32[]{:S(2)}) collective-permute-start(bf16[4,198,256]{2,1,0:T(8,128)(2,1)} %add_convert_fusion.17), channel_id=1, source_target_pairs={{0,8},{4,36},{8,16},{12,44},{16,24},{20,52},{24,0},{28,60},{32,40}... | collective-permute-start | bytes 1216520 | tf_op jit(solution)/shard_map/ppermute | solution.py:149
  29.9 11.1 %collective-permute-start.2 = (bf16[4,198,256]{2,1,0:T(8,128)(2,1)}, bf16[4,198,256]{2,1,0:T(8,128)(2,1)}, u32[]{:S(2)}, u32[]{:S(2)}) collective-permute-start(bf16[4,198,256]{2,1,0:T(8,128)(2,1)} %add_convert_fusion.18), channel_id=1, source_target_pairs={{0,16},{4,68},{8,24},{12,76},{16,0},{20,84},{24,8},{28,92},{32,48}... | collective-permute-start | bytes 1216520 | tf_op jit(solution)/shard_map/ppermute | solution.py:149
  67.2 13.0 %collective-permute-start.18 = (bf16[4,198,256]{2,1,0:T(8,128)(2,1)S(1)}, bf16[4,198,256]{2,1,0:T(8,128)(2,1)S(1)}, u32[]{:S(2)}, u32[]{:S(2)}) collective-permute-start(bf16[4,198,256]{2,1,0:T(8,128)(2,1)S(1)} %get-tuple-element.55), channel_id=1, source_target_pairs={{0,4},{4,0},{1,5},{5,1},{2,6},{6,2},{3,7},{7,3},{8,12},{12,8},{9,1... | collective-permute-start | bytes 1216520 | tf_op jit(solution)/shard_map/ppermute | solution.py:50
  72.0 10.8 %collective-permute-start.16 = (bf16[4,198,256]{2,1,0:T(8,128)(2,1)S(1)}, bf16[4,198,256]{2,1,0:T(8,128)(2,1)S(1)}, u32[]{:S(2)}, u32[]{:S(2)}) collective-permute-start(bf16[4,198,256]{2,1,0:T(8,128)(2,1)S(1)} %get-tuple-element.53), channel_id=1, source_target_pairs={{0,4},{4,0},{1,5},{5,1},{2,6},{6,2},{3,7},{7,3},{8,12},{12,8},{9,1... | collective-permute-start | bytes 1216520 | tf_op jit(solution)/shard_map/ppermute | solution.py:50
  72.1 10.9 %collective-permute-start.14 = (bf16[4,198,256]{2,1,0:T(8,128)(2,1)S(1)}, bf16[4,198,256]{2,1,0:T(8,128)(2,1)S(1)}, u32[]{:S(2)}, u32[]{:S(2)}) collective-permute-start(bf16[4,198,256]{2,1,0:T(8,128)(2,1)S(1)} %get-tuple-element.51), channel_id=1, source_target_pairs={{0,4},{4,0},{1,5},{5,1},{2,6},{6,2},{3,7},{7,3},{8,12},{12,8},{9,1... | collective-permute-start | bytes 1216520 | tf_op jit(solution)/shard_map/ppermute | solution.py:50
  72.5 11.9 %collective-permute-start.13 = (bf16[4,198,256]{2,1,0:T(8,128)(2,1)S(1)}, bf16[4,198,256]{2,1,0:T(8,128)(2,1)S(1)}, u32[]{:S(2)}, u32[]{:S(2)}) collective-permute-start(bf16[4,198,256]{2,1,0:T(8,128)(2,1)S(1)} %get-tuple-element.49), channel_id=1, source_target_pairs={{0,4},{4,0},{1,5},{5,1},{2,6},{6,2},{3,7},{7,3},{8,12},{12,8},{9,1... | collective-permute-start | bytes 1216520 | tf_op jit(solution)/shard_map/ppermute | solution.py:50
  80.4 11.7 %collective-permute-start.19 = (bf16[4,198,256]{2,1,0:T(8,128)(2,1)S(1)}, bf16[4,198,256]{2,1,0:T(8,128)(2,1)S(1)}, u32[]{:S(2)}, u32[]{:S(2)}) collective-permute-start(bf16[4,198,256]{2,1,0:T(8,128)(2,1)S(1)} %add_convert_fusion.11), channel_id=1, source_target_pairs={{0,24},{4,100},{8,0},{12,108},{16,8},{20,116},{24,16},{28,124},{32... | collective-permute-start | bytes 1216520 | tf_op jit(solution)/shard_map/ppermute | solution.py:149
  82.9 12.5 %collective-permute-start.17 = (bf16[4,198,256]{2,1,0:T(8,128)(2,1)S(1)}, bf16[4,198,256]{2,1,0:T(8,128)(2,1)S(1)}, u32[]{:S(2)}, u32[]{:S(2)}) collective-permute-start(bf16[4,198,256]{2,1,0:T(8,128)(2,1)S(1)} %add_convert_fusion.12), channel_id=1, source_target_pairs={{0,8},{4,36},{8,16},{12,44},{16,24},{20,52},{24,0},{28,60},{32,40}... | collective-permute-start | bytes 1216520 | tf_op jit(solution)/shard_map/ppermute | solution.py:149
  83.1 12.3 %collective-permute-start.15 = (bf16[4,198,256]{2,1,0:T(8,128)(2,1)S(1)}, bf16[4,198,256]{2,1,0:T(8,128)(2,1)S(1)}, u32[]{:S(2)}, u32[]{:S(2)}) collective-permute-start(bf16[4,198,256]{2,1,0:T(8,128)(2,1)S(1)} %add_convert_fusion.13), channel_id=1, source_target_pairs={{0,16},{4,68},{8,24},{12,76},{16,0},{20,84},{24,8},{28,92},{32,48}... | collective-permute-start | bytes 1216520 | tf_op jit(solution)/shard_map/ppermute | solution.py:149
  113.3 9.8 %collective-permute-start.31 = (bf16[4,198,256]{2,1,0:T(8,128)(2,1)S(1)}, bf16[4,198,256]{2,1,0:T(8,128)(2,1)S(1)}, u32[]{:S(2)}, u32[]{:S(2)}) collective-permute-start(bf16[4,198,256]{2,1,0:T(8,128)(2,1)S(1)} %get-tuple-element.64), channel_id=1, source_target_pairs={{0,4},{4,0},{1,5},{5,1},{2,6},{6,2},{3,7},{7,3},{8,12},{12,8},{9,1... | collective-permute-start | bytes 1216520 | tf_op jit(solution)/shard_map/ppermute | solution.py:50
  123.2 11.5 %collective-permute-start.32 = (bf16[4,198,256]{2,1,0:T(8,128)(2,1)S(1)}, bf16[4,198,256]{2,1,0:T(8,128)(2,1)S(1)}, u32[]{:S(2)}, u32[]{:S(2)}) collective-permute-start(bf16[4,198,256]{2,1,0:T(8,128)(2,1)S(1)} %add_convert_fusion.6), channel_id=1, source_target_pairs={{0,24},{4,100},{8,0},{12,108},{16,8},{20,116},{24,16},{28,124},{32... | collective-permute-start | bytes 1216520 | tf_op jit(solution)/shard_map/ppermute | solution.py:149
  125.5 12.5 %collective-permute-start.30 = (bf16[4,198,256]{2,1,0:T(8,128)(2,1)S(1)}, bf16[4,198,256]{2,1,0:T(8,128)(2,1)S(1)}, u32[]{:S(2)}, u32[]{:S(2)}) collective-permute-start(bf16[4,198,256]{2,1,0:T(8,128)(2,1)S(1)} %add_convert_fusion.7), channel_id=1, source_target_pairs={{0,8},{4,36},{8,16},{12,44},{16,24},{20,52},{24,0},{28,60},{32,40}... | collective-permute-start | bytes 1216520 | tf_op jit(solution)/shard_map/ppermute | solution.py:149
  125.7 12.3 %collective-permute-start.28 = (bf16[4,198,256]{2,1,0:T(8,128)(2,1)S(1)}, bf16[4,198,256]{2,1,0:T(8,128)(2,1)S(1)}, u32[]{:S(2)}, u32[]{:S(2)}) collective-permute-start(bf16[4,198,256]{2,1,0:T(8,128)(2,1)S(1)} %add_convert_fusion.8), channel_id=1, source_target_pairs={{0,16},{4,68},{8,24},{12,76},{16,0},{20,84},{24,8},{28,92},{32,48}... | collective-permute-start | bytes 1216520 | tf_op jit(solution)/shard_map/ppermute | solution.py:149
  171.7 18.6 %collective-permute-start.44 = (bf16[4,198,256]{2,1,0:T(8,128)(2,1)S(1)}, bf16[4,198,256]{2,1,0:T(8,128)(2,1)S(1)}, u32[]{:S(2)}, u32[]{:S(2)}) collective-permute-start(bf16[4,198,256]{2,1,0:T(8,128)(2,1)S(1)} %get-tuple-element.73), channel_id=1, source_target_pairs={{0,4},{4,0},{1,5},{5,1},{2,6},{6,2},{3,7},{7,3},{8,12},{12,8},{9,1... | collective-permute-start | bytes 1216520 | tf_op jit(solution)/shard_map/ppermute | solution.py:50
  185.7 23.8 %collective-permute-start.39 = (bf16[4,198,256]{2,1,0:T(8,128)(2,1)S(1)}, bf16[4,198,256]{2,1,0:T(8,128)(2,1)S(1)}, u32[]{:S(2)}, u32[]{:S(2)}) collective-permute-start(bf16[4,198,256]{2,1,0:T(8,128)(2,1)S(1)} %get-tuple-element.67), channel_id=1, source_target_pairs={{0,4},{4,0},{1,5},{5,1},{2,6},{6,2},{3,7},{7,3},{8,12},{12,8},{9,1... | collective-permute-start | bytes 1216520 | tf_op jit(solution)/shard_map/ppermute | solution.py:50
  190.5 19.0 %collective-permute-start.45 = (bf16[4,198,256]{2,1,0:T(8,128)(2,1)S(1)}, bf16[4,198,256]{2,1,0:T(8,128)(2,1)S(1)}, u32[]{:S(2)}, u32[]{:S(2)}) collective-permute-start(bf16[4,198,256]{2,1,0:T(8,128)(2,1)S(1)} %add_convert_fusion.1), channel_id=1, source_target_pairs={{0,24},{4,100},{8,0},{12,108},{16,8},{20,116},{24,16},{28,124},{32... | collective-permute-start | bytes 1216520 | tf_op jit(solution)/shard_map/ppermute | solution.py:149
  190.7 18.8 %collective-permute-start.43 = (bf16[4,198,256]{2,1,0:T(8,128)(2,1)S(1)}, bf16[4,198,256]{2,1,0:T(8,128)(2,1)S(1)}, u32[]{:S(2)}, u32[]{:S(2)}) collective-permute-start(bf16[4,198,256]{2,1,0:T(8,128)(2,1)S(1)} %add_convert_fusion.2), channel_id=1, source_target_pairs={{0,8},{4,36},{8,16},{12,44},{16,24},{20,52},{24,0},{28,60},{32,40}... | collective-permute-start | bytes 1216520 | tf_op jit(solution)/shard_map/ppermute | solution.py:149
  192.3 17.2 %collective-permute-start.41 = (bf16[4,198,256]{2,1,0:T(8,128)(2,1)S(1)}, bf16[4,198,256]{2,1,0:T(8,128)(2,1)S(1)}, u32[]{:S(2)}, u32[]{:S(2)}) collective-permute-start(bf16[4,198,256]{2,1,0:T(8,128)(2,1)S(1)} %add_convert_fusion.3), channel_id=1, source_target_pairs={{0,16},{4,68},{8,24},{12,76},{16,0},{20,84},{24,8},{28,92},{32,48}... | collective-permute-start | bytes 1216520 | tf_op jit(solution)/shard_map/ppermute | solution.py:149
  192.4 11.8 %collective-permute-start.60 = (bf16[198,198]{1,0:T(8,128)(2,1)S(1)}, bf16[198,198]{1,0:T(8,128)(2,1)S(1)}, u32[]{:S(2)}, u32[]{:S(2)}) collective-permute-start(bf16[198,198]{1,0:T(8,128)(2,1)S(1)} %add_convert_fusion.20), channel_id=1, source_target_pairs={{0,64},{32,96},{64,0},{96,32},{1,65},{33,97},{65,1},{97,33},{2,66}... | collective-permute-start | bytes 235232 | tf_op jit(solution)/shard_map/ppermute | solution.py:196
  (50 other events, 323.7 us)

commit v2 on v1

--- a/solution.py
+++ b/solution.py
@@ -17,6 +17,7 @@
 BOND = ("y", "x", "core")
 RING = 4
 BLOCK = 256
+SENT = (2, 1, 3, 0)
 F32 = jnp.float32
 BF16 = jnp.bfloat16
 
@@ -59,29 +60,26 @@
     return (((y + dy) % RING * RING + (x + dx) % RING) * 2 + core).astype(jnp.int32)
 
 
-def column_copy(site, order, weights, tiles, sems, i):
-    first = pl.multiple_of(order[i] * BLOCK, BLOCK)
-    source = weights.at[pl.ds(site * BLOCK, BLOCK), pl.ds(first, BLOCK)]
-    return pltpu.make_async_copy(source, tiles.at[i], sems.at[i])
-
-
 def start_columns(site, order, weights, tiles, sems):
-    @pl.loop(0, RING * RING)
-    def _(i):
-        column_copy(site, order, weights, tiles, sems, i).start()
-
-    return functools.partial(column_copy, site, order, weights, tiles, sems)
+    copies = []
+    for i in range(RING * RING):
+        first = pl.multiple_of(order[i] * BLOCK, BLOCK)
+        source = weights.at[pl.ds(site * BLOCK, BLOCK), pl.ds(first, BLOCK)]
+        target = tiles.at[:, pl.ds(i * BLOCK, BLOCK)]
+        copies.append(pltpu.make_async_copy(source, target, sems.at[i]))
+        copies[-1].start()
+    return copies
 
 
 def multiply_columns(left, copies, tiles, outs):
-    for d, out in enumerate(outs):
-
-        @pl.loop(0, RING)
-        def _(e, d=d, out=out):
-            i = d * RING + e
-            copies(i).wait()
-            product = jnp.dot(left[...], tiles[i], preferred_element_type=F32)
-            out[e] = product.astype(BF16)
+    width = RING * BLOCK
+    for d in SENT:
+        for copy in copies[d * RING : (d + 1) * RING]:
+            copy.wait()
+        columns = tiles[:, d * width : (d + 1) * width]
+        product = jnp.dot(left[...], columns, preferred_element_type=F32).astype(BF16)
+        for e in range(RING):
+            outs[d][e] = product[:, e * BLOCK : (e + 1) * BLOCK]
 
 
 def plain_kernel(site, order, left, weights, *rest):
@@ -130,48 +128,66 @@
         out_shape=shapes,
         in_specs=[pl.BlockSpec(memory_space=pltpu.SMEM)]
         + [VMEM] * len(operands)
-        + [pl.BlockSpec(memory_space=pl.ANY)],
+        + [pl.BlockSpec(memory_space=pltpu.HBM)],
         out_specs=[VMEM] * len(shapes),
         scratch_shapes=[
-            pltpu.VMEM((RING * RING, BLOCK, BLOCK), BF16),
+            pltpu.VMEM((BLOCK, RING * RING * BLOCK), BF16),
             pltpu.SemaphoreType.DMA((RING * RING,)),
         ],
-        compiler_params=pltpu.CompilerParams(vmem_limit_bytes=24 * 2**20),
+        compiler_params=pltpu.CompilerParams(vmem_limit_bytes=48 * 2**20),
         cost_estimate=pl.CostEstimate(
             flops=flops, bytes_accessed=4 * 2**20, transcendentals=0
         ),
     )(order, *operands, weights)
 
 
-def scattered(theirs, ours):
-    arrived = [swap_cores(theirs[d]) for d in (2, 1, 3, 0)]
-    mine = {d: summed([ours[d], got]).astype(BF16) for d, got in zip((2, 1, 3, 0), arrived)}
+def scattered(theirs, ours, extra=None):
+    arrived = [swap_cores(theirs[d]) for d in SENT]
+    mine = {d: summed([ours[d], got]).astype(BF16) for d, got in zip(SENT, arrived)}
+    if extra is not None:
+        mine = {d: jnp.concatenate([piece, extra[None]]) for d, piece in mine.items()}
     got = [lax.ppermute(mine[d], BOND, shifts(d, 0)) for d in (2, 1, 3)]
     near = summed([mine[0], *got]).astype(BF16)
-    got = [lax.ppermute(near[e], BOND, shifts(e, 1)) for e in (2, 1, 3)]
-    return summed([near[0], *got]).astype(BF16)
+    pieces = [near[e] for e in range(RING)]
+    if extra is not None:
+        pieces = [jnp.stack([piece, near[RING]]) for piece in pieces]
+    got = [lax.ppermute(pieces[e], BOND, shifts(e, 1)) for e in (2, 1, 3)]
+    return summed([pieces[0], *got]).astype(BF16)
 
 
 def along_z(array):
     return [array] + [lax.ppermute(array, "z", ring_shift(d)) for d in (1, 2, 3)]
 
 
+def mixing_kernel(z, operator_tensors, mixing):
+    def iota(shape, dim):
+        return lax.broadcasted_iota(jnp.int32, shape, dim)
+
+    wide, tall = (ROWS, PHYSICAL * MPO_BOND), (MPO_BOND, ROWS)
+    first = z[0] * MPO_BOND
+    pick = (iota(wide, 1) == first + lax.rem(iota(wide, 0), MPO_BOND)).astype(BF16)
+    spread = (iota(tall, 0) == lax.rem(iota(tall, 1), MPO_BOND)).astype(BF16)
+    square = (ROWS, ROWS)
+    same = lax.div(iota(square, 0), MPO_BOND) == lax.div(iota(square, 1), MPO_BOND)
+    for site in range(SITE_COUNT):
+        for d in range(RING):
+            weights = operator_tensors[site, lax.rem(z[0] + RING - d, RING)]
+            narrow = lax.dot_general(
+                pick, weights, (((1,), (1,)), ((), ())), preferred_element_type=F32
+            ).astype(BF16)
+            full = jnp.dot(narrow, spread, preferred_element_type=F32)
+            mixing[site, d] = jnp.where(same, full, 0.0).astype(BF16)
+
+
 def mixing_weights(operator_tensors):
-    z = lax.axis_index("z")
-    turned = jnp.stack(
-        [
-            lax.dynamic_index_in_dim(operator_tensors, (z - d) % RING, 1, keepdims=False)
-            for d in range(RING)
-        ],
-        1,
-    )
-    row = jnp.arange(ROWS)
-    pick = (z * MPO_BOND + row[:, None] % MPO_BOND == jnp.arange(PHYSICAL * MPO_BOND)).astype(BF16)
-    spread = (jnp.arange(MPO_BOND)[:, None] == row[None] % MPO_BOND).astype(BF16)
-    narrow = jnp.einsum("xc,kdac->kdxa", pick, turned, preferred_element_type=F32).astype(BF16)
-    wide = jnp.einsum("kdxa,aw->kdxw", narrow, spread, preferred_element_type=F32)
-    same = row[:, None] // MPO_BOND == row[None] // MPO_BOND
-    return jnp.where(same, wide, 0.0).astype(BF16)
+    return pl.pallas_call(
+        mixing_kernel,
+        out_shape=jax.ShapeDtypeStruct((SITE_COUNT, RING, ROWS, ROWS), BF16),
+        in_specs=[pl.BlockSpec(memory_space=pltpu.SMEM), VMEM],
+        out_specs=VMEM,
+        compiler_params=pltpu.CompilerParams(vmem_limit_bytes=8 * 2**20),
+        cost_estimate=pl.CostEstimate(flops=10**9, bytes_accessed=10**6, transcendentals=0),
+    )(lax.axis_index("z").astype(jnp.int32)[None], operator_tensors)
 
 
 def chosen_columns(kept_columns):
@@ -188,17 +204,18 @@
     return (counts > 0.5).astype(F32).reshape(SITE_COUNT, 1, BLOCK)
 
 
-def total_grams(grams):
-    core = lax.axis_index("core")
-    own = jnp.where(core == 0, grams[0], grams[1])
-    total = summed([own, swap_cores(jnp.where(core == 0, grams[1], grams[0]))]).astype(BF16)
-    for axis in ("z", "x", "y"):
-        got = [lax.ppermute(total, axis, ring_shift(d)) for d in (1, 2, 3)]
-        total = summed([total, *got])
-        if axis != "y":
-            total = total.astype(BF16)
-    other = swap_cores(total)
-    return jnp.stack([jnp.where(core == 0, total, other), jnp.where(core == 0, other, total)])
+def chip_gram(grams):
+    first = lax.axis_index("core") == 0
+    got = swap_cores(jnp.where(first, grams[1], grams[0]))
+    total = summed([jnp.where(first, grams[0], grams[1]), got]).astype(BF16)
+    return jnp.pad(total, ((0, 0), (0, BLOCK - ROWS)))
+
+
+def both_grams(total):
+    own = total[:, :ROWS]
+    other = swap_cores(own)
+    first = lax.axis_index("core") == 0
+    return jnp.stack([jnp.where(first, own, other), jnp.where(first, other, own)])
 
 
 def on_device(carried, site_tensors, operator_tensors, rotation, kept_columns):
@@ -222,8 +239,10 @@
         )
         *ours, gram = call(gram_kernel, site, our_order, [kept], turns, after=[SQUARE])
         grams.append(gram)
-        parts = along_z(scattered(theirs, ours))
-    return summed(parts).astype(BF16), total_grams(grams)
+        last = site == SITE_COUNT - 1
+        parts = along_z(scattered(theirs, ours, chip_gram(grams) if last else None))
+    total = summed(parts)
+    return total[0].astype(BF16), both_grams(total[1])
 
 
 def solution(mesh):

time: 227 us -> 186 us (0.82); the launches traced: 224 us -> 185 us
  local copies, waits for them, and re-layouts: 20.3 us -> 3.27 us
  starting transfers between devices: 76 us -> 61.3 us
  waiting for transfers between devices: 78.6 us -> 84.9 us
  other arithmetic: 11.6 us -> 5.56 us
  Pallas kernels: 33.8 us -> 28.7 us
    unnamed x23 -> x12, local copies, waits for them, and re-layouts: 18.8 us -> 1.93 us
    ppermute x21 -> x12, waiting for transfers between devices: 34.8 us -> 18.2 us  [scattered(): got = [lax.ppermute(pieces[e], BOND, shifts(e, 1)) for e in (2, 1, 3)]]
    ppermute x12, waiting for transfers between devices: 29.4 us -> 44.2 us  [scattered(): got = [lax.ppermute(mine[d], BOND, shifts(d, 0)) for d in (2, 1, 3)]]
    ppermute x21 -> x12, starting transfers between devices: 23.6 us -> 11.3 us  [scattered(): got = [lax.ppermute(pieces[e], BOND, shifts(e, 1)) for e in (2, 1, 3)]]
    ppermute x12, waiting for transfers between devices: 13.4 us -> 20.5 us  [along_z(): lax.ppermute(array, 'z', ring_shift(d))]
    pallas_call x8, Pallas kernels: 33.8 us -> 26.9 us  [call(): pl.pallas_call(functools.partial(kernel, site), out_shape=shapes, in_spec...]
    ppermute x18, starting transfers between devices: 24.7 us -> 19.5 us  [swap_cores(): return lax.ppermute(array, 'core', [(0, 1), (1, 0)])]
    convert_element_type x12 -> x13, other arithmetic: 5.67 us -> 2.5 us  [scattered(): summed([ours[d], got]).astype(BF16)]
  transfers between devices with their start and end apart: 63 -> 54, of which waited for: 32 -> 33; matrix products, arithmetic and copies ran while one was open for 6% -> 3% of each run, Pallas kernels for 6% -> 6%
where the time goes in v2:
time: 186 us; the launch traced here: 185 us
  waiting for transfers between devices  84.9 us (46%)
  starting transfers between devices  61.3 us (33%)
  Pallas kernels  28.7 us (15%)
  other arithmetic  5.56 us (3%)
  local copies, waits for them, and re-layouts  3.27 us (2%)
    ppermute x12, waiting for transfers between devices, scattered(): got = [lax.ppermute(mine[d], BOND, shifts(d, 0)) for d in (2, 1, 3)]  44.2 us
    pallas_call x8, Pallas kernels, call(): pl.pallas_call(functools.partial(kernel, site), out_shape=shapes, in_spec...  26.9 us
    ppermute x12, waiting for transfers between devices, along_z(): lax.ppermute(array, 'z', ring_shift(d))  20.5 us
    ppermute x18, starting transfers between devices, swap_cores(): return lax.ppermute(array, 'core', [(0, 1), (1, 0)])  19.5 us
    ppermute x12, waiting for transfers between devices, scattered(): got = [lax.ppermute(pieces[e], BOND, shifts(e, 1)) for e in (2, 1, 3)]  18.2 us
    ppermute x12, starting transfers between devices, scattered(): got = [lax.ppermute(mine[d], BOND, shifts(d, 0)) for d in (2, 1, 3)]  15.3 us
    ppermute x12, starting transfers between devices, along_z(): lax.ppermute(array, 'z', ring_shift(d))  15.2 us
    ppermute x12, starting transfers between devices, scattered(): got = [lax.ppermute(pieces[e], BOND, shifts(e, 1)) for e in (2, 1, 3)]  11.3 us
  transfers between devices with their start and end apart: 54, of which 33 were waited for; matrix products, arithmetic and copies ran while one was open for 3% of the time, Pallas kernels for 6%

profile of v2, /device:TPU:1, one launch (start us, length us, event | category | flops | bytes accessed | tf_op | source)
XLA Modules:
  0.0 185.3 jit_solution(6837243542570942187)
XLA Ops:
  1.8 3.3 %shard_map.69 = (bf16[4,198,256]{2,1,0:T(8,128)(2,1)S(1)}, bf16[4,198,256]{2,1,0:T(8,128)(2,1)S(1)}, bf16[4,198,256]{2,1,0:T(8,128)(2,1)S(1)}, bf16[4,198,256]{2,1,0:T(8,128)(2,1)S(1)}) custom-call(s32[16]{0:T(128)S(1)} %multiply_add_fusion.order, bf16[198,256]{1,0:T(8,128)(2,1)S(1)} %copy-done, bf16[512,8192]{1,0:T(8,128)(2,1)} %bitcast.51), custom_call_target="tpu_custom_call" | custom-call | flops 415236096 | bytes 4194304 | tf_op jit(solution)/shard_map/pallas_call | solution.py:126
  8.4 3.3 %shard_map.68 = (bf16[4,198,256]{2,1,0:T(8,128)(2,1)S(1)}, bf16[4,198,256]{2,1,0:T(8,128)(2,1)S(1)}, bf16[4,198,256]{2,1,0:T(8,128)(2,1)S(1)}, bf16[4,198,256]{2,1,0:T(8,128)(2,1)S(1)}) custom-call(s32[16]{0:T(128)S(1)} %multiply_add_fusion.1.order, bf16[198,256]{1,0:T(8,128)(2,1)S(1)} %copy-done.1, bf16[512,8192]{1,0:T(8,128)(2,1)} %bitcast.52), custom_call_target="tpu_custom_call" | custom-call | flops 415236096 | bytes 4194304 | tf_op jit(solution)/shard_map/pallas_call | solution.py:126
  20.0 5.1 %collective-permute-done.6 = bf16[4,198,256]{2,1,0:T(8,128)(2,1)S(1)} collective-permute-done((bf16[4,198,256]{2,1,0:T(8,128)(2,1)S(1)}, bf16[4,198,256]{2,1,0:T(8,128)(2,1)S(1)}, u32[]{:S(2)}, u32[]{:S(2)}) %collective-permute-start.6) | collective-permute-done | bytes 405536 | tf_op jit(solution)/shard_map/ppermute | solution.py:149
  25.1 3.6 %collective-permute-done.4 = bf16[4,198,256]{2,1,0:T(8,128)(2,1)S(1)} collective-permute-done((bf16[4,198,256]{2,1,0:T(8,128)(2,1)S(1)}, bf16[4,198,256]{2,1,0:T(8,128)(2,1)S(1)}, u32[]{:S(2)}, u32[]{:S(2)}) %collective-permute-start.4) | collective-permute-done | bytes 405536 | tf_op jit(solution)/shard_map/ppermute | solution.py:149
  33.4 3.6 %collective-permute-done.8 = bf16[198,256]{1,0:T(8,128)(2,1)S(1)} collective-permute-done((bf16[198,256]{1,0:T(8,128)(2,1)S(1)}, bf16[198,256]{1,0:T(8,128)(2,1)S(1)}, u32[]{:S(2)}, u32[]{:S(2)}) %collective-permute-start.8) | collective-permute-done | bytes 101408 | tf_op jit(solution)/shard_map/ppermute | solution.py:154
  38.8 3.3 %collective-permute-start.11 = (bf16[198,256]{1,0:T(8,128)(2,1)S(1)}, bf16[198,256]{1,0:T(8,128)(2,1)S(1)}, u32[]{:S(2)}, u32[]{:S(2)}) collective-permute-start(bf16[198,256]{1,0:T(8,128)(2,1)S(1)} %fusion.14.a), channel_id=1, source_target_pairs={{0,2},{1,3},{2,0},{3,1},{4,6},{5,7},{6,4},{7,5},{8,10},{9,11},{10,... | collective-permute-start | bytes 304136 | tf_op jit(solution)/shard_map/ppermute | solution.py:159
  45.9 3.5 %shard_map.71 = (bf16[198,256]{1,0:T(8,128)(2,1)S(1)}, bf16[4,198,256]{2,1,0:T(8,128)(2,1)S(1)}, bf16[4,198,256]{2,1,0:T(8,128)(2,1)S(1)}, bf16[4,198,256]{2,1,0:T(8,128)(2,1)S(1)}, bf16[4,198,256]{2,1,0:T(8,128)(2,1)S(1)}) custom-call(s32[16]{0:T(128)S(1)} %multiply_add_fusion.order, bf16[198,256]{1,0:T(8,128)(2,1)S(1)} %fusion.14.a, ...), custom_call_target="tpu_custom_call" | custom-call | flops 415236096 | bytes 4194304 | tf_op jit(solution)/shard_map/pallas_call | solution.py:126
  49.5 4.8 %collective-permute-start.18 = (bf16[4,198,256]{2,1,0:T(8,128)(2,1)S(1)}, bf16[4,198,256]{2,1,0:T(8,128)(2,1)S(1)}, u32[]{:S(2)}, u32[]{:S(2)}) collective-permute-start(bf16[4,198,256]{2,1,0:T(8,128)(2,1)S(1)} %get-tuple-element.55), channel_id=1, source_target_pairs={{0,4},{4,0},{1,5},{5,1},{2,6},{6,2},{3,7},{7,3},{8,12},{12,8},{9,1... | collective-permute-start | bytes 1216520 | tf_op jit(solution)/shard_map/ppermute | solution.py:51
  54.8 3.3 %shard_map.72 = (bf16[4,198,256]{2,1,0:T(8,128)(2,1)S(1)}, bf16[4,198,256]{2,1,0:T(8,128)(2,1)S(1)}, bf16[4,198,256]{2,1,0:T(8,128)(2,1)S(1)}, bf16[4,198,256]{2,1,0:T(8,128)(2,1)S(1)}, bf16[198,198]{1,0:T(8,128)(2,1)S(1)}) custom-call(s32[16]{0:T(128)S(1)} %multiply_add_fusion.1.order, bf16[198,256]{1,0:T(8,128)(2,1)S(1)} %get-tuple-element.47.left, ...), custom_call_target="tpu_custom_call" | custom-call | flops 415236096 | bytes 4194304 | tf_op jit(solution)/shard_map/pallas_call | solution.py:126
  62.1 7.7 %collective-permute-done.19 = bf16[4,198,256]{2,1,0:T(8,128)(2,1)S(1)} collective-permute-done((bf16[4,198,256]{2,1,0:T(8,128)(2,1)S(1)}, bf16[4,198,256]{2,1,0:T(8,128)(2,1)S(1)}, u32[]{:S(2)}, u32[]{:S(2)}) %collective-permute-start.19) | collective-permute-done | bytes 405536 | tf_op jit(solution)/shard_map/ppermute | solution.py:149
  69.8 3.3 %collective-permute-done.17 = bf16[4,198,256]{2,1,0:T(8,128)(2,1)S(1)} collective-permute-done((bf16[4,198,256]{2,1,0:T(8,128)(2,1)S(1)}, bf16[4,198,256]{2,1,0:T(8,128)(2,1)S(1)}, u32[]{:S(2)}, u32[]{:S(2)}) %collective-permute-start.17) | collective-permute-done | bytes 405536 | tf_op jit(solution)/shard_map/ppermute | solution.py:149
  87.3 3.3 %shard_map.73 = (bf16[198,256]{1,0:T(8,128)(2,1)S(1)}, bf16[4,198,256]{2,1,0:T(8,128)(2,1)S(1)}, bf16[4,198,256]{2,1,0:T(8,128)(2,1)S(1)}, bf16[4,198,256]{2,1,0:T(8,128)(2,1)S(1)}, bf16[4,198,256]{2,1,0:T(8,128)(2,1)S(1)}) custom-call(s32[16]{0:T(128)S(1)} %multiply_add_fusion.order, bf16[198,256]{1,0:T(8,128)(2,1)S(1)} %fusion.11.a, ...), custom_call_target="tpu_custom_call" | custom-call | flops 415236096 | bytes 4194304 | tf_op jit(solution)/shard_map/pallas_call | solution.py:126
  90.6 3.6 %collective-permute-start.31 = (bf16[4,198,256]{2,1,0:T(8,128)(2,1)S(1)}, bf16[4,198,256]{2,1,0:T(8,128)(2,1)S(1)}, u32[]{:S(2)}, u32[]{:S(2)}) collective-permute-start(bf16[4,198,256]{2,1,0:T(8,128)(2,1)S(1)} %get-tuple-element.64), channel_id=1, source_target_pairs={{0,4},{4,0},{1,5},{5,1},{2,6},{6,2},{3,7},{7,3},{8,12},{12,8},{9,1... | collective-permute-start | bytes 1216520 | tf_op jit(solution)/shard_map/ppermute | solution.py:51
  94.8 3.3 %shard_map.74 = (bf16[4,198,256]{2,1,0:T(8,128)(2,1)S(1)}, bf16[4,198,256]{2,1,0:T(8,128)(2,1)S(1)}, bf16[4,198,256]{2,1,0:T(8,128)(2,1)S(1)}, bf16[4,198,256]{2,1,0:T(8,128)(2,1)S(1)}) custom-call(s32[16]{0:T(128)S(1)} %multiply_add_fusion.1.order, bf16[198,256]{1,0:T(8,128)(2,1)S(1)} %get-tuple-element.56.left, bf16[512,8192]{1,0:T(8,128)(2,1)} %bitcast.54), custom_call_target="tpu_custom_call" | custom-call | flops 415236096 | bytes 4194304 | tf_op jit(solution)/shard_map/pallas_call | solution.py:126
  102.0 7.7 %collective-permute-done.32 = bf16[4,198,256]{2,1,0:T(8,128)(2,1)S(1)} collective-permute-done((bf16[4,198,256]{2,1,0:T(8,128)(2,1)S(1)}, bf16[4,198,256]{2,1,0:T(8,128)(2,1)S(1)}, u32[]{:S(2)}, u32[]{:S(2)}) %collective-permute-start.32) | collective-permute-done | bytes 405536 | tf_op jit(solution)/shard_map/ppermute | solution.py:149
  109.7 3.6 %collective-permute-done.30 = bf16[4,198,256]{2,1,0:T(8,128)(2,1)S(1)} collective-permute-done((bf16[4,198,256]{2,1,0:T(8,128)(2,1)S(1)}, bf16[4,198,256]{2,1,0:T(8,128)(2,1)S(1)}, u32[]{:S(2)}, u32[]{:S(2)}) %collective-permute-start.30) | collective-permute-done | bytes 405536 | tf_op jit(solution)/shard_map/ppermute | solution.py:149
  126.9 3.5 %shard_map.75 = (bf16[198,256]{1,0:T(8,128)(2,1)S(1)}, bf16[4,198,256]{2,1,0:T(8,128)(2,1)S(1)}, bf16[4,198,256]{2,1,0:T(8,128)(2,1)S(1)}, bf16[4,198,256]{2,1,0:T(8,128)(2,1)S(1)}, bf16[4,198,256]{2,1,0:T(8,128)(2,1)S(1)}) custom-call(s32[16]{0:T(128)S(1)} %multiply_add_fusion.order, bf16[198,256]{1,0:T(8,128)(2,1)S(1)} %fusion.8.a, ...), custom_call_target="tpu_custom_call" | custom-call | flops 415236096 | bytes 4194304 | tf_op jit(solution)/shard_map/pallas_call | solution.py:126
  130.4 3.3 %shard_map.76 = (bf16[4,198,256]{2,1,0:T(8,128)(2,1)S(1)}, bf16[4,198,256]{2,1,0:T(8,128)(2,1)S(1)}, bf16[4,198,256]{2,1,0:T(8,128)(2,1)S(1)}, bf16[4,198,256]{2,1,0:T(8,128)(2,1)S(1)}, bf16[198,198]{1,0:T(8,128)(2,1)S(1)}) custom-call(s32[16]{0:T(128)S(1)} %multiply_add_fusion.1.order, bf16[198,256]{1,0:T(8,128)(2,1)S(1)} %get-tuple-element.65.left, ...), custom_call_target="tpu_custom_call" | custom-call | flops 415236096 | bytes 4194304 | tf_op jit(solution)/shard_map/pallas_call | solution.py:126
  133.8 5.1 %collective-permute-start.40 = (bf16[198,198]{1,0:T(8,128)(2,1)S(1)}, bf16[198,198]{1,0:T(8,128)(2,1)S(1)}, u32[]{:S(2)}, u32[]{:S(2)}) collective-permute-start(bf16[198,198]{1,0:T(8,128)(2,1)S(1)} %broadcast_select_fusion), channel_id=1, source_target_pairs={{0,4},{4,0},{1,5},{5,1},{2,6},{6,2},{3,7},{7,3},{8,12},{12,8},{9,1... | collective-permute-start | bytes 235232 | tf_op jit(solution)/shard_map/ppermute | solution.py:51
  145.6 10.1 %collective-permute-done.46 = bf16[5,198,256]{2,1,0:T(8,128)(2,1)S(1)} collective-permute-done((bf16[5,198,256]{2,1,0:T(8,128)(2,1)S(1)}, bf16[5,198,256]{2,1,0:T(8,128)(2,1)S(1)}, u32[]{:S(2)}, u32[]{:S(2)}) %collective-permute-start.46) | collective-permute-done | bytes 506912 | tf_op jit(solution)/shard_map/ppermute | solution.py:149
  155.7 3.1 %collective-permute-done.44 = bf16[5,198,256]{2,1,0:T(8,128)(2,1)S(1)} collective-permute-done((bf16[5,198,256]{2,1,0:T(8,128)(2,1)S(1)}, bf16[5,198,256]{2,1,0:T(8,128)(2,1)S(1)}, u32[]{:S(2)}, u32[]{:S(2)}) %collective-permute-start.44) | collective-permute-done | bytes 506912 | tf_op jit(solution)/shard_map/ppermute | solution.py:149
  163.9 3.8 %collective-permute-done.48 = bf16[2,198,256]{2,1,0:T(8,128)(2,1)S(1)} collective-permute-done((bf16[2,198,256]{2,1,0:T(8,128)(2,1)S(1)}, bf16[2,198,256]{2,1,0:T(8,128)(2,1)S(1)}, u32[]{:S(2)}, u32[]{:S(2)}) %collective-permute-start.48) | collective-permute-done | bytes 202784 | tf_op jit(solution)/shard_map/ppermute | solution.py:154
  170.5 3.8 %collective-permute-done.52 = bf16[2,198,256]{2,1,0:T(8,128)(2,1)S(1)} collective-permute-done((bf16[2,198,256]{2,1,0:T(8,128)(2,1)S(1)}, bf16[2,198,256]{2,1,0:T(8,128)(2,1)S(1)}, u32[]{:S(2)}, u32[]{:S(2)}) %collective-permute-start.52) | collective-permute-done | bytes 202784 | tf_op jit(solution)/shard_map/ppermute | solution.py:159
  176.0 5.2 %collective-permute-done.50 = bf16[2,198,256]{2,1,0:T(8,128)(2,1)S(1)} collective-permute-done((bf16[2,198,256]{2,1,0:T(8,128)(2,1)S(1)}, bf16[2,198,256]{2,1,0:T(8,128)(2,1)S(1)}, u32[]{:S(2)}, u32[]{:S(2)}) %collective-permute-start.50) | collective-permute-done | bytes 202784 | tf_op jit(solution)/shard_map/ppermute | solution.py:159
  (157 shorter events, 80.0 us)
Async XLA Ops:
  5.1 6.6 %collective-permute-start.5 = (bf16[4,198,256]{2,1,0:T(8,128)(2,1)S(1)}, bf16[4,198,256]{2,1,0:T(8,128)(2,1)}, u32[]{:S(2)}, u32[]{:S(2)}) collective-permute-start(bf16[4,198,256]{2,1,0:T(8,128)(2,1)S(1)} %get-tuple-element.46), channel_id=1, source_target_pairs={{0,4},{4,0},{1,5},{5,1},{2,6},{6,2},{3,7},{7,3},{8,12},{12,8},{9,1... | collective-permute-start | bytes 1216520 | tf_op jit(solution)/shard_map/ppermute | solution.py:51
  6.5 9.2 %collective-permute-start.3 = (bf16[4,198,256]{2,1,0:T(8,128)(2,1)S(1)}, bf16[4,198,256]{2,1,0:T(8,128)(2,1)S(1)}, u32[]{:S(2)}, u32[]{:S(2)}) collective-permute-start(bf16[4,198,256]{2,1,0:T(8,128)(2,1)S(1)} %get-tuple-element.44), channel_id=1, source_target_pairs={{0,4},{4,0},{1,5},{5,1},{2,6},{6,2},{3,7},{7,3},{8,12},{12,8},{9,1... | collective-permute-start | bytes 1216520 | tf_op jit(solution)/shard_map/ppermute | solution.py:51
  6.6 9.4 %collective-permute-start.1 = (bf16[4,198,256]{2,1,0:T(8,128)(2,1)S(1)}, bf16[4,198,256]{2,1,0:T(8,128)(2,1)S(1)}, u32[]{:S(2)}, u32[]{:S(2)}) collective-permute-start(bf16[4,198,256]{2,1,0:T(8,128)(2,1)S(1)} %get-tuple-element.42), channel_id=1, source_target_pairs={{0,4},{4,0},{1,5},{5,1},{2,6},{6,2},{3,7},{7,3},{8,12},{12,8},{9,1... | collective-permute-start | bytes 1216520 | tf_op jit(solution)/shard_map/ppermute | solution.py:51
  7.0 12.9 %collective-permute-start = (bf16[4,198,256]{2,1,0:T(8,128)(2,1)S(1)}, bf16[4,198,256]{2,1,0:T(8,128)(2,1)S(1)}, u32[]{:S(2)}, u32[]{:S(2)}) collective-permute-start(bf16[4,198,256]{2,1,0:T(8,128)(2,1)S(1)} %get-tuple-element.40), channel_id=1, source_target_pairs={{0,4},{4,0},{1,5},{5,1},{2,6},{6,2},{3,7},{7,3},{8,12},{12,8},{9,1... | collective-permute-start | bytes 1216520 | tf_op jit(solution)/shard_map/ppermute | solution.py:51
  12.9 12.2 %collective-permute-start.6 = (bf16[4,198,256]{2,1,0:T(8,128)(2,1)S(1)}, bf16[4,198,256]{2,1,0:T(8,128)(2,1)S(1)}, u32[]{:S(2)}, u32[]{:S(2)}) collective-permute-start(bf16[4,198,256]{2,1,0:T(8,128)(2,1)S(1)} %add_convert_fusion.16), channel_id=1, source_target_pairs={{0,24},{4,100},{8,0},{12,108},{16,8},{20,116},{24,16},{28,124},{32... | collective-permute-start | bytes 1216520 | tf_op jit(solution)/shard_map/ppermute | solution.py:149
  15.9 12.8 %collective-permute-start.4 = (bf16[4,198,256]{2,1,0:T(8,128)(2,1)S(1)}, bf16[4,198,256]{2,1,0:T(8,128)(2,1)S(1)}, u32[]{:S(2)}, u32[]{:S(2)}) collective-permute-start(bf16[4,198,256]{2,1,0:T(8,128)(2,1)S(1)} %add_convert_fusion.17), channel_id=1, source_target_pairs={{0,8},{4,36},{8,16},{12,44},{16,24},{20,52},{24,0},{28,60},{32,40}... | collective-permute-start | bytes 1216520 | tf_op jit(solution)/shard_map/ppermute | solution.py:149
  16.1 12.6 %collective-permute-start.2 = (bf16[4,198,256]{2,1,0:T(8,128)(2,1)S(1)}, bf16[4,198,256]{2,1,0:T(8,128)(2,1)S(1)}, u32[]{:S(2)}, u32[]{:S(2)}) collective-permute-start(bf16[4,198,256]{2,1,0:T(8,128)(2,1)S(1)} %add_convert_fusion.18), channel_id=1, source_target_pairs={{0,16},{4,68},{8,24},{12,76},{16,0},{20,84},{24,8},{28,92},{32,48}... | collective-permute-start | bytes 1216520 | tf_op jit(solution)/shard_map/ppermute | solution.py:149
  49.5 8.7 %collective-permute-start.18 = (bf16[4,198,256]{2,1,0:T(8,128)(2,1)S(1)}, bf16[4,198,256]{2,1,0:T(8,128)(2,1)S(1)}, u32[]{:S(2)}, u32[]{:S(2)}) collective-permute-start(bf16[4,198,256]{2,1,0:T(8,128)(2,1)S(1)} %get-tuple-element.55), channel_id=1, source_target_pairs={{0,4},{4,0},{1,5},{5,1},{2,6},{6,2},{3,7},{7,3},{8,12},{12,8},{9,1... | collective-permute-start | bytes 1216520 | tf_op jit(solution)/shard_map/ppermute | solution.py:51
  54.7 7.4 %collective-permute-start.13 = (bf16[4,198,256]{2,1,0:T(8,128)(2,1)S(1)}, bf16[4,198,256]{2,1,0:T(8,128)(2,1)S(1)}, u32[]{:S(2)}, u32[]{:S(2)}) collective-permute-start(bf16[4,198,256]{2,1,0:T(8,128)(2,1)S(1)} %get-tuple-element.49), channel_id=1, source_target_pairs={{0,4},{4,0},{1,5},{5,1},{2,6},{6,2},{3,7},{7,3},{8,12},{12,8},{9,1... | collective-permute-start | bytes 1216520 | tf_op jit(solution)/shard_map/ppermute | solution.py:51
  58.3 11.5 %collective-permute-start.19 = (bf16[4,198,256]{2,1,0:T(8,128)(2,1)S(1)}, bf16[4,198,256]{2,1,0:T(8,128)(2,1)S(1)}, u32[]{:S(2)}, u32[]{:S(2)}) collective-permute-start(bf16[4,198,256]{2,1,0:T(8,128)(2,1)S(1)} %add_convert_fusion.11), channel_id=1, source_target_pairs={{0,24},{4,100},{8,0},{12,108},{16,8},{20,116},{24,16},{28,124},{32... | collective-permute-start | bytes 1216520 | tf_op jit(solution)/shard_map/ppermute | solution.py:149
  60.6 12.5 %collective-permute-start.17 = (bf16[4,198,256]{2,1,0:T(8,128)(2,1)S(1)}, bf16[4,198,256]{2,1,0:T(8,128)(2,1)S(1)}, u32[]{:S(2)}, u32[]{:S(2)}) collective-permute-start(bf16[4,198,256]{2,1,0:T(8,128)(2,1)S(1)} %add_convert_fusion.12), channel_id=1, source_target_pairs={{0,8},{4,36},{8,16},{12,44},{16,24},{20,52},{24,0},{28,60},{32,40}... | collective-permute-start | bytes 1216520 | tf_op jit(solution)/shard_map/ppermute | solution.py:149
  60.8 12.3 %collective-permute-start.15 = (bf16[4,198,256]{2,1,0:T(8,128)(2,1)S(1)}, bf16[4,198,256]{2,1,0:T(8,128)(2,1)S(1)}, u32[]{:S(2)}, u32[]{:S(2)}) collective-permute-start(bf16[4,198,256]{2,1,0:T(8,128)(2,1)S(1)} %add_convert_fusion.13), channel_id=1, source_target_pairs={{0,16},{4,68},{8,24},{12,76},{16,0},{20,84},{24,8},{28,92},{32,48}... | collective-permute-start | bytes 1216520 | tf_op jit(solution)/shard_map/ppermute | solution.py:149
  90.6 7.5 %collective-permute-start.31 = (bf16[4,198,256]{2,1,0:T(8,128)(2,1)S(1)}, bf16[4,198,256]{2,1,0:T(8,128)(2,1)S(1)}, u32[]{:S(2)}, u32[]{:S(2)}) collective-permute-start(bf16[4,198,256]{2,1,0:T(8,128)(2,1)S(1)} %get-tuple-element.64), channel_id=1, source_target_pairs={{0,4},{4,0},{1,5},{5,1},{2,6},{6,2},{3,7},{7,3},{8,12},{12,8},{9,1... | collective-permute-start | bytes 1216520 | tf_op jit(solution)/shard_map/ppermute | solution.py:51
  94.7 7.3 %collective-permute-start.26 = (bf16[4,198,256]{2,1,0:T(8,128)(2,1)S(1)}, bf16[4,198,256]{2,1,0:T(8,128)(2,1)S(1)}, u32[]{:S(2)}, u32[]{:S(2)}) collective-permute-start(bf16[4,198,256]{2,1,0:T(8,128)(2,1)S(1)} %get-tuple-element.58), channel_id=1, source_target_pairs={{0,4},{4,0},{1,5},{5,1},{2,6},{6,2},{3,7},{7,3},{8,12},{12,8},{9,1... | collective-permute-start | bytes 1216520 | tf_op jit(solution)/shard_map/ppermute | solution.py:51
  98.2 11.5 %collective-permute-start.32 = (bf16[4,198,256]{2,1,0:T(8,128)(2,1)S(1)}, bf16[4,198,256]{2,1,0:T(8,128)(2,1)S(1)}, u32[]{:S(2)}, u32[]{:S(2)}) collective-permute-start(bf16[4,198,256]{2,1,0:T(8,128)(2,1)S(1)} %add_convert_fusion.6), channel_id=1, source_target_pairs={{0,24},{4,100},{8,0},{12,108},{16,8},{20,116},{24,16},{28,124},{32... | collective-permute-start | bytes 1216520 | tf_op jit(solution)/shard_map/ppermute | solution.py:149
  100.5 12.7 %collective-permute-start.30 = (bf16[4,198,256]{2,1,0:T(8,128)(2,1)S(1)}, bf16[4,198,256]{2,1,0:T(8,128)(2,1)S(1)}, u32[]{:S(2)}, u32[]{:S(2)}) collective-permute-start(bf16[4,198,256]{2,1,0:T(8,128)(2,1)S(1)} %add_convert_fusion.7), channel_id=1, source_target_pairs={{0,8},{4,36},{8,16},{12,44},{16,24},{20,52},{24,0},{28,60},{32,40}... | collective-permute-start | bytes 1216520 | tf_op jit(solution)/shard_map/ppermute | solution.py:149
  100.7 12.5 %collective-permute-start.28 = (bf16[4,198,256]{2,1,0:T(8,128)(2,1)S(1)}, bf16[4,198,256]{2,1,0:T(8,128)(2,1)S(1)}, u32[]{:S(2)}, u32[]{:S(2)}) collective-permute-start(bf16[4,198,256]{2,1,0:T(8,128)(2,1)S(1)} %add_convert_fusion.8), channel_id=1, source_target_pairs={{0,16},{4,68},{8,24},{12,76},{16,0},{20,84},{24,8},{28,92},{32,48}... | collective-permute-start | bytes 1216520 | tf_op jit(solution)/shard_map/ppermute | solution.py:149
  142.0 13.7 %collective-permute-start.46 = (bf16[5,198,256]{2,1,0:T(8,128)(2,1)S(1)}, bf16[5,198,256]{2,1,0:T(8,128)(2,1)S(1)}, u32[]{:S(2)}, u32[]{:S(2)}) collective-permute-start(bf16[5,198,256]{2,1,0:T(8,128)(2,1)S(1)} %get-tuple-element.101), channel_id=1, source_target_pairs={{0,24},{4,100},{8,0},{12,108},{16,8},{20,116},{24,16},{28,124},{32... | collective-permute-start | bytes 1520648 | tf_op jit(solution)/shard_map/ppermute | solution.py:149
  144.2 14.6 %collective-permute-start.44 = (bf16[5,198,256]{2,1,0:T(8,128)(2,1)S(1)}, bf16[5,198,256]{2,1,0:T(8,128)(2,1)S(1)}, u32[]{:S(2)}, u32[]{:S(2)}) collective-permute-start(bf16[5,198,256]{2,1,0:T(8,128)(2,1)S(1)} %get-tuple-element.100), channel_id=1, source_target_pairs={{0,8},{4,36},{8,16},{12,44},{16,24},{20,52},{24,0},{28,60},{32,40}... | collective-permute-start | bytes 1520648 | tf_op jit(solution)/shard_map/ppermute | solution.py:149
  144.2 14.6 %collective-permute-start.42 = (bf16[5,198,256]{2,1,0:T(8,128)(2,1)S(1)}, bf16[5,198,256]{2,1,0:T(8,128)(2,1)S(1)}, u32[]{:S(2)}, u32[]{:S(2)}) collective-permute-start(bf16[5,198,256]{2,1,0:T(8,128)(2,1)S(1)} %get-tuple-element.99), channel_id=1, source_target_pairs={{0,16},{4,68},{8,24},{12,76},{16,0},{20,84},{24,8},{28,92},{32,48}... | collective-permute-start | bytes 1520648 | tf_op jit(solution)/shard_map/ppermute | solution.py:149
  159.3 8.4 %collective-permute-start.48 = (bf16[2,198,256]{2,1,0:T(8,128)(2,1)S(1)}, bf16[2,198,256]{2,1,0:T(8,128)(2,1)S(1)}, u32[]{:S(2)}, u32[]{:S(2)}) collective-permute-start(bf16[2,198,256]{2,1,0:T(8,128)(2,1)S(1)} %get-tuple-element.98), channel_id=1, source_target_pairs={{4,12},{0,32},{12,20},{8,40},{20,28},{16,48},{28,4},{24,56},{36,44... | collective-permute-start | bytes 608264 | tf_op jit(solution)/shard_map/ppermute | solution.py:154
  160.9 6.9 %collective-permute-start.47 = (bf16[2,198,256]{2,1,0:T(8,128)(2,1)S(1)}, bf16[2,198,256]{2,1,0:T(8,128)(2,1)S(1)}, u32[]{:S(2)}, u32[]{:S(2)}) collective-permute-start(bf16[2,198,256]{2,1,0:T(8,128)(2,1)S(1)} %get-tuple-element.97), channel_id=1, source_target_pairs={{4,20},{0,64},{12,28},{8,72},{20,4},{16,80},{28,12},{24,88},{36,52... | collective-permute-start | bytes 608264 | tf_op jit(solution)/shard_map/ppermute | solution.py:154
  167.8 6.5 %collective-permute-start.52 = (bf16[2,198,256]{2,1,0:T(8,128)(2,1)S(1)}, bf16[2,198,256]{2,1,0:T(8,128)(2,1)S(1)}, u32[]{:S(2)}, u32[]{:S(2)}) collective-permute-start(bf16[2,198,256]{2,1,0:T(8,128)(2,1)S(1)} %add_convert_fusion.20), channel_id=1, source_target_pairs={{0,3},{1,0},{2,1},{3,2},{4,7},{5,4},{6,5},{7,6},{8,11},{9,8},{10,9... | collective-permute-start | bytes 608264 | tf_op jit(solution)/shard_map/ppermute | solution.py:159
  169.9 11.4 %collective-permute-start.50 = (bf16[2,198,256]{2,1,0:T(8,128)(2,1)S(1)}, bf16[2,198,256]{2,1,0:T(8,128)(2,1)S(1)}, u32[]{:S(2)}, u32[]{:S(2)}) collective-permute-start(bf16[2,198,256]{2,1,0:T(8,128)(2,1)S(1)} %add_convert_fusion.20), channel_id=1, source_target_pairs={{0,1},{1,2},{2,3},{3,0},{4,5},{5,6},{6,7},{7,4},{8,9},{9,10},{10,1... | collective-permute-start | bytes 608264 | tf_op jit(solution)/shard_map/ppermute | solution.py:159
  (35 other events, 193.3 us)

commit v3 on v2

v3 whole, which is shorter than its diff:
```python
import functools

import jax
import jax.numpy as jnp
from jax import lax
from jax.experimental import pallas as pl
from jax.experimental.pallas import tpu as pltpu
from jax.sharding import Mesh
from jax.sharding import PartitionSpec as P

BOND_DIM = 8192
PHYSICAL = 4
MPO_BOND = 66
LEFT_ROWS = 3
SITE_COUNT = 2
ROWS = LEFT_ROWS * MPO_BOND
BOND = ("y", "x", "core")
RING = 4
BLOCK = 256
SENT = (2, 1, 3, 0)
LOADS = 8
LOAD_GRANT = 48 * 2**20
GRANT = 16 * 2**20
F32 = jnp.float32
BF16 = jnp.bfloat16


def summed(terms):
    total = terms[0].astype(F32)
    for term in terms[1:]:
        total = total + term.astype(F32)
    return total


def chip_device(y, x, core):
    return (y % RING * RING + x % RING) * 2 + core


def shifts(step, x_core):
    pairs = []
    for y in range(RING):
        for x in range(RING):
            pairs.append((chip_device(y, x, x_core), chip_device(y, x + step, x_core)))
            other = 1 - x_core
            pairs.append((chip_device(y, x, other), chip_device(y + step, x, other)))
    return pairs


def ring_shift(step):
    return [(i, (i + step) % RING) for i in range(RING)]


def swap_cores(array):
    return lax.ppermute(array, "core", [(0, 1), (1, 0)])


def block_order(core):
    y, x = lax.axis_index("y"), lax.axis_index("x")
    far = jnp.repeat(jnp.arange(RING), RING)
    near = jnp.tile(jnp.arange(RING), RING)
    dy = jnp.where(core == 0, near, far)
    dx = jnp.where(core == 0, far, near)
    return (((y + dy) % RING * RING + (x + dx) % RING) * 2 + core).astype(jnp.int32)


def load_kernel(site, after, weights, loaded, sems):
    rows = BLOCK // LOADS
    copies = []
    for i in range(LOADS):
        source = weights.at[pl.ds(site * BLOCK + i * rows, rows), :]
        copies.append(
            pltpu.make_async_copy(source, loaded.at[pl.ds(i * rows, rows), :], sems.at[i])
        )
        copies[-1].start()
    for copy in copies:
        copy.wait()


def load(site, weights, after):
    return pl.pallas_call(
        functools.partial(load_kernel, site),
        out_shape=jax.ShapeDtypeStruct((BLOCK, BOND_DIM), BF16),
        in_specs=[pl.BlockSpec(memory_space=pl.ANY)] * 2,
        out_specs=VMEM,
        scratch_shapes=[pltpu.SemaphoreType.DMA((LOADS,))],
        compiler_params=pltpu.CompilerParams(vmem_limit_bytes=LOAD_GRANT),
        cost_estimate=pl.CostEstimate(flops=0, bytes_accessed=4 * 2**20, transcendentals=0),
    )(after, weights)


def multiply_kernel(prepare, given, order, *refs):
    operands, weights, refs = refs[:given], refs[given], refs[given + 1 :]
    if prepare is None:
        left, outs = operands[0], refs
    else:
        left, outs = refs[0], refs[1:]
        left[...] = prepare(*operands).astype(BF16)
    for group in range(len(outs) // RING):
        for d in SENT:
            for e in range(RING):
                number = order[(group * RING + d) * RING + e]
                columns = weights[:, pl.ds(pl.multiple_of(number * BLOCK, BLOCK), BLOCK)]
                product = jnp.dot(left[...], columns, preferred_element_type=F32)
                outs[group * RING + d][e] = product.astype(BF16)


def direct_kernel(site, order, left, weights, *rest):
    outs, (tiles, sems) = rest[:RING], rest[RING:]
    width = RING * BLOCK
    copies = []
    for i in range(RING**2):
        first = pl.multiple_of(order[i] * BLOCK, BLOCK)
        source = weights.at[pl.ds(site * BLOCK, BLOCK), pl.ds(first, BLOCK)]
        target = tiles.at[:, pl.ds(i * BLOCK, BLOCK)]
        copies.append(pltpu.make_async_copy(source, target, sems.at[i]))
    for d in SENT:
        for e in range(RING):
            copies[d * RING + e].start()
    for d in SENT:
        for e in range(RING):
            copies[d * RING + e].wait()
        columns = tiles[:, d * width : (d + 1) * width]
        product = jnp.dot(left[...], columns, preferred_element_type=F32).astype(BF16)
        for e in range(RING):
            outs[d][e] = product[:, e * BLOCK : (e + 1) * BLOCK]


def multiply_direct(site, left, order, weights):
    return pl.pallas_call(
        functools.partial(direct_kernel, site),
        out_shape=[jax.ShapeDtypeStruct((RING, ROWS, BLOCK), BF16)] * RING,
        in_specs=[pl.BlockSpec(memory_space=pltpu.SMEM), VMEM, pl.BlockSpec(memory_space=pl.ANY)],
        out_specs=[VMEM] * RING,
        scratch_shapes=[
            pltpu.VMEM((BLOCK, RING**2 * BLOCK), BF16),
            pltpu.SemaphoreType.DMA((RING**2,)),
        ],
        compiler_params=pltpu.CompilerParams(vmem_limit_bytes=LOAD_GRANT),
        cost_estimate=pl.CostEstimate(flops=10**9, bytes_accessed=2**22, transcendentals=0),
    )(order, left, weights)


def gram_kernel(*refs):
    kept, gram = refs[-2:]
    whole = lax.dot_general(
        kept[...], kept[...], (((1,), (1,)), ((), ())), preferred_element_type=F32
    )
    gram[...] = (whole * (1.0 / BOND_DIM)).astype(BF16)


def gram_of(kept, after):
    return pl.pallas_call(
        gram_kernel,
        out_shape=jax.ShapeDtypeStruct((ROWS, ROWS), BF16),
        in_specs=[pl.BlockSpec(memory_space=pl.ANY)] * len(after) + [VMEM],
        out_specs=VMEM,
        compiler_params=pltpu.CompilerParams(vmem_limit_bytes=GRANT),
        cost_estimate=pl.CostEstimate(flops=10**8, bytes_accessed=10**5, transcendentals=0),
    )(*after, kept)


def total(a, b, c, d):
    return summed([a[...], b[...], c[...], d[...]])


def mix(a, b, c, d, mixing, chosen):
    mixed = jnp.dot(mixing[0], a[...], preferred_element_type=F32)
    for i, part in enumerate((b, c, d)):
        mixed = mixed + jnp.dot(mixing[i + 1], part[...], preferred_element_type=F32)
    return mixed * chosen[...]


VMEM = pl.BlockSpec(memory_space=pltpu.VMEM)


def multiply(prepare, operands, order, weights):
    rows = operands[0].shape[0]
    groups = len(order) // RING**2
    shapes = [jax.ShapeDtypeStruct((RING, rows, BLOCK), BF16)] * (RING * groups)
    if prepare is not None:
        shapes = [jax.ShapeDtypeStruct((rows, BLOCK), BF16), *shapes]
    flops = 2 * rows * BLOCK * BLOCK * RING**2 * groups
    return pl.pallas_call(
        functools.partial(multiply_kernel, prepare, len(operands)),
        out_shape=shapes,
        in_specs=[pl.BlockSpec(memory_space=pltpu.SMEM)] + [VMEM] * (len(operands) + 1),
        out_specs=[VMEM] * len(shapes),
        compiler_params=pltpu.CompilerParams(vmem_limit_bytes=GRANT),
        cost_estimate=pl.CostEstimate(
            flops=flops, bytes_accessed=2**20, transcendentals=0
        ),
    )(order, *operands, weights)


def to_cores(theirs, ours):
    arrived = [swap_cores(theirs[d]) for d in SENT]
    return {d: summed([ours[d], got]).astype(BF16) for d, got in zip(SENT, arrived)}


def along_first(mine):
    got = [lax.ppermute(mine[d], BOND, shifts(d, 0)) for d in (2, 1, 3)]
    return summed([mine[0], *got]).astype(BF16)


def along_second(pieces):
    got = [lax.ppermute(pieces[e], BOND, shifts(e, 1)) for e in (2, 1, 3)]
    return summed([pieces[0], *got]).astype(BF16)


def along_z(array):
    return [array] + [lax.ppermute(array, "z", ring_shift(d)) for d in (1, 2, 3)]


def mixing_kernel(z, operator_tensors, mixing):
    def iota(shape, dim):
        return lax.broadcasted_iota(jnp.int32, shape, dim)

    wide, tall = (ROWS, PHYSICAL * MPO_BOND), (MPO_BOND, ROWS)
    first = z[0] * MPO_BOND
    pick = (iota(wide, 1) == first + lax.rem(iota(wide, 0), MPO_BOND)).astype(BF16)
    spread = (iota(tall, 0) == lax.rem(iota(tall, 1), MPO_BOND)).astype(BF16)
    square = (ROWS, ROWS)
    same = lax.div(iota(square, 0), MPO_BOND) == lax.div(iota(square, 1), MPO_BOND)
    for site in range(SITE_COUNT):
        for d in range(RING):
            weights = operator_tensors[site, lax.rem(z[0] + RING - d, RING)]
            narrow = lax.dot_general(
                pick, weights, (((1,), (1,)), ((), ())), preferred_element_type=F32
            ).astype(BF16)
            full = jnp.dot(narrow, spread, preferred_element_type=F32)
            mixing[site, d] = jnp.where(same, full, 0.0).astype(BF16)


def mixing_weights(operator_tensors):
    return pl.pallas_call(
        mixing_kernel,
        out_shape=jax.ShapeDtypeStruct((SITE_COUNT, RING, ROWS, ROWS), BF16),
        in_specs=[pl.BlockSpec(memory_space=pltpu.SMEM), VMEM],
        out_specs=VMEM,
        compiler_params=pltpu.CompilerParams(vmem_limit_bytes=8 * 2**20),
        cost_estimate=pl.CostEstimate(flops=10**9, bytes_accessed=10**6, transcendentals=0),
    )(lax.axis_index("z").astype(jnp.int32)[None], operator_tensors)


def chosen_columns(kept_columns):
    first = lax.axis_index(BOND) * BLOCK * PHYSICAL
    place = kept_columns - first
    here = (place >= 0) & (place < BLOCK * PHYSICAL) & (place % PHYSICAL == lax.axis_index("z"))
    column = place // PHYSICAL
    digits = jnp.arange(16)[None, :, None]
    high = ((column // 16)[:, None] == digits) & here[:, None]
    low = (column % 16)[:, None] == digits
    counts = jnp.einsum(
        "khn,kln->khl", high.astype(BF16), low.astype(BF16), preferred_element_type=F32
    )
    return (counts > 0.5).astype(F32).reshape(SITE_COUNT, 1, BLOCK)


def chip_gram(grams):
    first = lax.axis_index("core") == 0
    got = swap_cores(jnp.where(first, grams[1], grams[0]))
    whole = summed([jnp.where(first, grams[0], grams[1]), got])
    whole = summed(along_z(whole.astype(BF16))).astype(BF16)
    return jnp.pad(whole, ((0, 0), (0, BLOCK - ROWS)))


def both_grams(own):
    other = swap_cores(own)
    first = lax.axis_index("core") == 0
    return jnp.stack([jnp.where(first, own, other), jnp.where(first, other, own)])


def on_device(carried, site_tensors, operator_tensors, rotation, kept_columns):
    core = lax.axis_index("core")
    their_order, our_order = block_order(1 - core), block_order(core)
    tensors = site_tensors.reshape(SITE_COUNT * BLOCK, BOND_DIM)
    turns = rotation.reshape(SITE_COUNT * BLOCK, BOND_DIM)
    mixing = mixing_weights(operator_tensors)
    chosen = chosen_columns(kept_columns)
    grams, near, parts = [], None, None
    for site in range(SITE_COUNT):
        if near is None:
            theirs = multiply_direct(site, carried, their_order, tensors)
            ours = multiply_direct(site, carried, our_order, tensors)
        else:
            weights = load(site, tensors, near)
            state, *theirs = multiply(total, parts, their_order, weights)
            ours = multiply(None, [state], our_order, weights)
        near = along_first(to_cores(theirs, ours))
        parts = along_z(along_second([near[e] for e in range(RING)]))
        weights = load(site, turns, near)
        mixed = [*parts, mixing[site], chosen[site]]
        kept, *theirs = multiply(mix, mixed, their_order, weights)
        ours = multiply(None, [kept], our_order, weights)
        mine = to_cores(theirs, ours)
        grams.append(gram_of(kept, [mine[d] for d in (1, 2, 3)]))
        near = along_first(mine)
        pieces = [near[e] for e in range(RING)]
        if site == SITE_COUNT - 1:
            gram = chip_gram(grams)
            both = along_second([jnp.stack([piece, gram]) for piece in pieces])
            state = summed(along_z(both[0])).astype(BF16)
            got = [lax.ppermute(both[1], BOND, shifts(d, 0)) for d in (1, 2, 3)]
            return state, both_grams(summed([both[1], *got])[:, :ROWS])
        parts = along_z(along_second(pieces))


def solution(mesh):
    finer = Mesh(mesh.devices.reshape(RING, RING, 2, mesh.shape["mpo"]), (*BOND, "z"))
    placed = (P(None, BOND), P(None, BOND, "z", None), P(), P(None, BOND, "z", None), P())
    return jax.shard_map(
        on_device, mesh=finer, in_specs=placed, out_specs=(P(None, BOND), P()), check_vma=False
    )
```

time: 186 us -> 164 us (0.88)
  waiting for transfers between devices: 84.9 us -> 65.6 us
  Pallas kernels: 28.7 us -> 22.5 us
  starting transfers between devices: 61.3 us -> 64.5 us
    ppermute x24 -> x27, waiting for transfers between devices: 62.3 us -> 49 us  [the longest x12 30.5 us: along_first(): got = [lax.ppermute(mine[d], BOND, shifts(d, 0)) for d in (2, 1, 3)]]
    pallas_call x8 -> x13, Pallas kernels: 26.9 us -> 20.7 us  [the longest x6 7.81 us: multiply(): pl.pallas_call(functools.partial(multiply_kernel, prepare, len(operands))...]
    ppermute x12 -> x15, waiting for transfers between devices: 20.5 us -> 15.2 us  [along_z(): lax.ppermute(array, 'z', ring_shift(d))]
    ppermute x24 -> x27, starting transfers between devices: 26.6 us -> 29.3 us  [the longest x12 14 us: along_second(): got = [lax.ppermute(pieces[e], BOND, shifts(e, 1)) for e in (2, 1, 3)]]
    ppermute x12 -> x15, starting transfers between devices: 15.2 us -> 16.3 us  [along_z(): lax.ppermute(array, 'z', ring_shift(d))]
    convert_element_type x22 -> x23, other arithmetic: 3.95 us -> 4.63 us  [the longest x12 2.37 us: to_cores(): summed([ours[d], got]).astype(BF16)]
  transfers between devices with their start and end apart: 54 -> 60, of which waited for: 33 -> 32; matrix products, arithmetic and copies ran while one was open for 3% -> 3% of each run, Pallas kernels for 6% -> 9%
where the time goes in v3:
time: 164 us; the launch traced here: 162 us
  waiting for transfers between devices  65.6 us (40%)
  starting transfers between devices  64.5 us (39%)
  Pallas kernels  22.5 us (14%)
  other arithmetic  5.44 us (3%)
  local copies, waits for them, and re-layouts  2.6 us (2%)
    ppermute x12, waiting for transfers between devices, along_first(): got = [lax.ppermute(mine[d], BOND, shifts(d, 0)) for d in (2, 1, 3)]  30.5 us
    ppermute x18, starting transfers between devices, swap_cores(): return lax.ppermute(array, 'core', [(0, 1), (1, 0)])  18.9 us
    ppermute x12, waiting for transfers between devices, along_second(): got = [lax.ppermute(pieces[e], BOND, shifts(e, 1)) for e in (2, 1, 3)]  18.4 us
    ppermute x15, starting transfers between devices, along_z(): lax.ppermute(array, 'z', ring_shift(d))  16.3 us
    ppermute x15, waiting for transfers between devices, along_z(): lax.ppermute(array, 'z', ring_shift(d))  15.2 us
    ppermute x12, starting transfers between devices, along_second(): got = [lax.ppermute(pieces[e], BOND, shifts(e, 1)) for e in (2, 1, 3)]  14 us
    ppermute x12, starting transfers between devices, along_first(): got = [lax.ppermute(mine[d], BOND, shifts(d, 0)) for d in (2, 1, 3)]  13.7 us
    pallas_call x6, Pallas kernels, multiply(): pl.pallas_call(functools.partial(multiply_kernel, prepare, len(operands))...  7.81 us
  transfers between devices with their start and end apart: 60, of which 32 were waited for; matrix products, arithmetic and copies ran while one was open for 3% of the time, Pallas kernels for 9%

profile of v3, /device:TPU:1, one launch (start us, length us, event | category | flops | bytes accessed | tf_op | source)
XLA Modules:
  0.0 162.2 jit_solution(6834248997476423396)
XLA Ops:
  1.8 2.9 %shard_map.69 = (bf16[4,198,256]{2,1,0:T(8,128)(2,1)S(1)}, bf16[4,198,256]{2,1,0:T(8,128)(2,1)S(1)}, bf16[4,198,256]{2,1,0:T(8,128)(2,1)S(1)}, bf16[4,198,256]{2,1,0:T(8,128)(2,1)S(1)}) custom-call(s32[16]{0:T(128)S(1)} %multiply_add_fusion.order, bf16[198,256]{1,0:T(8,128)(2,1)S(1)} %copy-done, bf16[512,8192]{1,0:T(8,128)(2,1)} %bitcast.52), custom_call_target="tpu_custom_call" | custom-call | flops 1000000000 | bytes 4194304 | tf_op jit(solution)/shard_map/pallas_call | solution.py:129
  7.4 2.9 %shard_map.68 = (bf16[4,198,256]{2,1,0:T(8,128)(2,1)S(1)}, bf16[4,198,256]{2,1,0:T(8,128)(2,1)S(1)}, bf16[4,198,256]{2,1,0:T(8,128)(2,1)S(1)}, bf16[4,198,256]{2,1,0:T(8,128)(2,1)S(1)}) custom-call(s32[16]{0:T(128)S(1)} %multiply_add_fusion.1.order, bf16[198,256]{1,0:T(8,128)(2,1)S(1)} %copy-done.1, bf16[512,8192]{1,0:T(8,128)(2,1)} %bitcast.53), custom_call_target="tpu_custom_call" | custom-call | flops 1000000000 | bytes 4194304 | tf_op jit(solution)/shard_map/pallas_call | solution.py:129
  11.4 3.1 %collective-permute-start.2 = (bf16[4,198,256]{2,1,0:T(8,128)(2,1)S(1)}, bf16[4,198,256]{2,1,0:T(8,128)(2,1)S(1)}, u32[]{:S(2)}, u32[]{:S(2)}) collective-permute-start(bf16[4,198,256]{2,1,0:T(8,128)(2,1)S(1)} %add_convert_fusion.18), channel_id=1, source_target_pairs={{0,16},{4,68},{8,24},{12,76},{16,0},{20,84},{24,8},{28,92},{32,48}... | collective-permute-start | bytes 1216520 | tf_op jit(solution)/shard_map/ppermute | solution.py:201
  15.2 2.3 %collective-permute-start.6 = (bf16[4,198,256]{2,1,0:T(8,128)(2,1)S(1)}, bf16[4,198,256]{2,1,0:T(8,128)(2,1)S(1)}, u32[]{:S(2)}, u32[]{:S(2)}) collective-permute-start(bf16[4,198,256]{2,1,0:T(8,128)(2,1)S(1)} %add_convert_fusion.16), channel_id=1, source_target_pairs={{0,24},{4,100},{8,0},{12,108},{16,8},{20,116},{24,16},{28,124},{32... | collective-permute-start | bytes 1216520 | tf_op jit(solution)/shard_map/ppermute | solution.py:201
  20.2 4.4 %collective-permute-done.4 = bf16[4,198,256]{2,1,0:T(8,128)(2,1)S(1)} collective-permute-done((bf16[4,198,256]{2,1,0:T(8,128)(2,1)S(1)}, bf16[4,198,256]{2,1,0:T(8,128)(2,1)S(1)}, u32[]{:S(2)}, u32[]{:S(2)}) %collective-permute-start.4) | collective-permute-done | bytes 405536 | tf_op jit(solution)/shard_map/ppermute | solution.py:201
  25.3 2.7 %collective-permute-start.7 = (bf16[198,256]{1,0:T(8,128)(2,1)S(1)}, bf16[198,256]{1,0:T(8,128)(2,1)S(1)}, u32[]{:S(2)}, u32[]{:S(2)}) collective-permute-start(bf16[198,256]{1,0:T(8,128)(2,1)S(1)} %get-tuple-element.90), channel_id=1, source_target_pairs={{4,20},{0,64},{12,28},{8,72},{20,4},{16,80},{28,12},{24,88},{36,52... | collective-permute-start | bytes 304136 | tf_op jit(solution)/shard_map/ppermute | solution.py:206
  33.7 3.8 %collective-permute-start.12 = (bf16[198,256]{1,0:T(8,128)(2,1)S(1)}, bf16[198,256]{1,0:T(8,128)(2,1)S(1)}, u32[]{:S(2)}, u32[]{:S(2)}) collective-permute-start(bf16[198,256]{1,0:T(8,128)(2,1)S(1)} %fusion.14.refs_0_), channel_id=1, source_target_pairs={{0,3},{1,0},{2,1},{3,2},{4,7},{5,4},{6,5},{7,6},{8,11},{9,8},{10,9... | collective-permute-start | bytes 304136 | tf_op jit(solution)/shard_map/ppermute | solution.py:211
  38.3 2.2 %shard_map.71.refs_6_.refs_1_ = bf16[256,8192]{1,0:T(8,128)(2,1)S(1)} custom-call(bf16[4,198,256]{2,1,0:T(8,128)(2,1)S(1)} %add_convert_fusion.15.after, bf16[512,8192]{1,0:T(8,128)(2,1)} %bitcast.55), custom_call_target="tpu_custom_call" | custom-call | bytes 4194304 | tf_op jit(solution)/shard_map/pallas_call | solution.py:80
  44.9 4.3 %collective-permute-start.14 = (bf16[4,198,256]{2,1,0:T(8,128)(2,1)S(1)}, bf16[4,198,256]{2,1,0:T(8,128)(2,1)S(1)}, u32[]{:S(2)}, u32[]{:S(2)}) collective-permute-start(bf16[4,198,256]{2,1,0:T(8,128)(2,1)S(1)} %get-tuple-element.49), channel_id=1, source_target_pairs={{0,4},{4,0},{1,5},{5,1},{2,6},{6,2},{3,7},{7,3},{8,12},{12,8},{9,1... | collective-permute-start | bytes 1216520 | tf_op jit(solution)/shard_map/ppermute | solution.py:54
  55.1 4.8 %collective-permute-done.15 = bf16[4,198,256]{2,1,0:T(8,128)(2,1)S(1)} collective-permute-done((bf16[4,198,256]{2,1,0:T(8,128)(2,1)S(1)}, bf16[4,198,256]{2,1,0:T(8,128)(2,1)S(1)}, u32[]{:S(2)}, u32[]{:S(2)}) %collective-permute-start.15) | collective-permute-done | bytes 405536 | tf_op jit(solution)/shard_map/ppermute | solution.py:201
  59.9 4.3 %collective-permute-done.17 = bf16[4,198,256]{2,1,0:T(8,128)(2,1)S(1)} collective-permute-done((bf16[4,198,256]{2,1,0:T(8,128)(2,1)S(1)}, bf16[4,198,256]{2,1,0:T(8,128)(2,1)S(1)}, u32[]{:S(2)}, u32[]{:S(2)}) %collective-permute-start.17) | collective-permute-done | bytes 405536 | tf_op jit(solution)/shard_map/ppermute | solution.py:201
  74.9 2.2 %shard_map.74.refs_4_.refs_1_ = bf16[256,8192]{1,0:T(8,128)(2,1)S(1)} custom-call(bf16[4,198,256]{2,1,0:T(8,128)(2,1)S(1)} %add_convert_fusion.10.after, bf16[512,8192]{1,0:T(8,128)(2,1)} %bitcast.54), custom_call_target="tpu_custom_call" | custom-call | bytes 4194304 | tf_op jit(solution)/shard_map/pallas_call | solution.py:80
  80.8 3.3 %collective-permute-start.27 = (bf16[4,198,256]{2,1,0:T(8,128)(2,1)S(1)}, bf16[4,198,256]{2,1,0:T(8,128)(2,1)S(1)}, u32[]{:S(2)}, u32[]{:S(2)}) collective-permute-start(bf16[4,198,256]{2,1,0:T(8,128)(2,1)S(1)} %get-tuple-element.58), channel_id=1, source_target_pairs={{0,4},{4,0},{1,5},{5,1},{2,6},{6,2},{3,7},{7,3},{8,12},{12,8},{9,1... | collective-permute-start | bytes 1216520 | tf_op jit(solution)/shard_map/ppermute | solution.py:54
  89.3 5.5 %collective-permute-done.28 = bf16[4,198,256]{2,1,0:T(8,128)(2,1)S(1)} collective-permute-done((bf16[4,198,256]{2,1,0:T(8,128)(2,1)S(1)}, bf16[4,198,256]{2,1,0:T(8,128)(2,1)S(1)}, u32[]{:S(2)}, u32[]{:S(2)}) %collective-permute-start.28) | collective-permute-done | bytes 405536 | tf_op jit(solution)/shard_map/ppermute | solution.py:201
  94.7 4.3 %collective-permute-done.30 = bf16[4,198,256]{2,1,0:T(8,128)(2,1)S(1)} collective-permute-done((bf16[4,198,256]{2,1,0:T(8,128)(2,1)S(1)}, bf16[4,198,256]{2,1,0:T(8,128)(2,1)S(1)}, u32[]{:S(2)}, u32[]{:S(2)}) %collective-permute-start.30) | collective-permute-done | bytes 405536 | tf_op jit(solution)/shard_map/ppermute | solution.py:201
  109.2 2.2 %shard_map.77.refs_6_.refs_1_ = bf16[256,8192]{1,0:T(8,128)(2,1)S(1)} custom-call(bf16[4,198,256]{2,1,0:T(8,128)(2,1)S(1)} %add_convert_fusion.5.after, bf16[512,8192]{1,0:T(8,128)(2,1)} %bitcast.56), custom_call_target="tpu_custom_call" | custom-call | bytes 4194304 | tf_op jit(solution)/shard_map/pallas_call | solution.py:80
  113.6 2.5 %collective-permute-done.36.refs_1_ = bf16[198,256]{1,0:T(8,128)(2,1)S(1)} collective-permute-done((bf16[198,256]{1,0:T(8,128)(2,1)S(1)}, bf16[198,256]{1,0:T(8,128)(2,1)S(1)}, u32[]{:S(2)}, u32[]{:S(2)}) %collective-permute-start.36) | collective-permute-done | bytes 101408 | tf_op jit(solution)/shard_map/ppermute | solution.py:211
  130.3 2.4 %collective-permute-done.47 = bf16[198,198]{1,0:T(8,128)(2,1)S(1)} collective-permute-done((bf16[198,198]{1,0:T(8,128)(2,1)S(1)}, bf16[198,198]{1,0:T(8,128)(2,1)S(1)}, u32[]{:S(2)}, u32[]{:S(2)}) %collective-permute-start.47) | collective-permute-done | bytes 78440 | tf_op jit(solution)/shard_map/ppermute | solution.py:211
  134.9 4.3 %collective-permute-done.43 = bf16[4,198,256]{2,1,0:T(8,128)(2,1)S(1)} collective-permute-done((bf16[4,198,256]{2,1,0:T(8,128)(2,1)S(1)}, bf16[4,198,256]{2,1,0:T(8,128)(2,1)S(1)}, u32[]{:S(2)}, u32[]{:S(2)}) %collective-permute-start.43) | collective-permute-done | bytes 405536 | tf_op jit(solution)/shard_map/ppermute | solution.py:201
  143.1 3.0 %collective-permute-done.50 = bf16[2,198,256]{2,1,0:T(8,128)(2,1)S(1)} collective-permute-done((bf16[2,198,256]{2,1,0:T(8,128)(2,1)S(1)}, bf16[2,198,256]{2,1,0:T(8,128)(2,1)S(1)}, u32[]{:S(2)}, u32[]{:S(2)}) %collective-permute-start.50) | collective-permute-done | bytes 202784 | tf_op jit(solution)/shard_map/ppermute | solution.py:206
  146.1 2.2 %collective-permute-done.51 = bf16[2,198,256]{2,1,0:T(8,128)(2,1)S(1)} collective-permute-done((bf16[2,198,256]{2,1,0:T(8,128)(2,1)S(1)}, bf16[2,198,256]{2,1,0:T(8,128)(2,1)S(1)}, u32[]{:S(2)}, u32[]{:S(2)}) %collective-permute-start.51) | collective-permute-done | bytes 202784 | tf_op jit(solution)/shard_map/ppermute | solution.py:206
  150.0 3.4 %collective-permute-start.54 = (bf16[198,256]{1,0:T(8,128)(2,1)S(1)}, bf16[198,256]{1,0:T(8,128)(2,1)S(1)}, u32[]{:S(2)}, u32[]{:S(2)}) collective-permute-start(bf16[198,256]{1,0:T(8,128)(2,1)S(1)} %get-tuple-element.94), channel_id=1, source_target_pairs={{0,2},{1,3},{2,0},{3,1},{4,6},{5,7},{6,4},{7,5},{8,10},{9,11},{10,... | collective-permute-start | bytes 304136 | tf_op jit(solution)/shard_map/ppermute | solution.py:211
  153.4 2.7 %collective-permute-start.55 = (bf16[198,256]{1,0:T(8,128)(2,1)S(1)}, bf16[198,256]{1,0:T(8,128)(2,1)S(1)}, u32[]{:S(2)}, u32[]{:S(2)}) collective-permute-start(bf16[198,256]{1,0:T(8,128)(2,1)S(1)} %get-tuple-element.94), channel_id=1, source_target_pairs={{0,3},{1,0},{2,1},{3,2},{4,7},{5,4},{6,5},{7,6},{8,11},{9,8},{10,9... | collective-permute-start | bytes 304136 | tf_op jit(solution)/shard_map/ppermute | solution.py:211
  156.1 4.0 %collective-permute-start.59 = (f32[198,198]{1,0:T(8,128)S(1)}, f32[198,198]{1,0:T(8,128)S(1)}, u32[]{:S(2)}, u32[]{:S(2)}) collective-permute-start(f32[198,198]{1,0:T(8,128)S(1)} %convert_add_fusion.3), channel_id=1, source_target_pairs={{0,4},{4,0},{1,5},{5,1},{2,6},{6,2},{3,7},{7,3},{8,12},{12,8},{9,1... | collective-permute-start | bytes 470456 | tf_op jit(solution)/shard_map/ppermute | solution.py:54
  (170 shorter events, 81.2 us)
Async XLA Ops:
  4.7 15.1 %collective-permute-start = (bf16[4,198,256]{2,1,0:T(8,128)(2,1)S(1)}, bf16[4,198,256]{2,1,0:T(8,128)(2,1)S(1)}, u32[]{:S(2)}, u32[]{:S(2)}) collective-permute-start(bf16[4,198,256]{2,1,0:T(8,128)(2,1)S(1)} %get-tuple-element.38), channel_id=1, source_target_pairs={{0,4},{4,0},{1,5},{5,1},{2,6},{6,2},{3,7},{7,3},{8,12},{12,8},{9,1... | collective-permute-start | bytes 1216520 | tf_op jit(solution)/shard_map/ppermute | solution.py:54
  6.2 8.3 %collective-permute-start.3 = (bf16[4,198,256]{2,1,0:T(8,128)(2,1)S(1)}, bf16[4,198,256]{2,1,0:T(8,128)(2,1)S(1)}, u32[]{:S(2)}, u32[]{:S(2)}) collective-permute-start(bf16[4,198,256]{2,1,0:T(8,128)(2,1)S(1)} %get-tuple-element.42), channel_id=1, source_target_pairs={{0,4},{4,0},{1,5},{5,1},{2,6},{6,2},{3,7},{7,3},{8,12},{12,8},{9,1... | collective-permute-start | bytes 1216520 | tf_op jit(solution)/shard_map/ppermute | solution.py:54
  6.6 8.5 %collective-permute-start.5 = (bf16[4,198,256]{2,1,0:T(8,128)(2,1)S(1)}, bf16[4,198,256]{2,1,0:T(8,128)(2,1)S(1)}, u32[]{:S(2)}, u32[]{:S(2)}) collective-permute-start(bf16[4,198,256]{2,1,0:T(8,128)(2,1)S(1)} %get-tuple-element.44), channel_id=1, source_target_pairs={{0,4},{4,0},{1,5},{5,1},{2,6},{6,2},{3,7},{7,3},{8,12},{12,8},{9,1... | collective-permute-start | bytes 1216520 | tf_op jit(solution)/shard_map/ppermute | solution.py:54
  11.4 8.7 %collective-permute-start.2 = (bf16[4,198,256]{2,1,0:T(8,128)(2,1)S(1)}, bf16[4,198,256]{2,1,0:T(8,128)(2,1)S(1)}, u32[]{:S(2)}, u32[]{:S(2)}) collective-permute-start(bf16[4,198,256]{2,1,0:T(8,128)(2,1)S(1)} %add_convert_fusion.18), channel_id=1, source_target_pairs={{0,16},{4,68},{8,24},{12,76},{16,0},{20,84},{24,8},{28,92},{32,48}... | collective-permute-start | bytes 1216520 | tf_op jit(solution)/shard_map/ppermute | solution.py:201
  14.6 9.9 %collective-permute-start.4 = (bf16[4,198,256]{2,1,0:T(8,128)(2,1)S(1)}, bf16[4,198,256]{2,1,0:T(8,128)(2,1)S(1)}, u32[]{:S(2)}, u32[]{:S(2)}) collective-permute-start(bf16[4,198,256]{2,1,0:T(8,128)(2,1)S(1)} %add_convert_fusion.17), channel_id=1, source_target_pairs={{0,8},{4,36},{8,16},{12,44},{16,24},{20,52},{24,0},{28,60},{32,40}... | collective-permute-start | bytes 1216520 | tf_op jit(solution)/shard_map/ppermute | solution.py:201
  15.2 9.7 %collective-permute-start.6 = (bf16[4,198,256]{2,1,0:T(8,128)(2,1)S(1)}, bf16[4,198,256]{2,1,0:T(8,128)(2,1)S(1)}, u32[]{:S(2)}, u32[]{:S(2)}) collective-permute-start(bf16[4,198,256]{2,1,0:T(8,128)(2,1)S(1)} %add_convert_fusion.16), channel_id=1, source_target_pairs={{0,24},{4,100},{8,0},{12,108},{16,8},{20,116},{24,16},{28,124},{32... | collective-permute-start | bytes 1216520 | tf_op jit(solution)/shard_map/ppermute | solution.py:201
  33.7 6.8 %collective-permute-start.12 = (bf16[198,256]{1,0:T(8,128)(2,1)S(1)}, bf16[198,256]{1,0:T(8,128)(2,1)S(1)}, u32[]{:S(2)}, u32[]{:S(2)}) collective-permute-start(bf16[198,256]{1,0:T(8,128)(2,1)S(1)} %fusion.14.refs_0_), channel_id=1, source_target_pairs={{0,3},{1,0},{2,1},{3,2},{4,7},{5,4},{6,5},{7,6},{8,11},{9,8},{10,9... | collective-permute-start | bytes 304136 | tf_op jit(solution)/shard_map/ppermute | solution.py:211
  51.2 8.7 %collective-permute-start.15 = (bf16[4,198,256]{2,1,0:T(8,128)(2,1)S(1)}, bf16[4,198,256]{2,1,0:T(8,128)(2,1)S(1)}, u32[]{:S(2)}, u32[]{:S(2)}) collective-permute-start(bf16[4,198,256]{2,1,0:T(8,128)(2,1)S(1)} %add_convert_fusion.13.refs_1_), channel_id=1, source_target_pairs={{0,16},{4,68},{8,24},{12,76},{16,0},{20,84},{24,8},{28,92},{32,48}... | collective-permute-start | bytes 1216520 | tf_op jit(solution)/shard_map/ppermute | solution.py:201
  52.0 12.2 %collective-permute-start.17 = (bf16[4,198,256]{2,1,0:T(8,128)(2,1)S(1)}, bf16[4,198,256]{2,1,0:T(8,128)(2,1)S(1)}, u32[]{:S(2)}, u32[]{:S(2)}) collective-permute-start(bf16[4,198,256]{2,1,0:T(8,128)(2,1)S(1)} %add_convert_fusion.12.refs_0_), channel_id=1, source_target_pairs={{0,8},{4,36},{8,16},{12,44},{16,24},{20,52},{24,0},{28,60},{32,40}... | collective-permute-start | bytes 1216520 | tf_op jit(solution)/shard_map/ppermute | solution.py:201
  53.2 11.0 %collective-permute-start.19 = (bf16[4,198,256]{2,1,0:T(8,128)(2,1)S(1)}, bf16[4,198,256]{2,1,0:T(8,128)(2,1)S(1)}, u32[]{:S(2)}, u32[]{:S(2)}) collective-permute-start(bf16[4,198,256]{2,1,0:T(8,128)(2,1)S(1)} %add_convert_fusion.11.refs_2_), channel_id=1, source_target_pairs={{0,24},{4,100},{8,0},{12,108},{16,8},{20,116},{24,16},{28,124},{32... | collective-permute-start | bytes 1216520 | tf_op jit(solution)/shard_map/ppermute | solution.py:201
  86.0 8.7 %collective-permute-start.28 = (bf16[4,198,256]{2,1,0:T(8,128)(2,1)S(1)}, bf16[4,198,256]{2,1,0:T(8,128)(2,1)S(1)}, u32[]{:S(2)}, u32[]{:S(2)}) collective-permute-start(bf16[4,198,256]{2,1,0:T(8,128)(2,1)S(1)} %add_convert_fusion.8), channel_id=1, source_target_pairs={{0,16},{4,68},{8,24},{12,76},{16,0},{20,84},{24,8},{28,92},{32,48}... | collective-permute-start | bytes 1216520 | tf_op jit(solution)/shard_map/ppermute | solution.py:201
  86.3 12.7 %collective-permute-start.30 = (bf16[4,198,256]{2,1,0:T(8,128)(2,1)S(1)}, bf16[4,198,256]{2,1,0:T(8,128)(2,1)S(1)}, u32[]{:S(2)}, u32[]{:S(2)}) collective-permute-start(bf16[4,198,256]{2,1,0:T(8,128)(2,1)S(1)} %add_convert_fusion.7), channel_id=1, source_target_pairs={{0,8},{4,36},{8,16},{12,44},{16,24},{20,52},{24,0},{28,60},{32,40}... | collective-permute-start | bytes 1216520 | tf_op jit(solution)/shard_map/ppermute | solution.py:201
  87.5 11.6 %collective-permute-start.32 = (bf16[4,198,256]{2,1,0:T(8,128)(2,1)S(1)}, bf16[4,198,256]{2,1,0:T(8,128)(2,1)S(1)}, u32[]{:S(2)}, u32[]{:S(2)}) collective-permute-start(bf16[4,198,256]{2,1,0:T(8,128)(2,1)S(1)} %add_convert_fusion.6), channel_id=1, source_target_pairs={{0,24},{4,100},{8,0},{12,108},{16,8},{20,116},{24,16},{28,124},{32... | collective-permute-start | bytes 1216520 | tf_op jit(solution)/shard_map/ppermute | solution.py:201
  109.1 6.9 %collective-permute-start.36 = (bf16[198,256]{1,0:T(8,128)(2,1)S(1)}, bf16[198,256]{1,0:T(8,128)(2,1)S(1)}, u32[]{:S(2)}, u32[]{:S(2)}) collective-permute-start(bf16[198,256]{1,0:T(8,128)(2,1)S(1)} %fusion.8.refs_0_), channel_id=1, source_target_pairs={{0,1},{1,2},{2,3},{3,0},{4,5},{5,6},{6,7},{7,4},{8,9},{9,10},{10,1... | collective-permute-start | bytes 304136 | tf_op jit(solution)/shard_map/ppermute | solution.py:211
  124.9 7.8 %collective-permute-start.47 = (bf16[198,198]{1,0:T(8,128)(2,1)S(1)}, bf16[198,198]{1,0:T(8,128)(2,1)S(1)}, u32[]{:S(2)}, u32[]{:S(2)}) collective-permute-start(bf16[198,198]{1,0:T(8,128)(2,1)S(1)} %add_convert_fusion.23), channel_id=1, source_target_pairs={{0,1},{1,2},{2,3},{3,0},{4,5},{5,6},{6,7},{7,4},{8,9},{9,10},{10,1... | collective-permute-start | bytes 235232 | tf_op jit(solution)/shard_map/ppermute | solution.py:211
  125.0 7.7 %collective-permute-start.39 = (bf16[4,198,256]{2,1,0:T(8,128)(2,1)S(1)}, bf16[4,198,256]{2,1,0:T(8,128)(2,1)S(1)}, u32[]{:S(2)}, u32[]{:S(2)}) collective-permute-start(bf16[4,198,256]{2,1,0:T(8,128)(2,1)S(1)} %get-tuple-element.65), channel_id=1, source_target_pairs={{0,4},{4,0},{1,5},{5,1},{2,6},{6,2},{3,7},{7,3},{8,12},{12,8},{9,1... | collective-permute-start | bytes 1216520 | tf_op jit(solution)/shard_map/ppermute | solution.py:54
  126.2 8.6 %collective-permute-start.41 = (bf16[4,198,256]{2,1,0:T(8,128)(2,1)S(1)}, bf16[4,198,256]{2,1,0:T(8,128)(2,1)S(1)}, u32[]{:S(2)}, u32[]{:S(2)}) collective-permute-start(bf16[4,198,256]{2,1,0:T(8,128)(2,1)S(1)} %add_convert_fusion.3.refs_1_), channel_id=1, source_target_pairs={{0,16},{4,68},{8,24},{12,76},{16,0},{20,84},{24,8},{28,92},{32,48}... | collective-permute-start | bytes 1216520 | tf_op jit(solution)/shard_map/ppermute | solution.py:201
  127.6 11.6 %collective-permute-start.43 = (bf16[4,198,256]{2,1,0:T(8,128)(2,1)S(1)}, bf16[4,198,256]{2,1,0:T(8,128)(2,1)S(1)}, u32[]{:S(2)}, u32[]{:S(2)}) collective-permute-start(bf16[4,198,256]{2,1,0:T(8,128)(2,1)S(1)} %add_convert_fusion.2.refs_0_), channel_id=1, source_target_pairs={{0,8},{4,36},{8,16},{12,44},{16,24},{20,52},{24,0},{28,60},{32,40}... | collective-permute-start | bytes 1216520 | tf_op jit(solution)/shard_map/ppermute | solution.py:201
  129.3 9.9 %collective-permute-start.45 = (bf16[4,198,256]{2,1,0:T(8,128)(2,1)S(1)}, bf16[4,198,256]{2,1,0:T(8,128)(2,1)S(1)}, u32[]{:S(2)}, u32[]{:S(2)}) collective-permute-start(bf16[4,198,256]{2,1,0:T(8,128)(2,1)S(1)} %add_convert_fusion.1.refs_2_), channel_id=1, source_target_pairs={{0,24},{4,100},{8,0},{12,108},{16,8},{20,116},{24,16},{28,124},{32... | collective-permute-start | bytes 1216520 | tf_op jit(solution)/shard_map/ppermute | solution.py:201
  140.4 7.9 %collective-permute-start.51 = (bf16[2,198,256]{2,1,0:T(8,128)(2,1)S(1)}, bf16[2,198,256]{2,1,0:T(8,128)(2,1)S(1)}, u32[]{:S(2)}, u32[]{:S(2)}) collective-permute-start(bf16[2,198,256]{2,1,0:T(8,128)(2,1)S(1)} %get-tuple-element.96), channel_id=1, source_target_pairs={{4,12},{0,32},{12,20},{8,40},{20,28},{16,48},{28,4},{24,56},{36,44... | collective-permute-start | bytes 608264 | tf_op jit(solution)/shard_map/ppermute | solution.py:206
  148.9 7.1 %collective-permute-start.57 = (bf16[198,256]{1,0:T(8,128)(2,1)S(1)}, bf16[198,256]{1,0:T(8,128)(2,1)S(1)}, u32[]{:S(2)}, u32[]{:S(2)}) collective-permute-start(bf16[198,256]{1,0:T(8,128)(2,1)S(1)} %get-tuple-element.93), channel_id=1, source_target_pairs={{0,16},{4,68},{8,24},{12,76},{16,0},{20,84},{24,8},{28,92},{32,48}... | collective-permute-start | bytes 304136 | tf_op jit(solution)/shard_map/ppermute | solution.py:303
  148.9 7.1 %collective-permute-start.56 = (bf16[198,256]{1,0:T(8,128)(2,1)S(1)}, bf16[198,256]{1,0:T(8,128)(2,1)S(1)}, u32[]{:S(2)}, u32[]{:S(2)}) collective-permute-start(bf16[198,256]{1,0:T(8,128)(2,1)S(1)} %get-tuple-element.93), channel_id=1, source_target_pairs={{0,8},{4,36},{8,16},{12,44},{16,24},{20,52},{24,0},{28,60},{32,40}... | collective-permute-start | bytes 304136 | tf_op jit(solution)/shard_map/ppermute | solution.py:303
  150.0 10.2 %collective-permute-start.54 = (bf16[198,256]{1,0:T(8,128)(2,1)S(1)}, bf16[198,256]{1,0:T(8,128)(2,1)S(1)}, u32[]{:S(2)}, u32[]{:S(2)}) collective-permute-start(bf16[198,256]{1,0:T(8,128)(2,1)S(1)} %get-tuple-element.94), channel_id=1, source_target_pairs={{0,2},{1,3},{2,0},{3,1},{4,6},{5,7},{6,4},{7,5},{8,10},{9,11},{10,... | collective-permute-start | bytes 304136 | tf_op jit(solution)/shard_map/ppermute | solution.py:211
  153.4 6.8 %collective-permute-start.53 = (bf16[198,256]{1,0:T(8,128)(2,1)S(1)}, bf16[198,256]{1,0:T(8,128)(2,1)S(1)}, u32[]{:S(2)}, u32[]{:S(2)}) collective-permute-start(bf16[198,256]{1,0:T(8,128)(2,1)S(1)} %get-tuple-element.94), channel_id=1, source_target_pairs={{0,1},{1,2},{2,3},{3,0},{4,5},{5,6},{6,7},{7,4},{8,9},{9,10},{10,1... | collective-permute-start | bytes 304136 | tf_op jit(solution)/shard_map/ppermute | solution.py:211
  (40 other events, 185.8 us)

commit v4 on v3

--- a/solution.py
+++ b/solution.py
@@ -7,6 +7,7 @@
 from jax.experimental.pallas import tpu as pltpu
 from jax.sharding import Mesh
 from jax.sharding import PartitionSpec as P
+
 
 BOND_DIM = 8192
 PHYSICAL = 4
@@ -63,7 +64,8 @@
     return (((y + dy) % RING * RING + (x + dx) % RING) * 2 + core).astype(jnp.int32)
 
 
-def load_kernel(site, after, weights, loaded, sems):
+def load_kernel(site, weights, *rest):
+    loaded, sems = rest[-2:]
     rows = BLOCK // LOADS
     copies = []
     for i in range(LOADS):
@@ -76,16 +78,16 @@
         copy.wait()
 
 
-def load(site, weights, after):
+def load(site, weights, *after):
     return pl.pallas_call(
         functools.partial(load_kernel, site),
         out_shape=jax.ShapeDtypeStruct((BLOCK, BOND_DIM), BF16),
-        in_specs=[pl.BlockSpec(memory_space=pl.ANY)] * 2,
+        in_specs=[pl.BlockSpec(memory_space=pl.ANY)] * (1 + len(after)),
         out_specs=VMEM,
         scratch_shapes=[pltpu.SemaphoreType.DMA((LOADS,))],
         compiler_params=pltpu.CompilerParams(vmem_limit_bytes=LOAD_GRANT),
         cost_estimate=pl.CostEstimate(flops=0, bytes_accessed=4 * 2**20, transcendentals=0),
-    )(after, weights)
+    )(weights, *after)
 
 
 def multiply_kernel(prepare, given, order, *refs):
@@ -104,59 +106,22 @@
                 outs[group * RING + d][e] = product.astype(BF16)
 
 
-def direct_kernel(site, order, left, weights, *rest):
-    outs, (tiles, sems) = rest[:RING], rest[RING:]
-    width = RING * BLOCK
-    copies = []
-    for i in range(RING**2):
-        first = pl.multiple_of(order[i] * BLOCK, BLOCK)
-        source = weights.at[pl.ds(site * BLOCK, BLOCK), pl.ds(first, BLOCK)]
-        target = tiles.at[:, pl.ds(i * BLOCK, BLOCK)]
-        copies.append(pltpu.make_async_copy(source, target, sems.at[i]))
-    for d in SENT:
-        for e in range(RING):
-            copies[d * RING + e].start()
-    for d in SENT:
-        for e in range(RING):
-            copies[d * RING + e].wait()
-        columns = tiles[:, d * width : (d + 1) * width]
-        product = jnp.dot(left[...], columns, preferred_element_type=F32).astype(BF16)
-        for e in range(RING):
-            outs[d][e] = product[:, e * BLOCK : (e + 1) * BLOCK]
-
-
-def multiply_direct(site, left, order, weights):
-    return pl.pallas_call(
-        functools.partial(direct_kernel, site),
-        out_shape=[jax.ShapeDtypeStruct((RING, ROWS, BLOCK), BF16)] * RING,
-        in_specs=[pl.BlockSpec(memory_space=pltpu.SMEM), VMEM, pl.BlockSpec(memory_space=pl.ANY)],
-        out_specs=[VMEM] * RING,
-        scratch_shapes=[
-            pltpu.VMEM((BLOCK, RING**2 * BLOCK), BF16),
-            pltpu.SemaphoreType.DMA((RING**2,)),
-        ],
-        compiler_params=pltpu.CompilerParams(vmem_limit_bytes=LOAD_GRANT),
-        cost_estimate=pl.CostEstimate(flops=10**9, bytes_accessed=2**22, transcendentals=0),
-    )(order, left, weights)
-
-
-def gram_kernel(*refs):
-    kept, gram = refs[-2:]
+def gram_kernel(kept, gram):
     whole = lax.dot_general(
         kept[...], kept[...], (((1,), (1,)), ((), ())), preferred_element_type=F32
     )
     gram[...] = (whole * (1.0 / BOND_DIM)).astype(BF16)
 
 
-def gram_of(kept, after):
+def gram_of(kept):
     return pl.pallas_call(
         gram_kernel,
         out_shape=jax.ShapeDtypeStruct((ROWS, ROWS), BF16),
-        in_specs=[pl.BlockSpec(memory_space=pl.ANY)] * len(after) + [VMEM],
+        in_specs=[VMEM],
         out_specs=VMEM,
         compiler_params=pltpu.CompilerParams(vmem_limit_bytes=GRANT),
         cost_estimate=pl.CostEstimate(flops=10**8, bytes_accessed=10**5, transcendentals=0),
-    )(*after, kept)
+    )(kept)
 
 
 def total(a, b, c, d):
@@ -211,7 +176,7 @@
     return [array] + [lax.ppermute(array, "z", ring_shift(d)) for d in (1, 2, 3)]
 
 
-def mixing_kernel(z, operator_tensors, mixing):
+def mixing_kernel(z, near, operator_tensors, mixing):
     def iota(shape, dim):
         return lax.broadcasted_iota(jnp.int32, shape, dim)
 
@@ -231,29 +196,59 @@
             mixing[site, d] = jnp.where(same, full, 0.0).astype(BF16)
 
 
-def mixing_weights(operator_tensors):
+def mixing_weights(operator_tensors, near):
     return pl.pallas_call(
         mixing_kernel,
         out_shape=jax.ShapeDtypeStruct((SITE_COUNT, RING, ROWS, ROWS), BF16),
-        in_specs=[pl.BlockSpec(memory_space=pltpu.SMEM), VMEM],
+        in_specs=[
+            pl.BlockSpec(memory_space=pltpu.SMEM),
+            pl.BlockSpec(memory_space=pl.ANY),
+            VMEM,
+        ],
         out_specs=VMEM,
         compiler_params=pltpu.CompilerParams(vmem_limit_bytes=8 * 2**20),
         cost_estimate=pl.CostEstimate(flops=10**9, bytes_accessed=10**6, transcendentals=0),
-    )(lax.axis_index("z").astype(jnp.int32)[None], operator_tensors)
-
-
-def chosen_columns(kept_columns):
-    first = lax.axis_index(BOND) * BLOCK * PHYSICAL
-    place = kept_columns - first
-    here = (place >= 0) & (place < BLOCK * PHYSICAL) & (place % PHYSICAL == lax.axis_index("z"))
-    column = place // PHYSICAL
-    digits = jnp.arange(16)[None, :, None]
-    high = ((column // 16)[:, None] == digits) & here[:, None]
-    low = (column % 16)[:, None] == digits
-    counts = jnp.einsum(
-        "khn,kln->khl", high.astype(BF16), low.astype(BF16), preferred_element_type=F32
-    )
-    return (counts > 0.5).astype(F32).reshape(SITE_COUNT, 1, BLOCK)
+    )(lax.axis_index("z").astype(jnp.int32)[None], near, operator_tensors)
+
+
+def chosen_kernel(place, near, kept_columns, chosen):
+    def iota(shape, dim):
+        return lax.broadcasted_iota(jnp.int32, shape, dim)
+
+    digits, wide = (16, kept_columns.shape[-1]), (16, BLOCK)
+    high_of = lax.div(iota(wide, 1), 16) == iota(wide, 0)
+    low_of = (lax.rem(iota(wide, 1), 16) == iota(wide, 0)).astype(F32)
+    for site in range(SITE_COUNT):
+        number = kept_columns[site : site + 1, :] - place[0]
+        here = (number >= 0) & (number < BLOCK * PHYSICAL) & (lax.rem(number, PHYSICAL) == place[1])
+        column = jnp.where(here, lax.div(number, PHYSICAL), -1)
+        high = (lax.div(column, 16) == iota(digits, 0)) & (column >= 0)
+        low = lax.rem(column, 16) == iota(digits, 0)
+        counts = lax.dot_general(
+            high.astype(F32).astype(BF16),
+            low.astype(F32).astype(BF16),
+            (((1,), (1,)), ((), ())),
+            preferred_element_type=F32,
+        )
+        spread = jnp.dot(counts, low_of, preferred_element_type=F32)
+        total = jnp.sum(jnp.where(high_of, spread, 0.0), axis=0, keepdims=True)
+        chosen[site] = (total > 0.5).astype(F32)
+
+
+def chosen_columns(kept_columns, near):
+    place = jnp.stack([lax.axis_index(BOND) * BLOCK * PHYSICAL, lax.axis_index("z")])
+    return pl.pallas_call(
+        chosen_kernel,
+        out_shape=jax.ShapeDtypeStruct((SITE_COUNT, 1, BLOCK), F32),
+        in_specs=[
+            pl.BlockSpec(memory_space=pltpu.SMEM),
+            pl.BlockSpec(memory_space=pl.ANY),
+            VMEM,
+        ],
+        out_specs=VMEM,
+        compiler_params=pltpu.CompilerParams(vmem_limit_bytes=GRANT),
+        cost_estimate=pl.CostEstimate(flops=10**8, bytes_accessed=10**5, transcendentals=0),
+    )(place.astype(jnp.int32), near, kept_columns)
 
 
 def chip_gram(grams):
@@ -264,10 +259,23 @@
     return jnp.pad(whole, ((0, 0), (0, BLOCK - ROWS)))
 
 
-def both_grams(own):
-    other = swap_cores(own)
-    first = lax.axis_index("core") == 0
-    return jnp.stack([jnp.where(first, own, other), jnp.where(first, other, own)])
+def finish_kernel(core, a, b, c, d, own, other, state, grams):
+    state[...] = total(a, b, c, d).astype(BF16)
+    grams[core[0]] = own[...]
+    grams[1 - core[0]] = other[...]
+
+
+def finish(parts, own):
+    return pl.pallas_call(
+        finish_kernel,
+        out_shape=[
+            jax.ShapeDtypeStruct((ROWS, BLOCK), BF16),
+            jax.ShapeDtypeStruct((SITE_COUNT, ROWS, ROWS), F32),
+        ],
+        in_specs=[pl.BlockSpec(memory_space=pltpu.SMEM)] + [VMEM] * 6,
+        out_specs=[VMEM] * 2,
+        compiler_params=pltpu.CompilerParams(vmem_limit_bytes=GRANT),
+    )(lax.axis_index("core").astype(jnp.int32)[None], *parts, own, swap_cores(own))
 
 
 def on_device(carried, site_tensors, operator_tensors, rotation, kept_columns):
@@ -275,33 +283,35 @@
     their_order, our_order = block_order(1 - core), block_order(core)
     tensors = site_tensors.reshape(SITE_COUNT * BLOCK, BOND_DIM)
     turns = rotation.reshape(SITE_COUNT * BLOCK, BOND_DIM)
-    mixing = mixing_weights(operator_tensors)
-    chosen = chosen_columns(kept_columns)
     grams, near, parts = [], None, None
     for site in range(SITE_COUNT):
         if near is None:
-            theirs = multiply_direct(site, carried, their_order, tensors)
-            ours = multiply_direct(site, carried, our_order, tensors)
+            both_orders = jnp.concatenate([their_order, our_order])
+            pieces = multiply(None, [carried], both_orders, load(site, tensors))
+            theirs, ours = pieces[:RING], pieces[RING:]
         else:
             weights = load(site, tensors, near)
             state, *theirs = multiply(total, parts, their_order, weights)
             ours = multiply(None, [state], our_order, weights)
         near = along_first(to_cores(theirs, ours))
+        if site == 0:
+            mixing = mixing_weights(operator_tensors, near)
+            chosen = chosen_columns(kept_columns, near)
         parts = along_z(along_second([near[e] for e in range(RING)]))
         weights = load(site, turns, near)
         mixed = [*parts, mixing[site], chosen[site]]
         kept, *theirs = multiply(mix, mixed, their_order, weights)
+        grams.append(gram_of(kept))
         ours = multiply(None, [kept], our_order, weights)
         mine = to_cores(theirs, ours)
-        grams.append(gram_of(kept, [mine[d] for d in (1, 2, 3)]))
         near = along_first(mine)
         pieces = [near[e] for e in range(RING)]
         if site == SITE_COUNT - 1:
             gram = chip_gram(grams)
             both = along_second([jnp.stack([piece, gram]) for piece in pieces])
-            state = summed(along_z(both[0])).astype(BF16)
+            parts = along_z(both[0])
             got = [lax.ppermute(both[1], BOND, shifts(d, 0)) for d in (1, 2, 3)]
-            return state, both_grams(summed([both[1], *got])[:, :ROWS])
+            return tuple(finish(parts, summed([both[1], *got])[:, :ROWS]))
         parts = along_z(along_second(pieces))
 
 

time: 164 us -> 167 us (1.018); the launches traced: 162 us -> 167 us
  waiting for transfers between devices: 65.6 us -> 70.1 us
    ppermute x15, waiting for transfers between devices: 15.2 us -> 21.2 us  [along_z(): lax.ppermute(array, 'z', ring_shift(d))]
    ppermute x3, waiting for transfers between devices: 0.01 us -> 5.31 us  [on_device(): got = [lax.ppermute(both[1], BOND, shifts(d, 0)) for d in (1, 2, 3)]]
    ppermute x12, waiting for transfers between devices: 18.4 us -> 13.9 us  [along_second(): got = [lax.ppermute(pieces[e], BOND, shifts(e, 1)) for e in (2, 1, 3)]]
    pallas_call x2, Pallas kernels: 5.83 us -> 2.05 us  [the longest x1 1.33 us: chosen_columns(): pl.pallas_call(chosen_kernel, out_shape=jax.ShapeDtypeStruct((SITE_COUNT,...]
    pallas_call x3 -> x4, Pallas kernels: 6.65 us -> 8.9 us  [load(): pl.pallas_call(functools.partial(load_kernel, site), out_shape=jax.ShapeD...]
    ppermute x18, starting transfers between devices: 18.9 us -> 21.1 us  [swap_cores(): return lax.ppermute(array, 'core', [(0, 1), (1, 0)])]
    ppermute x15, starting transfers between devices: 16.3 us -> 14.2 us  [along_z(): lax.ppermute(array, 'z', ring_shift(d))]
    ppermute x12, waiting for transfers between devices: 30.5 us -> 28.9 us  [along_first(): got = [lax.ppermute(mine[d], BOND, shifts(d, 0)) for d in (2, 1, 3)]]
  transfers between devices with their start and end apart: 60 -> 60, of which waited for: 32 -> 35; matrix products, arithmetic and copies ran while one was open for 3% -> 3% of each run, Pallas kernels for 9% -> 8%
where the time goes in v4:
time: 167 us
  waiting for transfers between devices  70.1 us (42%)
  starting transfers between devices  66 us (40%)
  Pallas kernels  22.6 us (14%)
  other arithmetic  4.7 us (3%)
  local copies, waits for them, and re-layouts  2.54 us (2%)
    ppermute x12, waiting for transfers between devices, along_first(): got = [lax.ppermute(mine[d], BOND, shifts(d, 0)) for d in (2, 1, 3)]  28.9 us
    ppermute x15, waiting for transfers between devices, along_z(): lax.ppermute(array, 'z', ring_shift(d))  21.2 us
    ppermute x18, starting transfers between devices, swap_cores(): return lax.ppermute(array, 'core', [(0, 1), (1, 0)])  21.1 us
    ppermute x12, starting transfers between devices, along_second(): got = [lax.ppermute(pieces[e], BOND, shifts(e, 1)) for e in (2, 1, 3)]  15.3 us
    ppermute x15, starting transfers between devices, along_z(): lax.ppermute(array, 'z', ring_shift(d))  14.2 us
    ppermute x12, waiting for transfers between devices, along_second(): got = [lax.ppermute(pieces[e], BOND, shifts(e, 1)) for e in (2, 1, 3)]  13.9 us
    ppermute x12, starting transfers between devices, along_first(): got = [lax.ppermute(mine[d], BOND, shifts(d, 0)) for d in (2, 1, 3)]  13.9 us
    pallas_call x7, Pallas kernels, multiply(): pl.pallas_call(functools.partial(multiply_kernel, prepare, len(operands))...  9.45 us
  transfers between devices with their start and end apart: 60, of which 35 were waited for; matrix products, arithmetic and copies ran while one was open for 3% of the time, Pallas kernels for 8%

profile of v4, /device:TPU:1, one launch (start us, length us, event | category | flops | bytes accessed | tf_op | source)
XLA Modules:
  0.0 167.1 jit_solution(4343142369692400822)
XLA Ops:
  1.0 2.3 %shard_map.68.refs_1_ = bf16[256,8192]{1,0:T(8,128)(2,1)S(1)} custom-call(bf16[512,8192]{1,0:T(8,128)(2,1)} %bitcast.52), custom_call_target="tpu_custom_call" | custom-call | bytes 4194304 | tf_op jit(solution)/shard_map/pallas_call | solution.py:82
  8.0 3.1 %collective-permute-start.2 = (bf16[4,198,256]{2,1,0:T(8,128)(2,1)S(1)}, bf16[4,198,256]{2,1,0:T(8,128)(2,1)S(1)}, u32[]{:S(2)}, u32[]{:S(2)}) collective-permute-start(bf16[4,198,256]{2,1,0:T(8,128)(2,1)S(1)} %add_convert_fusion.18), channel_id=1, source_target_pairs={{0,16},{4,68},{8,24},{12,76},{16,0},{20,84},{24,8},{28,92},{32,48}... | collective-permute-start | bytes 1216520 | tf_op jit(solution)/shard_map/ppermute | solution.py:166
  13.2 2.3 %collective-permute-start.6 = (bf16[4,198,256]{2,1,0:T(8,128)(2,1)}, bf16[4,198,256]{2,1,0:T(8,128)(2,1)S(1)}, u32[]{:S(2)}, u32[]{:S(2)}) collective-permute-start(bf16[4,198,256]{2,1,0:T(8,128)(2,1)} %add_convert_fusion.16), channel_id=1, source_target_pairs={{0,24},{4,100},{8,0},{12,108},{16,8},{20,116},{24,16},{28,124},{32... | collective-permute-start | bytes 1216520 | tf_op jit(solution)/shard_map/ppermute | solution.py:166
  16.7 4.4 %collective-permute-done.4 = bf16[4,198,256]{2,1,0:T(8,128)(2,1)S(1)} collective-permute-done((bf16[4,198,256]{2,1,0:T(8,128)(2,1)}, bf16[4,198,256]{2,1,0:T(8,128)(2,1)S(1)}, u32[]{:S(2)}, u32[]{:S(2)}) %collective-permute-start.4) | collective-permute-done | bytes 405536 | tf_op jit(solution)/shard_map/ppermute | solution.py:166
  21.8 2.8 %collective-permute-start.7 = (bf16[198,256]{1,0:T(8,128)(2,1)S(1)}, bf16[198,256]{1,0:T(8,128)(2,1)S(1)}, u32[]{:S(2)}, u32[]{:S(2)}) collective-permute-start(bf16[198,256]{1,0:T(8,128)(2,1)S(1)} %get-tuple-element.86), channel_id=1, source_target_pairs={{4,20},{0,64},{12,28},{8,72},{20,4},{16,80},{28,12},{24,88},{36,52... | collective-permute-start | bytes 304136 | tf_op jit(solution)/shard_map/ppermute | solution.py:171
  30.3 3.8 %collective-permute-start.12 = (bf16[198,256]{1,0:T(8,128)(2,1)S(1)}, bf16[198,256]{1,0:T(8,128)(2,1)S(1)}, u32[]{:S(2)}, u32[]{:S(2)}) collective-permute-start(bf16[198,256]{1,0:T(8,128)(2,1)S(1)} %fusion.8.refs_0_), channel_id=1, source_target_pairs={{0,3},{1,0},{2,1},{3,2},{4,7},{5,4},{6,5},{7,6},{8,11},{9,8},{10,9... | collective-permute-start | bytes 304136 | tf_op jit(solution)/shard_map/ppermute | solution.py:176
  41.5 4.3 %collective-permute-start.14 = (bf16[4,198,256]{2,1,0:T(8,128)(2,1)S(1)}, bf16[4,198,256]{2,1,0:T(8,128)(2,1)S(1)}, u32[]{:S(2)}, u32[]{:S(2)}) collective-permute-start(bf16[4,198,256]{2,1,0:T(8,128)(2,1)S(1)} %get-tuple-element.49), channel_id=1, source_target_pairs={{0,4},{4,0},{1,5},{5,1},{2,6},{6,2},{3,7},{7,3},{8,12},{12,8},{9,1... | collective-permute-start | bytes 1216520 | tf_op jit(solution)/shard_map/ppermute | solution.py:55
  49.6 2.7 %collective-permute-start.19 = (bf16[4,198,256]{2,1,0:T(8,128)(2,1)S(1)}, bf16[4,198,256]{2,1,0:T(8,128)(2,1)S(1)}, u32[]{:S(2)}, u32[]{:S(2)}) collective-permute-start(bf16[4,198,256]{2,1,0:T(8,128)(2,1)S(1)} %add_convert_fusion.11), channel_id=1, source_target_pairs={{0,24},{4,100},{8,0},{12,108},{16,8},{20,116},{24,16},{28,124},{32... | collective-permute-start | bytes 1216520 | tf_op jit(solution)/shard_map/ppermute | solution.py:166
  52.2 4.1 %collective-permute-done.15 = bf16[4,198,256]{2,1,0:T(8,128)(2,1)S(1)} collective-permute-done((bf16[4,198,256]{2,1,0:T(8,128)(2,1)S(1)}, bf16[4,198,256]{2,1,0:T(8,128)(2,1)S(1)}, u32[]{:S(2)}, u32[]{:S(2)}) %collective-permute-start.15) | collective-permute-done | bytes 405536 | tf_op jit(solution)/shard_map/ppermute | solution.py:166
  56.4 4.3 %collective-permute-done.17 = bf16[4,198,256]{2,1,0:T(8,128)(2,1)S(1)} collective-permute-done((bf16[4,198,256]{2,1,0:T(8,128)(2,1)S(1)}, bf16[4,198,256]{2,1,0:T(8,128)(2,1)S(1)}, u32[]{:S(2)}, u32[]{:S(2)}) %collective-permute-start.17) | collective-permute-done | bytes 405536 | tf_op jit(solution)/shard_map/ppermute | solution.py:166
  61.0 2.5 %collective-permute-start.20 = (bf16[198,256]{1,0:T(8,128)(2,1)S(1)}, bf16[198,256]{1,0:T(8,128)(2,1)S(1)}, u32[]{:S(2)}, u32[]{:S(2)}) collective-permute-start(bf16[198,256]{1,0:T(8,128)(2,1)S(1)} %get-tuple-element.83), channel_id=1, source_target_pairs={{4,20},{0,64},{12,28},{8,72},{20,4},{16,80},{28,12},{24,88},{36,52... | collective-permute-start | bytes 304136 | tf_op jit(solution)/shard_map/ppermute | solution.py:171
  66.1 2.2 %collective-permute-done.22 = bf16[198,256]{1,0:T(8,128)(2,1)S(1)} collective-permute-done((bf16[198,256]{1,0:T(8,128)(2,1)S(1)}, bf16[198,256]{1,0:T(8,128)(2,1)S(1)}, u32[]{:S(2)}, u32[]{:S(2)}) %collective-permute-start.22) | collective-permute-done | bytes 101408 | tf_op jit(solution)/shard_map/ppermute | solution.py:171
  77.2 3.9 %collective-permute-start.27 = (bf16[4,198,256]{2,1,0:T(8,128)(2,1)S(1)}, bf16[4,198,256]{2,1,0:T(8,128)(2,1)S(1)}, u32[]{:S(2)}, u32[]{:S(2)}) collective-permute-start(bf16[4,198,256]{2,1,0:T(8,128)(2,1)S(1)} %get-tuple-element.58), channel_id=1, source_target_pairs={{0,4},{4,0},{1,5},{5,1},{2,6},{6,2},{3,7},{7,3},{8,12},{12,8},{9,1... | collective-permute-start | bytes 1216520 | tf_op jit(solution)/shard_map/ppermute | solution.py:55
  86.1 5.6 %collective-permute-done.28 = bf16[4,198,256]{2,1,0:T(8,128)(2,1)S(1)} collective-permute-done((bf16[4,198,256]{2,1,0:T(8,128)(2,1)S(1)}, bf16[4,198,256]{2,1,0:T(8,128)(2,1)S(1)}, u32[]{:S(2)}, u32[]{:S(2)}) %collective-permute-start.28) | collective-permute-done | bytes 405536 | tf_op jit(solution)/shard_map/ppermute | solution.py:166
  91.7 4.3 %collective-permute-done.30 = bf16[4,198,256]{2,1,0:T(8,128)(2,1)S(1)} collective-permute-done((bf16[4,198,256]{2,1,0:T(8,128)(2,1)S(1)}, bf16[4,198,256]{2,1,0:T(8,128)(2,1)S(1)}, u32[]{:S(2)}, u32[]{:S(2)}) %collective-permute-start.30) | collective-permute-done | bytes 405536 | tf_op jit(solution)/shard_map/ppermute | solution.py:166
  105.8 2.2 %shard_map.78.refs_6_.refs_1_ = bf16[256,8192]{1,0:T(8,128)(2,1)S(1)} custom-call(bf16[512,8192]{1,0:T(8,128)(2,1)} %bitcast.55, bf16[4,198,256]{2,1,0:T(8,128)(2,1)S(1)} %add_convert_fusion.5.rest_0_), custom_call_target="tpu_custom_call" | custom-call | bytes 4194304 | tf_op jit(solution)/shard_map/pallas_call | solution.py:82
  112.8 3.0 %collective-permute-start.40 = (bf16[4,198,256]{2,1,0:T(8,128)(2,1)S(1)}, bf16[4,198,256]{2,1,0:T(8,128)(2,1)S(1)}, u32[]{:S(2)}, u32[]{:S(2)}) collective-permute-start(bf16[4,198,256]{2,1,0:T(8,128)(2,1)S(1)} %get-tuple-element.67), channel_id=1, source_target_pairs={{0,4},{4,0},{1,5},{5,1},{2,6},{6,2},{3,7},{7,3},{8,12},{12,8},{9,1... | collective-permute-start | bytes 1216520 | tf_op jit(solution)/shard_map/ppermute | solution.py:55
  125.3 2.2 %collective-permute-done.47 = bf16[198,198]{1,0:T(8,128)(2,1)S(1)} collective-permute-done((bf16[198,198]{1,0:T(8,128)(2,1)S(1)}, bf16[198,198]{1,0:T(8,128)(2,1)S(1)}, u32[]{:S(2)}, u32[]{:S(2)}) %collective-permute-start.47) | collective-permute-done | bytes 78440 | tf_op jit(solution)/shard_map/ppermute | solution.py:176
  129.0 4.3 %collective-permute-done.43 = bf16[4,198,256]{2,1,0:T(8,128)(2,1)S(1)} collective-permute-done((bf16[4,198,256]{2,1,0:T(8,128)(2,1)S(1)}, bf16[4,198,256]{2,1,0:T(8,128)(2,1)S(1)}, u32[]{:S(2)}, u32[]{:S(2)}) %collective-permute-start.43) | collective-permute-done | bytes 405536 | tf_op jit(solution)/shard_map/ppermute | solution.py:166
  137.6 2.5 %collective-permute-done.50 = bf16[2,198,256]{2,1,0:T(8,128)(2,1)S(1)} collective-permute-done((bf16[2,198,256]{2,1,0:T(8,128)(2,1)S(1)}, bf16[2,198,256]{2,1,0:T(8,128)(2,1)S(1)}, u32[]{:S(2)}, u32[]{:S(2)}) %collective-permute-start.50) | collective-permute-done | bytes 202784 | tf_op jit(solution)/shard_map/ppermute | solution.py:171
  146.1 2.3 %collective-permute-done.57 = bf16[198,256]{1,0:T(8,128)(2,1)S(1)} collective-permute-done((bf16[198,256]{1,0:T(8,128)(2,1)S(1)}, bf16[198,256]{1,0:T(8,128)(2,1)S(1)}, u32[]{:S(2)}, u32[]{:S(2)}) %collective-permute-start.57) | collective-permute-done | bytes 101408 | tf_op jit(solution)/shard_map/ppermute | solution.py:313
  149.4 5.6 %collective-permute-start.59 = (f32[198,198]{1,0:T(8,128)S(1)}, f32[198,198]{1,0:T(8,128)S(1)}, u32[]{:S(2)}, u32[]{:S(2)}) collective-permute-start(f32[198,198]{1,0:T(8,128)S(1)} %convert_add_fusion.3.own), channel_id=1, source_target_pairs={{0,4},{4,0},{1,5},{5,1},{2,6},{6,2},{3,7},{7,3},{8,12},{12,8},{9,1... | collective-permute-start | bytes 470456 | tf_op jit(solution)/shard_map/ppermute | solution.py:55
  159.4 3.3 %collective-permute-done.54.c = bf16[198,256]{1,0:T(8,128)(2,1)S(1)} collective-permute-done((bf16[198,256]{1,0:T(8,128)(2,1)S(1)}, bf16[198,256]{1,0:T(8,128)(2,1)S(1)}, u32[]{:S(2)}, u32[]{:S(2)}) %collective-permute-start.54) | collective-permute-done | bytes 101408 | tf_op jit(solution)/shard_map/ppermute | solution.py:176
  162.7 2.7 %collective-permute-done.53.b = bf16[198,256]{1,0:T(8,128)(2,1)S(1)} collective-permute-done((bf16[198,256]{1,0:T(8,128)(2,1)S(1)}, bf16[198,256]{1,0:T(8,128)(2,1)S(1)}, u32[]{:S(2)}, u32[]{:S(2)}) %collective-permute-start.53) | collective-permute-done | bytes 101408 | tf_op jit(solution)/shard_map/ppermute | solution.py:176
  (161 shorter events, 85.3 us)
Async XLA Ops:
  6.6 10.1 %collective-permute-start = (bf16[4,198,256]{2,1,0:T(8,128)(2,1)S(1)}, bf16[4,198,256]{2,1,0:T(8,128)(2,1)S(1)}, u32[]{:S(2)}, u32[]{:S(2)}) collective-permute-start(bf16[4,198,256]{2,1,0:T(8,128)(2,1)S(1)} %get-tuple-element.38), channel_id=1, source_target_pairs={{0,4},{4,0},{1,5},{5,1},{2,6},{6,2},{3,7},{7,3},{8,12},{12,8},{9,1... | collective-permute-start | bytes 1216520 | tf_op jit(solution)/shard_map/ppermute | solution.py:55
  8.0 8.7 %collective-permute-start.2 = (bf16[4,198,256]{2,1,0:T(8,128)(2,1)S(1)}, bf16[4,198,256]{2,1,0:T(8,128)(2,1)S(1)}, u32[]{:S(2)}, u32[]{:S(2)}) collective-permute-start(bf16[4,198,256]{2,1,0:T(8,128)(2,1)S(1)} %add_convert_fusion.18), channel_id=1, source_target_pairs={{0,16},{4,68},{8,24},{12,76},{16,0},{20,84},{24,8},{28,92},{32,48}... | collective-permute-start | bytes 1216520 | tf_op jit(solution)/shard_map/ppermute | solution.py:166
  12.0 9.2 %collective-permute-start.4 = (bf16[4,198,256]{2,1,0:T(8,128)(2,1)}, bf16[4,198,256]{2,1,0:T(8,128)(2,1)S(1)}, u32[]{:S(2)}, u32[]{:S(2)}) collective-permute-start(bf16[4,198,256]{2,1,0:T(8,128)(2,1)} %add_convert_fusion.17), channel_id=1, source_target_pairs={{0,8},{4,36},{8,16},{12,44},{16,24},{20,52},{24,0},{28,60},{32,40}... | collective-permute-start | bytes 1216520 | tf_op jit(solution)/shard_map/ppermute | solution.py:166
  13.2 8.3 %collective-permute-start.6 = (bf16[4,198,256]{2,1,0:T(8,128)(2,1)}, bf16[4,198,256]{2,1,0:T(8,128)(2,1)S(1)}, u32[]{:S(2)}, u32[]{:S(2)}) collective-permute-start(bf16[4,198,256]{2,1,0:T(8,128)(2,1)} %add_convert_fusion.16), channel_id=1, source_target_pairs={{0,24},{4,100},{8,0},{12,108},{16,8},{20,116},{24,16},{28,124},{32... | collective-permute-start | bytes 1216520 | tf_op jit(solution)/shard_map/ppermute | solution.py:166
  21.8 7.6 %collective-permute-start.7 = (bf16[198,256]{1,0:T(8,128)(2,1)S(1)}, bf16[198,256]{1,0:T(8,128)(2,1)S(1)}, u32[]{:S(2)}, u32[]{:S(2)}) collective-permute-start(bf16[198,256]{1,0:T(8,128)(2,1)S(1)} %get-tuple-element.86), channel_id=1, source_target_pairs={{4,20},{0,64},{12,28},{8,72},{20,4},{16,80},{28,12},{24,88},{36,52... | collective-permute-start | bytes 304136 | tf_op jit(solution)/shard_map/ppermute | solution.py:171
  30.3 6.7 %collective-permute-start.12 = (bf16[198,256]{1,0:T(8,128)(2,1)S(1)}, bf16[198,256]{1,0:T(8,128)(2,1)S(1)}, u32[]{:S(2)}, u32[]{:S(2)}) collective-permute-start(bf16[198,256]{1,0:T(8,128)(2,1)S(1)} %fusion.8.refs_0_), channel_id=1, source_target_pairs={{0,3},{1,0},{2,1},{3,2},{4,7},{5,4},{6,5},{7,6},{8,11},{9,8},{10,9... | collective-permute-start | bytes 304136 | tf_op jit(solution)/shard_map/ppermute | solution.py:176
  45.9 6.4 %collective-permute-start.13 = (bf16[4,198,256]{2,1,0:T(8,128)(2,1)S(1)}, bf16[4,198,256]{2,1,0:T(8,128)(2,1)S(1)}, u32[]{:S(2)}, u32[]{:S(2)}) collective-permute-start(bf16[4,198,256]{2,1,0:T(8,128)(2,1)S(1)} %get-tuple-element.47), channel_id=1, source_target_pairs={{0,4},{4,0},{1,5},{5,1},{2,6},{6,2},{3,7},{7,3},{8,12},{12,8},{9,1... | collective-permute-start | bytes 1216520 | tf_op jit(solution)/shard_map/ppermute | solution.py:55
  47.7 8.7 %collective-permute-start.15 = (bf16[4,198,256]{2,1,0:T(8,128)(2,1)S(1)}, bf16[4,198,256]{2,1,0:T(8,128)(2,1)S(1)}, u32[]{:S(2)}, u32[]{:S(2)}) collective-permute-start(bf16[4,198,256]{2,1,0:T(8,128)(2,1)S(1)} %add_convert_fusion.13), channel_id=1, source_target_pairs={{0,16},{4,68},{8,24},{12,76},{16,0},{20,84},{24,8},{28,92},{32,48}... | collective-permute-start | bytes 1216520 | tf_op jit(solution)/shard_map/ppermute | solution.py:166
  49.1 11.6 %collective-permute-start.17 = (bf16[4,198,256]{2,1,0:T(8,128)(2,1)S(1)}, bf16[4,198,256]{2,1,0:T(8,128)(2,1)S(1)}, u32[]{:S(2)}, u32[]{:S(2)}) collective-permute-start(bf16[4,198,256]{2,1,0:T(8,128)(2,1)S(1)} %add_convert_fusion.12), channel_id=1, source_target_pairs={{0,8},{4,36},{8,16},{12,44},{16,24},{20,52},{24,0},{28,60},{32,40}... | collective-permute-start | bytes 1216520 | tf_op jit(solution)/shard_map/ppermute | solution.py:166
  49.6 11.2 %collective-permute-start.19 = (bf16[4,198,256]{2,1,0:T(8,128)(2,1)S(1)}, bf16[4,198,256]{2,1,0:T(8,128)(2,1)S(1)}, u32[]{:S(2)}, u32[]{:S(2)}) collective-permute-start(bf16[4,198,256]{2,1,0:T(8,128)(2,1)S(1)} %add_convert_fusion.11), channel_id=1, source_target_pairs={{0,24},{4,100},{8,0},{12,108},{16,8},{20,116},{24,16},{28,124},{32... | collective-permute-start | bytes 1216520 | tf_op jit(solution)/shard_map/ppermute | solution.py:166
  83.0 8.7 %collective-permute-start.28 = (bf16[4,198,256]{2,1,0:T(8,128)(2,1)S(1)}, bf16[4,198,256]{2,1,0:T(8,128)(2,1)S(1)}, u32[]{:S(2)}, u32[]{:S(2)}) collective-permute-start(bf16[4,198,256]{2,1,0:T(8,128)(2,1)S(1)} %add_convert_fusion.8), channel_id=1, source_target_pairs={{0,16},{4,68},{8,24},{12,76},{16,0},{20,84},{24,8},{28,92},{32,48}... | collective-permute-start | bytes 1216520 | tf_op jit(solution)/shard_map/ppermute | solution.py:166
  83.2 12.8 %collective-permute-start.30 = (bf16[4,198,256]{2,1,0:T(8,128)(2,1)S(1)}, bf16[4,198,256]{2,1,0:T(8,128)(2,1)S(1)}, u32[]{:S(2)}, u32[]{:S(2)}) collective-permute-start(bf16[4,198,256]{2,1,0:T(8,128)(2,1)S(1)} %add_convert_fusion.7), channel_id=1, source_target_pairs={{0,8},{4,36},{8,16},{12,44},{16,24},{20,52},{24,0},{28,60},{32,40}... | collective-permute-start | bytes 1216520 | tf_op jit(solution)/shard_map/ppermute | solution.py:166
  84.3 11.7 %collective-permute-start.32 = (bf16[4,198,256]{2,1,0:T(8,128)(2,1)S(1)}, bf16[4,198,256]{2,1,0:T(8,128)(2,1)S(1)}, u32[]{:S(2)}, u32[]{:S(2)}) collective-permute-start(bf16[4,198,256]{2,1,0:T(8,128)(2,1)S(1)} %add_convert_fusion.6), channel_id=1, source_target_pairs={{0,24},{4,100},{8,0},{12,108},{16,8},{20,116},{24,16},{28,124},{32... | collective-permute-start | bytes 1216520 | tf_op jit(solution)/shard_map/ppermute | solution.py:166
  112.8 6.2 %collective-permute-start.40 = (bf16[4,198,256]{2,1,0:T(8,128)(2,1)S(1)}, bf16[4,198,256]{2,1,0:T(8,128)(2,1)S(1)}, u32[]{:S(2)}, u32[]{:S(2)}) collective-permute-start(bf16[4,198,256]{2,1,0:T(8,128)(2,1)S(1)} %get-tuple-element.67), channel_id=1, source_target_pairs={{0,4},{4,0},{1,5},{5,1},{2,6},{6,2},{3,7},{7,3},{8,12},{12,8},{9,1... | collective-permute-start | bytes 1216520 | tf_op jit(solution)/shard_map/ppermute | solution.py:55
  116.0 11.7 %collective-permute-start.39 = (bf16[4,198,256]{2,1,0:T(8,128)(2,1)S(1)}, bf16[4,198,256]{2,1,0:T(8,128)(2,1)S(1)}, u32[]{:S(2)}, u32[]{:S(2)}) collective-permute-start(bf16[4,198,256]{2,1,0:T(8,128)(2,1)S(1)} %get-tuple-element.65), channel_id=1, source_target_pairs={{0,4},{4,0},{1,5},{5,1},{2,6},{6,2},{3,7},{7,3},{8,12},{12,8},{9,1... | collective-permute-start | bytes 1216520 | tf_op jit(solution)/shard_map/ppermute | solution.py:55
  119.8 7.7 %collective-permute-start.47 = (bf16[198,198]{1,0:T(8,128)(2,1)S(1)}, bf16[198,198]{1,0:T(8,128)(2,1)S(1)}, u32[]{:S(2)}, u32[]{:S(2)}) collective-permute-start(bf16[198,198]{1,0:T(8,128)(2,1)S(1)} %add_convert_fusion.22), channel_id=1, source_target_pairs={{0,1},{1,2},{2,3},{3,0},{4,5},{5,6},{6,7},{7,4},{8,9},{9,10},{10,1... | collective-permute-start | bytes 235232 | tf_op jit(solution)/shard_map/ppermute | solution.py:176
  120.2 8.7 %collective-permute-start.41 = (bf16[4,198,256]{2,1,0:T(8,128)(2,1)S(1)}, bf16[4,198,256]{2,1,0:T(8,128)(2,1)S(1)}, u32[]{:S(2)}, u32[]{:S(2)}) collective-permute-start(bf16[4,198,256]{2,1,0:T(8,128)(2,1)S(1)} %add_convert_fusion.3), channel_id=1, source_target_pairs={{0,16},{4,68},{8,24},{12,76},{16,0},{20,84},{24,8},{28,92},{32,48}... | collective-permute-start | bytes 1216520 | tf_op jit(solution)/shard_map/ppermute | solution.py:166
  122.6 10.7 %collective-permute-start.43 = (bf16[4,198,256]{2,1,0:T(8,128)(2,1)S(1)}, bf16[4,198,256]{2,1,0:T(8,128)(2,1)S(1)}, u32[]{:S(2)}, u32[]{:S(2)}) collective-permute-start(bf16[4,198,256]{2,1,0:T(8,128)(2,1)S(1)} %add_convert_fusion.2), channel_id=1, source_target_pairs={{0,8},{4,36},{8,16},{12,44},{16,24},{20,52},{24,0},{28,60},{32,40}... | collective-permute-start | bytes 1216520 | tf_op jit(solution)/shard_map/ppermute | solution.py:166
  124.6 8.7 %collective-permute-start.45 = (bf16[4,198,256]{2,1,0:T(8,128)(2,1)S(1)}, bf16[4,198,256]{2,1,0:T(8,128)(2,1)S(1)}, u32[]{:S(2)}, u32[]{:S(2)}) collective-permute-start(bf16[4,198,256]{2,1,0:T(8,128)(2,1)S(1)} %add_convert_fusion.1), channel_id=1, source_target_pairs={{0,24},{4,100},{8,0},{12,108},{16,8},{20,116},{24,16},{28,124},{32... | collective-permute-start | bytes 1216520 | tf_op jit(solution)/shard_map/ppermute | solution.py:166
  133.7 6.5 %collective-permute-start.50 = (bf16[2,198,256]{2,1,0:T(8,128)(2,1)S(1)}, bf16[2,198,256]{2,1,0:T(8,128)(2,1)S(1)}, u32[]{:S(2)}, u32[]{:S(2)}) collective-permute-start(bf16[2,198,256]{2,1,0:T(8,128)(2,1)S(1)} %get-tuple-element.91), channel_id=1, source_target_pairs={{4,20},{0,64},{12,28},{8,72},{20,4},{16,80},{28,12},{24,88},{36,52... | collective-permute-start | bytes 608264 | tf_op jit(solution)/shard_map/ppermute | solution.py:171
  135.0 7.4 %collective-permute-start.51 = (bf16[2,198,256]{2,1,0:T(8,128)(2,1)S(1)}, bf16[2,198,256]{2,1,0:T(8,128)(2,1)S(1)}, u32[]{:S(2)}, u32[]{:S(2)}) collective-permute-start(bf16[2,198,256]{2,1,0:T(8,128)(2,1)S(1)} %get-tuple-element.92), channel_id=1, source_target_pairs={{4,12},{0,32},{12,20},{8,40},{20,28},{16,48},{28,4},{24,56},{36,44... | collective-permute-start | bytes 608264 | tf_op jit(solution)/shard_map/ppermute | solution.py:171
  143.3 6.1 %collective-permute-start.56 = (bf16[198,256]{1,0:T(8,128)(2,1)S(1)}, bf16[198,256]{1,0:T(8,128)(2,1)S(1)}, u32[]{:S(2)}, u32[]{:S(2)}) collective-permute-start(bf16[198,256]{1,0:T(8,128)(2,1)S(1)} %get-tuple-element.89), channel_id=1, source_target_pairs={{0,8},{4,36},{8,16},{12,44},{16,24},{20,52},{24,0},{28,60},{32,40}... | collective-permute-start | bytes 304136 | tf_op jit(solution)/shard_map/ppermute | solution.py:313
  149.4 16.0 %collective-permute-start.59 = (f32[198,198]{1,0:T(8,128)S(1)}, f32[198,198]{1,0:T(8,128)S(1)}, u32[]{:S(2)}, u32[]{:S(2)}) collective-permute-start(f32[198,198]{1,0:T(8,128)S(1)} %convert_add_fusion.3.own), channel_id=1, source_target_pairs={{0,4},{4,0},{1,5},{5,1},{2,6},{6,2},{3,7},{7,3},{8,12},{12,8},{9,1... | collective-permute-start | bytes 470456 | tf_op jit(solution)/shard_map/ppermute | solution.py:55
  158.2 7.2 %collective-permute-start.53 = (bf16[198,256]{1,0:T(8,128)(2,1)S(1)}, bf16[198,256]{1,0:T(8,128)(2,1)S(1)}, u32[]{:S(2)}, u32[]{:S(2)}) collective-permute-start(bf16[198,256]{1,0:T(8,128)(2,1)S(1)} %get-tuple-element.90.a), channel_id=1, source_target_pairs={{0,1},{1,2},{2,3},{3,0},{4,5},{5,6},{6,7},{7,4},{8,9},{9,10},{10,1... | collective-permute-start | bytes 304136 | tf_op jit(solution)/shard_map/ppermute | solution.py:176
  (38 other events, 173.0 us)

commit v5 on v4

--- a/solution.py
+++ b/solution.py
@@ -259,23 +259,22 @@
     return jnp.pad(whole, ((0, 0), (0, BLOCK - ROWS)))
 
 
-def finish_kernel(core, a, b, c, d, own, other, state, grams):
-    state[...] = total(a, b, c, d).astype(BF16)
-    grams[core[0]] = own[...]
-    grams[1 - core[0]] = other[...]
-
-
-def finish(parts, own):
-    return pl.pallas_call(
+def finish_kernel(core, own, other, grams):
+    mine, theirs = own[...], other[...]
+    first = core[0] == 0
+    grams[:, 0, :] = jnp.where(first, mine, theirs)
+    grams[:, 1, :] = jnp.where(first, theirs, mine)
+
+
+def both_grams(own):
+    grams = pl.pallas_call(
         finish_kernel,
-        out_shape=[
-            jax.ShapeDtypeStruct((ROWS, BLOCK), BF16),
-            jax.ShapeDtypeStruct((SITE_COUNT, ROWS, ROWS), F32),
-        ],
-        in_specs=[pl.BlockSpec(memory_space=pltpu.SMEM)] + [VMEM] * 6,
-        out_specs=[VMEM] * 2,
+        out_shape=jax.ShapeDtypeStruct((ROWS, SITE_COUNT, ROWS), F32),
+        in_specs=[pl.BlockSpec(memory_space=pltpu.SMEM)] + [VMEM] * 2,
+        out_specs=VMEM,
         compiler_params=pltpu.CompilerParams(vmem_limit_bytes=GRANT),
-    )(lax.axis_index("core").astype(jnp.int32)[None], *parts, own, swap_cores(own))
+    )(lax.axis_index("core").astype(jnp.int32)[None], own, swap_cores(own))
+    return jnp.swapaxes(grams, 0, 1)
 
 
 def on_device(carried, site_tensors, operator_tensors, rotation, kept_columns):
@@ -293,9 +292,10 @@
             weights = load(site, tensors, near)
             state, *theirs = multiply(total, parts, their_order, weights)
             ours = multiply(None, [state], our_order, weights)
-        near = along_first(to_cores(theirs, ours))
+        mine = to_cores(theirs, ours)
+        near = along_first(mine)
         if site == 0:
-            mixing = mixing_weights(operator_tensors, near)
+            mixing = mixing_weights(operator_tensors, mine[SENT[2]])
             chosen = chosen_columns(kept_columns, near)
         parts = along_z(along_second([near[e] for e in range(RING)]))
         weights = load(site, turns, near)
@@ -309,9 +309,13 @@
         if site == SITE_COUNT - 1:
             gram = chip_gram(grams)
             both = along_second([jnp.stack([piece, gram]) for piece in pieces])
-            parts = along_z(both[0])
-            got = [lax.ppermute(both[1], BOND, shifts(d, 0)) for d in (1, 2, 3)]
-            return tuple(finish(parts, summed([both[1], *got])[:, :ROWS]))
+            parts, got = [both[0]], []
+            for d in (2, 1, 3):
+                got.append(lax.ppermute(both[1], BOND, shifts(d, 0)))
+            for d in (2, 1, 3):
+                parts.append(lax.ppermute(both[0], "z", ring_shift(d)))
+            grams = both_grams(summed([both[1], *got])[:, :ROWS])
+            return summed(parts).astype(BF16), grams
         parts = along_z(along_second(pieces))
 
 

time: 167 us -> 159 us (0.952)
  waiting for transfers between devices: 70.1 us -> 59.9 us
    ppermute x15 -> x12, waiting for transfers between devices: 21.2 us -> 14.6 us  [along_z(): lax.ppermute(array, 'z', ring_shift(d))]
    ppermute x3 -> x6, starting transfers between devices: 1.54 us -> 7.48 us  [the longest x3 5.63 us: on_device(): parts.append(lax.ppermute(both[0], 'z', ring_shift(d)))]
    ppermute x3 -> x6, waiting for transfers between devices: 5.31 us -> 0.02 us  [the longest x3 0.01 us: on_device(): parts.append(lax.ppermute(both[0], 'z', ring_shift(d)))]
    ppermute x15 -> x12, starting transfers between devices: 14.2 us -> 10.4 us  [along_z(): lax.ppermute(array, 'z', ring_shift(d))]
    ppermute x12, waiting for transfers between devices: 13.9 us -> 16.2 us  [along_second(): got = [lax.ppermute(pieces[e], BOND, shifts(e, 1)) for e in (2, 1, 3)]]
  transfers between devices with their start and end apart: 60 -> 60, of which waited for: 35 -> 29; matrix products, arithmetic and copies ran while one was open for 3% -> 3% of each run, Pallas kernels for 8% -> 9%
where the time goes in v5:
time: 159 us; the launch traced here: 158 us
  starting transfers between devices  67.6 us (43%)
  waiting for transfers between devices  59.9 us (38%)
  Pallas kernels  22.8 us (14%)
  other arithmetic  5.4 us (3%)
    ppermute x12, waiting for transfers between devices, along_first(): got = [lax.ppermute(mine[d], BOND, shifts(d, 0)) for d in (2, 1, 3)]  27.9 us
    ppermute x18, starting transfers between devices, swap_cores(): return lax.ppermute(array, 'core', [(0, 1), (1, 0)])  20.6 us
    ppermute x12, waiting for transfers between devices, along_second(): got = [lax.ppermute(pieces[e], BOND, shifts(e, 1)) for e in (2, 1, 3)]  16.2 us
    ppermute x12, starting transfers between devices, along_second(): got = [lax.ppermute(pieces[e], BOND, shifts(e, 1)) for e in (2, 1, 3)]  15.3 us
    ppermute x12, waiting for transfers between devices, along_z(): lax.ppermute(array, 'z', ring_shift(d))  14.6 us
    ppermute x12, starting transfers between devices, along_first(): got = [lax.ppermute(mine[d], BOND, shifts(d, 0)) for d in (2, 1, 3)]  13.9 us
    ppermute x12, starting transfers between devices, along_z(): lax.ppermute(array, 'z', ring_shift(d))  10.4 us
    pallas_call x7, Pallas kernels, multiply(): pl.pallas_call(functools.partial(multiply_kernel, prepare, len(operands))...  9.44 us
  transfers between devices with their start and end apart: 60, of which 29 were waited for; matrix products, arithmetic and copies ran while one was open for 3% of the time, Pallas kernels for 9%

profile of v5, /device:TPU:1, one launch (start us, length us, event | category | flops | bytes accessed | tf_op | source)
XLA Modules:
  0.0 158.5 jit_solution(7518048324008395239)
XLA Ops:
  1.0 2.3 %shard_map.68.refs_1_ = bf16[256,8192]{1,0:T(8,128)(2,1)S(1)} custom-call(bf16[512,8192]{1,0:T(8,128)(2,1)} %bitcast.55), custom_call_target="tpu_custom_call" | custom-call | bytes 4194304 | tf_op jit(solution)/shard_map/pallas_call | solution.py:82
  8.7 3.0 %collective-permute-start.2 = (bf16[4,198,256]{2,1,0:T(8,128)(2,1)}, bf16[4,198,256]{2,1,0:T(8,128)(2,1)S(1)}, u32[]{:S(2)}, u32[]{:S(2)}) collective-permute-start(bf16[4,198,256]{2,1,0:T(8,128)(2,1)} %add_convert_fusion.18), channel_id=1, source_target_pairs={{0,16},{4,68},{8,24},{12,76},{16,0},{20,84},{24,8},{28,92},{32,48}... | collective-permute-start | bytes 1216520 | tf_op jit(solution)/shard_map/ppermute | solution.py:166
  13.1 2.3 %collective-permute-start.6 = (bf16[4,198,256]{2,1,0:T(8,128)(2,1)S(1)}, bf16[4,198,256]{2,1,0:T(8,128)(2,1)S(1)}, u32[]{:S(2)}, u32[]{:S(2)}) collective-permute-start(bf16[4,198,256]{2,1,0:T(8,128)(2,1)S(1)} %add_convert_fusion.16.near), channel_id=1, source_target_pairs={{0,24},{4,100},{8,0},{12,108},{16,8},{20,116},{24,16},{28,124},{32... | collective-permute-start | bytes 1216520 | tf_op jit(solution)/shard_map/ppermute | solution.py:166
  18.5 3.5 %collective-permute-done.4 = bf16[4,198,256]{2,1,0:T(8,128)(2,1)S(1)} collective-permute-done((bf16[4,198,256]{2,1,0:T(8,128)(2,1)}, bf16[4,198,256]{2,1,0:T(8,128)(2,1)S(1)}, u32[]{:S(2)}, u32[]{:S(2)}) %collective-permute-start.4) | collective-permute-done | bytes 405536 | tf_op jit(solution)/shard_map/ppermute | solution.py:166
  22.7 2.8 %collective-permute-start.7 = (bf16[198,256]{1,0:T(8,128)(2,1)S(1)}, bf16[198,256]{1,0:T(8,128)(2,1)S(1)}, u32[]{:S(2)}, u32[]{:S(2)}) collective-permute-start(bf16[198,256]{1,0:T(8,128)(2,1)S(1)} %get-tuple-element.84), channel_id=1, source_target_pairs={{4,20},{0,64},{12,28},{8,72},{20,4},{16,80},{28,12},{24,88},{36,52... | collective-permute-start | bytes 304136 | tf_op jit(solution)/shard_map/ppermute | solution.py:171
  31.2 3.8 %collective-permute-start.12 = (bf16[198,256]{1,0:T(8,128)(2,1)S(1)}, bf16[198,256]{1,0:T(8,128)(2,1)S(1)}, u32[]{:S(2)}, u32[]{:S(2)}) collective-permute-start(bf16[198,256]{1,0:T(8,128)(2,1)S(1)} %fusion.8.refs_0_), channel_id=1, source_target_pairs={{0,3},{1,0},{2,1},{3,2},{4,7},{5,4},{6,5},{7,6},{8,11},{9,8},{10,9... | collective-permute-start | bytes 304136 | tf_op jit(solution)/shard_map/ppermute | solution.py:176
  35.7 2.2 %shard_map.72.refs_6_.refs_1_ = bf16[256,8192]{1,0:T(8,128)(2,1)S(1)} custom-call(bf16[512,8192]{1,0:T(8,128)(2,1)} %bitcast.57, bf16[4,198,256]{2,1,0:T(8,128)(2,1)S(1)} %add_convert_fusion.15.near.rest_0_), custom_call_target="tpu_custom_call" | custom-call | bytes 4194304 | tf_op jit(solution)/shard_map/pallas_call | solution.py:82
  37.9 2.2 %collective-permute-done.11.refs_2_ = bf16[198,256]{1,0:T(8,128)(2,1)S(1)} collective-permute-done((bf16[198,256]{1,0:T(8,128)(2,1)S(1)}, bf16[198,256]{1,0:T(8,128)(2,1)S(1)}, u32[]{:S(2)}, u32[]{:S(2)}) %collective-permute-start.11) | collective-permute-done | bytes 101408 | tf_op jit(solution)/shard_map/ppermute | solution.py:176
  42.4 4.3 %collective-permute-start.14 = (bf16[4,198,256]{2,1,0:T(8,128)(2,1)S(1)}, bf16[4,198,256]{2,1,0:T(8,128)(2,1)S(1)}, u32[]{:S(2)}, u32[]{:S(2)}) collective-permute-start(bf16[4,198,256]{2,1,0:T(8,128)(2,1)S(1)} %get-tuple-element.49), channel_id=1, source_target_pairs={{0,4},{4,0},{1,5},{5,1},{2,6},{6,2},{3,7},{7,3},{8,12},{12,8},{9,1... | collective-permute-start | bytes 1216520 | tf_op jit(solution)/shard_map/ppermute | solution.py:55
  50.5 2.7 %collective-permute-start.19 = (bf16[4,198,256]{2,1,0:T(8,128)(2,1)S(1)}, bf16[4,198,256]{2,1,0:T(8,128)(2,1)S(1)}, u32[]{:S(2)}, u32[]{:S(2)}) collective-permute-start(bf16[4,198,256]{2,1,0:T(8,128)(2,1)S(1)} %add_convert_fusion.11), channel_id=1, source_target_pairs={{0,24},{4,100},{8,0},{12,108},{16,8},{20,116},{24,16},{28,124},{32... | collective-permute-start | bytes 1216520 | tf_op jit(solution)/shard_map/ppermute | solution.py:166
  53.1 4.1 %collective-permute-done.15 = bf16[4,198,256]{2,1,0:T(8,128)(2,1)S(1)} collective-permute-done((bf16[4,198,256]{2,1,0:T(8,128)(2,1)S(1)}, bf16[4,198,256]{2,1,0:T(8,128)(2,1)S(1)}, u32[]{:S(2)}, u32[]{:S(2)}) %collective-permute-start.15) | collective-permute-done | bytes 405536 | tf_op jit(solution)/shard_map/ppermute | solution.py:166
  57.3 4.3 %collective-permute-done.17 = bf16[4,198,256]{2,1,0:T(8,128)(2,1)S(1)} collective-permute-done((bf16[4,198,256]{2,1,0:T(8,128)(2,1)S(1)}, bf16[4,198,256]{2,1,0:T(8,128)(2,1)S(1)}, u32[]{:S(2)}, u32[]{:S(2)}) %collective-permute-start.17) | collective-permute-done | bytes 405536 | tf_op jit(solution)/shard_map/ppermute | solution.py:166
  61.9 2.5 %collective-permute-start.20 = (bf16[198,256]{1,0:T(8,128)(2,1)S(1)}, bf16[198,256]{1,0:T(8,128)(2,1)S(1)}, u32[]{:S(2)}, u32[]{:S(2)}) collective-permute-start(bf16[198,256]{1,0:T(8,128)(2,1)S(1)} %get-tuple-element.81), channel_id=1, source_target_pairs={{4,20},{0,64},{12,28},{8,72},{20,4},{16,80},{28,12},{24,88},{36,52... | collective-permute-start | bytes 304136 | tf_op jit(solution)/shard_map/ppermute | solution.py:171
  72.3 2.2 %shard_map.75.refs_4_.refs_1_ = bf16[256,8192]{1,0:T(8,128)(2,1)S(1)} custom-call(bf16[512,8192]{1,0:T(8,128)(2,1)} %bitcast.56, bf16[4,198,256]{2,1,0:T(8,128)(2,1)S(1)} %add_convert_fusion.10.rest_0_), custom_call_target="tpu_custom_call" | custom-call | bytes 4194304 | tf_op jit(solution)/shard_map/pallas_call | solution.py:82
  78.1 3.4 %collective-permute-start.27 = (bf16[4,198,256]{2,1,0:T(8,128)(2,1)S(1)}, bf16[4,198,256]{2,1,0:T(8,128)(2,1)S(1)}, u32[]{:S(2)}, u32[]{:S(2)}) collective-permute-start(bf16[4,198,256]{2,1,0:T(8,128)(2,1)S(1)} %get-tuple-element.58), channel_id=1, source_target_pairs={{0,4},{4,0},{1,5},{5,1},{2,6},{6,2},{3,7},{7,3},{8,12},{12,8},{9,1... | collective-permute-start | bytes 1216520 | tf_op jit(solution)/shard_map/ppermute | solution.py:55
  86.6 5.5 %collective-permute-done.28 = bf16[4,198,256]{2,1,0:T(8,128)(2,1)S(1)} collective-permute-done((bf16[4,198,256]{2,1,0:T(8,128)(2,1)S(1)}, bf16[4,198,256]{2,1,0:T(8,128)(2,1)S(1)}, u32[]{:S(2)}, u32[]{:S(2)}) %collective-permute-start.28) | collective-permute-done | bytes 405536 | tf_op jit(solution)/shard_map/ppermute | solution.py:166
  92.1 4.3 %collective-permute-done.30 = bf16[4,198,256]{2,1,0:T(8,128)(2,1)S(1)} collective-permute-done((bf16[4,198,256]{2,1,0:T(8,128)(2,1)S(1)}, bf16[4,198,256]{2,1,0:T(8,128)(2,1)S(1)}, u32[]{:S(2)}, u32[]{:S(2)}) %collective-permute-start.30) | collective-permute-done | bytes 405536 | tf_op jit(solution)/shard_map/ppermute | solution.py:166
  106.7 2.2 %shard_map.78.refs_6_.refs_1_ = bf16[256,8192]{1,0:T(8,128)(2,1)S(1)} custom-call(bf16[512,8192]{1,0:T(8,128)(2,1)} %bitcast.58, bf16[4,198,256]{2,1,0:T(8,128)(2,1)S(1)} %add_convert_fusion.5.rest_0_), custom_call_target="tpu_custom_call" | custom-call | bytes 4194304 | tf_op jit(solution)/shard_map/pallas_call | solution.py:82
  113.7 3.0 %collective-permute-start.40 = (bf16[4,198,256]{2,1,0:T(8,128)(2,1)S(1)}, bf16[4,198,256]{2,1,0:T(8,128)(2,1)S(1)}, u32[]{:S(2)}, u32[]{:S(2)}) collective-permute-start(bf16[4,198,256]{2,1,0:T(8,128)(2,1)S(1)} %get-tuple-element.67), channel_id=1, source_target_pairs={{0,4},{4,0},{1,5},{5,1},{2,6},{6,2},{3,7},{7,3},{8,12},{12,8},{9,1... | collective-permute-start | bytes 1216520 | tf_op jit(solution)/shard_map/ppermute | solution.py:55
  126.2 2.2 %collective-permute-done.47 = bf16[198,198]{1,0:T(8,128)(2,1)S(1)} collective-permute-done((bf16[198,198]{1,0:T(8,128)(2,1)S(1)}, bf16[198,198]{1,0:T(8,128)(2,1)S(1)}, u32[]{:S(2)}, u32[]{:S(2)}) %collective-permute-start.47) | collective-permute-done | bytes 78440 | tf_op jit(solution)/shard_map/ppermute | solution.py:176
  129.9 4.3 %collective-permute-done.43 = bf16[4,198,256]{2,1,0:T(8,128)(2,1)S(1)} collective-permute-done((bf16[4,198,256]{2,1,0:T(8,128)(2,1)S(1)}, bf16[4,198,256]{2,1,0:T(8,128)(2,1)S(1)}, u32[]{:S(2)}, u32[]{:S(2)}) %collective-permute-start.43) | collective-permute-done | bytes 405536 | tf_op jit(solution)/shard_map/ppermute | solution.py:166
  138.5 2.5 %collective-permute-done.50 = bf16[2,198,256]{2,1,0:T(8,128)(2,1)S(1)} collective-permute-done((bf16[2,198,256]{2,1,0:T(8,128)(2,1)S(1)}, bf16[2,198,256]{2,1,0:T(8,128)(2,1)S(1)}, u32[]{:S(2)}, u32[]{:S(2)}) %collective-permute-start.50) | collective-permute-done | bytes 202784 | tf_op jit(solution)/shard_map/ppermute | solution.py:171
  141.1 2.2 %collective-permute-done.51 = bf16[2,198,256]{2,1,0:T(8,128)(2,1)S(1)} collective-permute-done((bf16[2,198,256]{2,1,0:T(8,128)(2,1)S(1)}, bf16[2,198,256]{2,1,0:T(8,128)(2,1)S(1)}, u32[]{:S(2)}, u32[]{:S(2)}) %collective-permute-start.51) | collective-permute-done | bytes 202784 | tf_op jit(solution)/shard_map/ppermute | solution.py:171
  150.9 5.5 %collective-permute-start.59 = (f32[198,198]{1,0:T(8,128)S(1)}, f32[198,198]{1,0:T(8,128)S(1)}, u32[]{:S(2)}, u32[]{:S(2)}) collective-permute-start(f32[198,198]{1,0:T(8,128)S(1)} %convert_add_fusion.3.own), channel_id=1, source_target_pairs={{0,4},{4,0},{1,5},{5,1},{2,6},{6,2},{3,7},{7,3},{8,12},{12,8},{9,1... | collective-permute-start | bytes 470456 | tf_op jit(solution)/shard_map/ppermute | solution.py:55
  (161 shorter events, 79.9 us)
Async XLA Ops:
  6.6 11.9 %collective-permute-start = (bf16[4,198,256]{2,1,0:T(8,128)(2,1)S(1)}, bf16[4,198,256]{2,1,0:T(8,128)(2,1)S(1)}, u32[]{:S(2)}, u32[]{:S(2)}) collective-permute-start(bf16[4,198,256]{2,1,0:T(8,128)(2,1)S(1)} %get-tuple-element.38), channel_id=1, source_target_pairs={{0,4},{4,0},{1,5},{5,1},{2,6},{6,2},{3,7},{7,3},{8,12},{12,8},{9,1... | collective-permute-start | bytes 1216520 | tf_op jit(solution)/shard_map/ppermute | solution.py:55
  8.7 9.8 %collective-permute-start.2 = (bf16[4,198,256]{2,1,0:T(8,128)(2,1)}, bf16[4,198,256]{2,1,0:T(8,128)(2,1)S(1)}, u32[]{:S(2)}, u32[]{:S(2)}) collective-permute-start(bf16[4,198,256]{2,1,0:T(8,128)(2,1)} %add_convert_fusion.18), channel_id=1, source_target_pairs={{0,16},{4,68},{8,24},{12,76},{16,0},{20,84},{24,8},{28,92},{32,48}... | collective-permute-start | bytes 1216520 | tf_op jit(solution)/shard_map/ppermute | solution.py:166
  12.6 9.4 %collective-permute-start.4 = (bf16[4,198,256]{2,1,0:T(8,128)(2,1)}, bf16[4,198,256]{2,1,0:T(8,128)(2,1)S(1)}, u32[]{:S(2)}, u32[]{:S(2)}) collective-permute-start(bf16[4,198,256]{2,1,0:T(8,128)(2,1)} %add_convert_fusion.17), channel_id=1, source_target_pairs={{0,8},{4,36},{8,16},{12,44},{16,24},{20,52},{24,0},{28,60},{32,40}... | collective-permute-start | bytes 1216520 | tf_op jit(solution)/shard_map/ppermute | solution.py:166
  13.1 9.2 %collective-permute-start.6 = (bf16[4,198,256]{2,1,0:T(8,128)(2,1)S(1)}, bf16[4,198,256]{2,1,0:T(8,128)(2,1)S(1)}, u32[]{:S(2)}, u32[]{:S(2)}) collective-permute-start(bf16[4,198,256]{2,1,0:T(8,128)(2,1)S(1)} %add_convert_fusion.16.near), channel_id=1, source_target_pairs={{0,24},{4,100},{8,0},{12,108},{16,8},{20,116},{24,16},{28,124},{32... | collective-permute-start | bytes 1216520 | tf_op jit(solution)/shard_map/ppermute | solution.py:166
  31.2 6.7 %collective-permute-start.12 = (bf16[198,256]{1,0:T(8,128)(2,1)S(1)}, bf16[198,256]{1,0:T(8,128)(2,1)S(1)}, u32[]{:S(2)}, u32[]{:S(2)}) collective-permute-start(bf16[198,256]{1,0:T(8,128)(2,1)S(1)} %fusion.8.refs_0_), channel_id=1, source_target_pairs={{0,3},{1,0},{2,1},{3,2},{4,7},{5,4},{6,5},{7,6},{8,11},{9,8},{10,9... | collective-permute-start | bytes 304136 | tf_op jit(solution)/shard_map/ppermute | solution.py:176
  48.5 8.7 %collective-permute-start.15 = (bf16[4,198,256]{2,1,0:T(8,128)(2,1)S(1)}, bf16[4,198,256]{2,1,0:T(8,128)(2,1)S(1)}, u32[]{:S(2)}, u32[]{:S(2)}) collective-permute-start(bf16[4,198,256]{2,1,0:T(8,128)(2,1)S(1)} %add_convert_fusion.13), channel_id=1, source_target_pairs={{0,16},{4,68},{8,24},{12,76},{16,0},{20,84},{24,8},{28,92},{32,48}... | collective-permute-start | bytes 1216520 | tf_op jit(solution)/shard_map/ppermute | solution.py:166
  50.0 11.6 %collective-permute-start.17 = (bf16[4,198,256]{2,1,0:T(8,128)(2,1)S(1)}, bf16[4,198,256]{2,1,0:T(8,128)(2,1)S(1)}, u32[]{:S(2)}, u32[]{:S(2)}) collective-permute-start(bf16[4,198,256]{2,1,0:T(8,128)(2,1)S(1)} %add_convert_fusion.12), channel_id=1, source_target_pairs={{0,8},{4,36},{8,16},{12,44},{16,24},{20,52},{24,0},{28,60},{32,40}... | collective-permute-start | bytes 1216520 | tf_op jit(solution)/shard_map/ppermute | solution.py:166
  50.5 11.2 %collective-permute-start.19 = (bf16[4,198,256]{2,1,0:T(8,128)(2,1)S(1)}, bf16[4,198,256]{2,1,0:T(8,128)(2,1)S(1)}, u32[]{:S(2)}, u32[]{:S(2)}) collective-permute-start(bf16[4,198,256]{2,1,0:T(8,128)(2,1)S(1)} %add_convert_fusion.11), channel_id=1, source_target_pairs={{0,24},{4,100},{8,0},{12,108},{16,8},{20,116},{24,16},{28,124},{32... | collective-permute-start | bytes 1216520 | tf_op jit(solution)/shard_map/ppermute | solution.py:166
  83.4 8.7 %collective-permute-start.28 = (bf16[4,198,256]{2,1,0:T(8,128)(2,1)S(1)}, bf16[4,198,256]{2,1,0:T(8,128)(2,1)S(1)}, u32[]{:S(2)}, u32[]{:S(2)}) collective-permute-start(bf16[4,198,256]{2,1,0:T(8,128)(2,1)S(1)} %add_convert_fusion.8), channel_id=1, source_target_pairs={{0,16},{4,68},{8,24},{12,76},{16,0},{20,84},{24,8},{28,92},{32,48}... | collective-permute-start | bytes 1216520 | tf_op jit(solution)/shard_map/ppermute | solution.py:166
  83.7 12.8 %collective-permute-start.30 = (bf16[4,198,256]{2,1,0:T(8,128)(2,1)S(1)}, bf16[4,198,256]{2,1,0:T(8,128)(2,1)S(1)}, u32[]{:S(2)}, u32[]{:S(2)}) collective-permute-start(bf16[4,198,256]{2,1,0:T(8,128)(2,1)S(1)} %add_convert_fusion.7), channel_id=1, source_target_pairs={{0,8},{4,36},{8,16},{12,44},{16,24},{20,52},{24,0},{28,60},{32,40}... | collective-permute-start | bytes 1216520 | tf_op jit(solution)/shard_map/ppermute | solution.py:166
  84.9 11.6 %collective-permute-start.32 = (bf16[4,198,256]{2,1,0:T(8,128)(2,1)S(1)}, bf16[4,198,256]{2,1,0:T(8,128)(2,1)S(1)}, u32[]{:S(2)}, u32[]{:S(2)}) collective-permute-start(bf16[4,198,256]{2,1,0:T(8,128)(2,1)S(1)} %add_convert_fusion.6), channel_id=1, source_target_pairs={{0,24},{4,100},{8,0},{12,108},{16,8},{20,116},{24,16},{28,124},{32... | collective-permute-start | bytes 1216520 | tf_op jit(solution)/shard_map/ppermute | solution.py:166
  116.8 11.7 %collective-permute-start.39 = (bf16[4,198,256]{2,1,0:T(8,128)(2,1)S(1)}, bf16[4,198,256]{2,1,0:T(8,128)(2,1)S(1)}, u32[]{:S(2)}, u32[]{:S(2)}) collective-permute-start(bf16[4,198,256]{2,1,0:T(8,128)(2,1)S(1)} %get-tuple-element.65), channel_id=1, source_target_pairs={{0,4},{4,0},{1,5},{5,1},{2,6},{6,2},{3,7},{7,3},{8,12},{12,8},{9,1... | collective-permute-start | bytes 1216520 | tf_op jit(solution)/shard_map/ppermute | solution.py:55
  120.7 7.7 %collective-permute-start.47 = (bf16[198,198]{1,0:T(8,128)(2,1)S(1)}, bf16[198,198]{1,0:T(8,128)(2,1)S(1)}, u32[]{:S(2)}, u32[]{:S(2)}) collective-permute-start(bf16[198,198]{1,0:T(8,128)(2,1)S(1)} %add_convert_fusion.23), channel_id=1, source_target_pairs={{0,1},{1,2},{2,3},{3,0},{4,5},{5,6},{6,7},{7,4},{8,9},{9,10},{10,1... | collective-permute-start | bytes 235232 | tf_op jit(solution)/shard_map/ppermute | solution.py:176
  121.1 8.7 %collective-permute-start.41 = (bf16[4,198,256]{2,1,0:T(8,128)(2,1)S(1)}, bf16[4,198,256]{2,1,0:T(8,128)(2,1)S(1)}, u32[]{:S(2)}, u32[]{:S(2)}) collective-permute-start(bf16[4,198,256]{2,1,0:T(8,128)(2,1)S(1)} %add_convert_fusion.3), channel_id=1, source_target_pairs={{0,16},{4,68},{8,24},{12,76},{16,0},{20,84},{24,8},{28,92},{32,48}... | collective-permute-start | bytes 1216520 | tf_op jit(solution)/shard_map/ppermute | solution.py:166
  123.5 10.7 %collective-permute-start.43 = (bf16[4,198,256]{2,1,0:T(8,128)(2,1)S(1)}, bf16[4,198,256]{2,1,0:T(8,128)(2,1)S(1)}, u32[]{:S(2)}, u32[]{:S(2)}) collective-permute-start(bf16[4,198,256]{2,1,0:T(8,128)(2,1)S(1)} %add_convert_fusion.2), channel_id=1, source_target_pairs={{0,8},{4,36},{8,16},{12,44},{16,24},{20,52},{24,0},{28,60},{32,40}... | collective-permute-start | bytes 1216520 | tf_op jit(solution)/shard_map/ppermute | solution.py:166
  125.5 8.7 %collective-permute-start.45 = (bf16[4,198,256]{2,1,0:T(8,128)(2,1)S(1)}, bf16[4,198,256]{2,1,0:T(8,128)(2,1)S(1)}, u32[]{:S(2)}, u32[]{:S(2)}) collective-permute-start(bf16[4,198,256]{2,1,0:T(8,128)(2,1)S(1)} %add_convert_fusion.1), channel_id=1, source_target_pairs={{0,24},{4,100},{8,0},{12,108},{16,8},{20,116},{24,16},{28,124},{32... | collective-permute-start | bytes 1216520 | tf_op jit(solution)/shard_map/ppermute | solution.py:166
  134.6 6.5 %collective-permute-start.50 = (bf16[2,198,256]{2,1,0:T(8,128)(2,1)S(1)}, bf16[2,198,256]{2,1,0:T(8,128)(2,1)S(1)}, u32[]{:S(2)}, u32[]{:S(2)}) collective-permute-start(bf16[2,198,256]{2,1,0:T(8,128)(2,1)S(1)} %get-tuple-element.89), channel_id=1, source_target_pairs={{4,20},{0,64},{12,28},{8,72},{20,4},{16,80},{28,12},{24,88},{36,52... | collective-permute-start | bytes 608264 | tf_op jit(solution)/shard_map/ppermute | solution.py:171
  135.8 7.4 %collective-permute-start.51 = (bf16[2,198,256]{2,1,0:T(8,128)(2,1)S(1)}, bf16[2,198,256]{2,1,0:T(8,128)(2,1)S(1)}, u32[]{:S(2)}, u32[]{:S(2)}) collective-permute-start(bf16[2,198,256]{2,1,0:T(8,128)(2,1)S(1)} %get-tuple-element.90), channel_id=1, source_target_pairs={{4,12},{0,32},{12,20},{8,40},{20,28},{16,48},{28,4},{24,56},{36,44... | collective-permute-start | bytes 608264 | tf_op jit(solution)/shard_map/ppermute | solution.py:171
  136.4 6.8 %collective-permute-start.52 = (bf16[2,198,256]{2,1,0:T(8,128)(2,1)S(1)}, bf16[2,198,256]{2,1,0:T(8,128)(2,1)S(1)}, u32[]{:S(2)}, u32[]{:S(2)}) collective-permute-start(bf16[2,198,256]{2,1,0:T(8,128)(2,1)S(1)} %get-tuple-element.91), channel_id=1, source_target_pairs={{4,28},{0,96},{12,4},{8,104},{20,12},{16,112},{28,20},{24,120},{36... | collective-permute-start | bytes 608264 | tf_op jit(solution)/shard_map/ppermute | solution.py:171
  144.0 6.9 %collective-permute-start.57 = (bf16[198,256]{1,0:T(8,128)(2,1)S(1)}, bf16[198,256]{1,0:T(8,128)(2,1)S(1)}, u32[]{:S(2)}, u32[]{:S(2)}) collective-permute-start(bf16[198,256]{1,0:T(8,128)(2,1)S(1)} %get-tuple-element.87), channel_id=1, source_target_pairs={{0,8},{4,36},{8,16},{12,44},{16,24},{20,52},{24,0},{28,60},{32,40}... | collective-permute-start | bytes 304136 | tf_op jit(solution)/shard_map/ppermute | solution.py:314
  145.2 11.3 %collective-permute-start.54 = (bf16[198,256]{1,0:T(8,128)(2,1)S(1)}, bf16[198,256]{1,0:T(8,128)(2,1)S(1)}, u32[]{:S(2)}, u32[]{:S(2)}) collective-permute-start(bf16[198,256]{1,0:T(8,128)(2,1)S(1)} %get-tuple-element.88), channel_id=1, source_target_pairs={{0,1},{1,2},{2,3},{3,0},{4,5},{5,6},{6,7},{7,4},{8,9},{9,10},{10,1... | collective-permute-start | bytes 304136 | tf_op jit(solution)/shard_map/ppermute | solution.py:316
  146.8 9.7 %collective-permute-start.53 = (bf16[198,256]{1,0:T(8,128)(2,1)S(1)}, bf16[198,256]{1,0:T(8,128)(2,1)S(1)}, u32[]{:S(2)}, u32[]{:S(2)}) collective-permute-start(bf16[198,256]{1,0:T(8,128)(2,1)S(1)} %get-tuple-element.88), channel_id=1, source_target_pairs={{0,2},{1,3},{2,0},{3,1},{4,6},{5,7},{6,4},{7,5},{8,10},{9,11},{10,... | collective-permute-start | bytes 304136 | tf_op jit(solution)/shard_map/ppermute | solution.py:316
  148.8 7.7 %collective-permute-start.55 = (bf16[198,256]{1,0:T(8,128)(2,1)S(1)}, bf16[198,256]{1,0:T(8,128)(2,1)S(1)}, u32[]{:S(2)}, u32[]{:S(2)}) collective-permute-start(bf16[198,256]{1,0:T(8,128)(2,1)S(1)} %get-tuple-element.88), channel_id=1, source_target_pairs={{0,3},{1,0},{2,1},{3,2},{4,7},{5,4},{6,5},{7,6},{8,11},{9,8},{10,9... | collective-permute-start | bytes 304136 | tf_op jit(solution)/shard_map/ppermute | solution.py:316
  150.9 6.6 %collective-permute-start.59 = (f32[198,198]{1,0:T(8,128)S(1)}, f32[198,198]{1,0:T(8,128)S(1)}, u32[]{:S(2)}, u32[]{:S(2)}) collective-permute-start(f32[198,198]{1,0:T(8,128)S(1)} %convert_add_fusion.3.own), channel_id=1, source_target_pairs={{0,4},{4,0},{1,5},{5,1},{2,6},{6,2},{3,7},{7,3},{8,12},{12,8},{9,1... | collective-permute-start | bytes 470456 | tf_op jit(solution)/shard_map/ppermute | solution.py:55
  (38 other events, 180.8 us)

commit v6 on v5

--- a/solution.py
+++ b/solution.py
@@ -18,6 +18,7 @@
 BOND = ("y", "x", "core")
 RING = 4
 BLOCK = 256
+PLACE = 2 * RING**2
 SENT = (2, 1, 3, 0)
 LOADS = 8
 LOAD_GRANT = 48 * 2**20
@@ -176,19 +177,25 @@
     return [array] + [lax.ppermute(array, "z", ring_shift(d)) for d in (1, 2, 3)]
 
 
-def mixing_kernel(z, near, operator_tensors, mixing):
+def mixing_kernel(place, near, operator_tensors, mixing):
     def iota(shape, dim):
         return lax.broadcasted_iota(jnp.int32, shape, dim)
 
     wide, tall = (ROWS, PHYSICAL * MPO_BOND), (MPO_BOND, ROWS)
-    first = z[0] * MPO_BOND
+    first = place[PLACE + 1] * MPO_BOND
     pick = (iota(wide, 1) == first + lax.rem(iota(wide, 0), MPO_BOND)).astype(BF16)
     spread = (iota(tall, 0) == lax.rem(iota(tall, 1), MPO_BOND)).astype(BF16)
     square = (ROWS, ROWS)
     same = lax.div(iota(square, 0), MPO_BOND) == lax.div(iota(square, 1), MPO_BOND)
     for site in range(SITE_COUNT):
+        whole = operator_tensors[site].astype(F32)
+        planes = [whole[:, number, :] for number in range(PHYSICAL)]
         for d in range(RING):
-            weights = operator_tensors[site, lax.rem(z[0] + RING - d, RING)]
+            turned = lax.rem(place[PLACE + 1] + RING - d, RING)
+            weights = planes[0]
+            for number in range(1, PHYSICAL):
+                weights = jnp.where(turned == number, planes[number], weights)
+            weights = weights.astype(BF16)
             narrow = lax.dot_general(
                 pick, weights, (((1,), (1,)), ((), ())), preferred_element_type=F32
             ).astype(BF16)
@@ -196,7 +203,7 @@
             mixing[site, d] = jnp.where(same, full, 0.0).astype(BF16)
 
 
-def mixing_weights(operator_tensors, near):
+def mixing_weights(operator_tensors, place, near):
     return pl.pallas_call(
         mixing_kernel,
         out_shape=jax.ShapeDtypeStruct((SITE_COUNT, RING, ROWS, ROWS), BF16),
@@ -208,7 +215,7 @@
         out_specs=VMEM,
         compiler_params=pltpu.CompilerParams(vmem_limit_bytes=8 * 2**20),
         cost_estimate=pl.CostEstimate(flops=10**9, bytes_accessed=10**6, transcendentals=0),
-    )(lax.axis_index("z").astype(jnp.int32)[None], near, operator_tensors)
+    )(place, near, jnp.swapaxes(operator_tensors, 1, 2))
 
 
 def chosen_kernel(place, near, kept_columns, chosen):
@@ -219,8 +226,8 @@
     high_of = lax.div(iota(wide, 1), 16) == iota(wide, 0)
     low_of = (lax.rem(iota(wide, 1), 16) == iota(wide, 0)).astype(F32)
     for site in range(SITE_COUNT):
-        number = kept_columns[site : site + 1, :] - place[0]
-        here = (number >= 0) & (number < BLOCK * PHYSICAL) & (lax.rem(number, PHYSICAL) == place[1])
+        number = kept_columns[site : site + 1, :] - place[PLACE]
+        here = (number >= 0) & (number < BLOCK * PHYSICAL) & (lax.rem(number, PHYSICAL) == place[PLACE + 1])
         column = jnp.where(here, lax.div(number, PHYSICAL), -1)
         high = (lax.div(column, 16) == iota(digits, 0)) & (column >= 0)
         low = lax.rem(column, 16) == iota(digits, 0)
@@ -235,8 +242,7 @@
         chosen[site] = (total > 0.5).astype(F32)
 
 
-def chosen_columns(kept_columns, near):
-    place = jnp.stack([lax.axis_index(BOND) * BLOCK * PHYSICAL, lax.axis_index("z")])
+def chosen_columns(kept_columns, place, near):
     return pl.pallas_call(
         chosen_kernel,
         out_shape=jax.ShapeDtypeStruct((SITE_COUNT, 1, BLOCK), F32),
@@ -248,7 +254,7 @@
         out_specs=VMEM,
         compiler_params=pltpu.CompilerParams(vmem_limit_bytes=GRANT),
         cost_estimate=pl.CostEstimate(flops=10**8, bytes_accessed=10**5, transcendentals=0),
-    )(place.astype(jnp.int32), near, kept_columns)
+    )(place, near, kept_columns)
 
 
 def chip_gram(grams):
@@ -280,13 +286,14 @@
 def on_device(carried, site_tensors, operator_tensors, rotation, kept_columns):
     core = lax.axis_index("core")
     their_order, our_order = block_order(1 - core), block_order(core)
+    own = jnp.stack([lax.axis_index(BOND) * BLOCK * PHYSICAL, lax.axis_index("z")])
+    places = jnp.concatenate([their_order, our_order, own.astype(jnp.int32)])
     tensors = site_tensors.reshape(SITE_COUNT * BLOCK, BOND_DIM)
     turns = rotation.reshape(SITE_COUNT * BLOCK, BOND_DIM)
     grams, near, parts = [], None, None
     for site in range(SITE_COUNT):
         if near is None:
-            both_orders = jnp.concatenate([their_order, our_order])
-            pieces = multiply(None, [carried], both_orders, load(site, tensors))
+            pieces = multiply(None, [carried], places, load(site, tensors, places))
             theirs, ours = pieces[:RING], pieces[RING:]
         else:
             weights = load(site, tensors, near)
@@ -295,8 +302,8 @@
         mine = to_cores(theirs, ours)
         near = along_first(mine)
         if site == 0:
-            mixing = mixing_weights(operator_tensors, mine[SENT[2]])
-            chosen = chosen_columns(kept_columns, near)
+            mixing = mixing_weights(operator_tensors, places, mine[SENT[2]])
+            chosen = chosen_columns(kept_columns, places, near)
         parts = along_z(along_second([near[e] for e in range(RING)]))
         weights = load(site, turns, near)
         mixed = [*parts, mixing[site], chosen[site]]

time: 159 us -> 159 us (level)
  starting transfers between devices: 67.6 us -> 63.8 us
  waiting for transfers between devices: 59.9 us -> 63.6 us
  other arithmetic: 5.4 us -> 3.78 us
    ppermute x18, starting transfers between devices: 20.6 us -> 18.4 us  [swap_cores(): return lax.ppermute(array, 'core', [(0, 1), (1, 0)])]
  transfers between devices with their start and end apart: 60 -> 60, of which waited for: 29 -> 29; matrix products, arithmetic and copies ran while one was open for 3% -> 1% of each run, Pallas kernels for 9% -> 10%
where the time goes in v6:
time: 159 us; the launch traced here: 157 us
  starting transfers between devices  63.8 us (40%)
  waiting for transfers between devices  63.6 us (40%)
  Pallas kernels  24.3 us (15%)
  other arithmetic  3.78 us (2%)
    ppermute x12, waiting for transfers between devices, along_first(): got = [lax.ppermute(mine[d], BOND, shifts(d, 0)) for d in (2, 1, 3)]  28.7 us
    ppermute x18, starting transfers between devices, swap_cores(): return lax.ppermute(array, 'core', [(0, 1), (1, 0)])  18.4 us
    ppermute x12, waiting for transfers between devices, along_second(): got = [lax.ppermute(pieces[e], BOND, shifts(e, 1)) for e in (2, 1, 3)]  17.6 us
    ppermute x12, waiting for transfers between devices, along_z(): lax.ppermute(array, 'z', ring_shift(d))  16.1 us
    ppermute x12, starting transfers between devices, along_second(): got = [lax.ppermute(pieces[e], BOND, shifts(e, 1)) for e in (2, 1, 3)]  13.9 us
    ppermute x12, starting transfers between devices, along_first(): got = [lax.ppermute(mine[d], BOND, shifts(d, 0)) for d in (2, 1, 3)]  13.6 us
    ppermute x12, starting transfers between devices, along_z(): lax.ppermute(array, 'z', ring_shift(d))  10.3 us
    pallas_call x7, Pallas kernels, multiply(): pl.pallas_call(functools.partial(multiply_kernel, prepare, len(operands))...  9.47 us
  transfers between devices with their start and end apart: 60, of which 29 were waited for; matrix products, arithmetic and copies ran while one was open for 1% of the time, Pallas kernels for 10%

profile of v6, /device:TPU:1, one launch (start us, length us, event | category | flops | bytes accessed | tf_op | source)
XLA Modules:
  0.0 157.1 jit_solution(6121384465824649631)
XLA Ops:
  1.1 2.2 %shard_map.68.refs_1_ = bf16[256,8192]{1,0:T(8,128)(2,1)S(1)} custom-call(bf16[512,8192]{1,0:T(8,128)(2,1)} %bitcast.57, s32[34]{0:T(128)S(1)} %pad_add_fusion.rest_0_.order.place), custom_call_target="tpu_custom_call" | custom-call | bytes 4194304 | tf_op jit(solution)/shard_map/pallas_call | solution.py:83
  8.0 3.1 %collective-permute-start.2 = (bf16[4,198,256]{2,1,0:T(8,128)(2,1)S(1)}, bf16[4,198,256]{2,1,0:T(8,128)(2,1)S(1)}, u32[]{:S(2)}, u32[]{:S(2)}) collective-permute-start(bf16[4,198,256]{2,1,0:T(8,128)(2,1)S(1)} %add_convert_fusion.18), channel_id=1, source_target_pairs={{0,16},{4,68},{8,24},{12,76},{16,0},{20,84},{24,8},{28,92},{32,48}... | collective-permute-start | bytes 1216520 | tf_op jit(solution)/shard_map/ppermute | solution.py:167
  11.8 2.3 %collective-permute-start.6 = (bf16[4,198,256]{2,1,0:T(8,128)(2,1)S(1)}, bf16[4,198,256]{2,1,0:T(8,128)(2,1)S(1)}, u32[]{:S(2)}, u32[]{:S(2)}) collective-permute-start(bf16[4,198,256]{2,1,0:T(8,128)(2,1)S(1)} %add_convert_fusion.16.near), channel_id=1, source_target_pairs={{0,24},{4,100},{8,0},{12,108},{16,8},{20,116},{24,16},{28,124},{32... | collective-permute-start | bytes 1216520 | tf_op jit(solution)/shard_map/ppermute | solution.py:167
  14.2 3.3 %shard_map.70 = bf16[2,4,198,198]{3,2,1,0:T(8,128)(2,1)S(1)} custom-call(s32[34]{0:T(128)S(1)} %pad_add_fusion.rest_0_.order.place, bf16[4,198,256]{2,1,0:T(8,128)(2,1)S(1)} %add_convert_fusion.16.near, bf16[2,66,4,264]{3,2,1,0:T(4,128)(2,1)S(1)} %bitcast.56), custom_call_target="tpu_custom_call" | custom-call | flops 1000000000 | bytes 1000000 | tf_op jit(solution)/shard_map/pallas_call | solution.py:207
  17.5 3.6 %collective-permute-done.4 = bf16[4,198,256]{2,1,0:T(8,128)(2,1)S(1)} collective-permute-done((bf16[4,198,256]{2,1,0:T(8,128)(2,1)S(1)}, bf16[4,198,256]{2,1,0:T(8,128)(2,1)S(1)}, u32[]{:S(2)}, u32[]{:S(2)}) %collective-permute-start.4) | collective-permute-done | bytes 405536 | tf_op jit(solution)/shard_map/ppermute | solution.py:167
  21.8 2.6 %collective-permute-start.7 = (bf16[198,256]{1,0:T(8,128)(2,1)S(1)}, bf16[198,256]{1,0:T(8,128)(2,1)S(1)}, u32[]{:S(2)}, u32[]{:S(2)}) collective-permute-start(bf16[198,256]{1,0:T(8,128)(2,1)S(1)} %get-tuple-element.84), channel_id=1, source_target_pairs={{4,20},{0,64},{12,28},{8,72},{20,4},{16,80},{28,12},{24,88},{36,52... | collective-permute-start | bytes 304136 | tf_op jit(solution)/shard_map/ppermute | solution.py:172
  30.3 3.8 %collective-permute-start.12 = (bf16[198,256]{1,0:T(8,128)(2,1)S(1)}, bf16[198,256]{1,0:T(8,128)(2,1)S(1)}, u32[]{:S(2)}, u32[]{:S(2)}) collective-permute-start(bf16[198,256]{1,0:T(8,128)(2,1)S(1)} %fusion.8.refs_0_), channel_id=1, source_target_pairs={{0,3},{1,0},{2,1},{3,2},{4,7},{5,4},{6,5},{7,6},{8,11},{9,8},{10,9... | collective-permute-start | bytes 304136 | tf_op jit(solution)/shard_map/ppermute | solution.py:177
  34.8 2.2 %shard_map.72.refs_6_.refs_1_ = bf16[256,8192]{1,0:T(8,128)(2,1)S(1)} custom-call(bf16[512,8192]{1,0:T(8,128)(2,1)} %bitcast.59, bf16[4,198,256]{2,1,0:T(8,128)(2,1)S(1)} %add_convert_fusion.15.near.rest_0_), custom_call_target="tpu_custom_call" | custom-call | bytes 4194304 | tf_op jit(solution)/shard_map/pallas_call | solution.py:83
  37.1 2.2 %collective-permute-done.11.refs_2_ = bf16[198,256]{1,0:T(8,128)(2,1)S(1)} collective-permute-done((bf16[198,256]{1,0:T(8,128)(2,1)S(1)}, bf16[198,256]{1,0:T(8,128)(2,1)S(1)}, u32[]{:S(2)}, u32[]{:S(2)}) %collective-permute-start.11) | collective-permute-done | bytes 101408 | tf_op jit(solution)/shard_map/ppermute | solution.py:177
  41.5 4.3 %collective-permute-start.14 = (bf16[4,198,256]{2,1,0:T(8,128)(2,1)S(1)}, bf16[4,198,256]{2,1,0:T(8,128)(2,1)S(1)}, u32[]{:S(2)}, u32[]{:S(2)}) collective-permute-start(bf16[4,198,256]{2,1,0:T(8,128)(2,1)S(1)} %get-tuple-element.49), channel_id=1, source_target_pairs={{0,4},{4,0},{1,5},{5,1},{2,6},{6,2},{3,7},{7,3},{8,12},{12,8},{9,1... | collective-permute-start | bytes 1216520 | tf_op jit(solution)/shard_map/ppermute | solution.py:56
  51.7 4.9 %collective-permute-done.15 = bf16[4,198,256]{2,1,0:T(8,128)(2,1)S(1)} collective-permute-done((bf16[4,198,256]{2,1,0:T(8,128)(2,1)S(1)}, bf16[4,198,256]{2,1,0:T(8,128)(2,1)S(1)}, u32[]{:S(2)}, u32[]{:S(2)}) %collective-permute-start.15) | collective-permute-done | bytes 405536 | tf_op jit(solution)/shard_map/ppermute | solution.py:167
  56.6 4.3 %collective-permute-done.17 = bf16[4,198,256]{2,1,0:T(8,128)(2,1)S(1)} collective-permute-done((bf16[4,198,256]{2,1,0:T(8,128)(2,1)S(1)}, bf16[4,198,256]{2,1,0:T(8,128)(2,1)S(1)}, u32[]{:S(2)}, u32[]{:S(2)}) %collective-permute-start.17) | collective-permute-done | bytes 405536 | tf_op jit(solution)/shard_map/ppermute | solution.py:167
  71.6 2.2 %shard_map.75.refs_4_.refs_1_ = bf16[256,8192]{1,0:T(8,128)(2,1)S(1)} custom-call(bf16[512,8192]{1,0:T(8,128)(2,1)} %bitcast.58, bf16[4,198,256]{2,1,0:T(8,128)(2,1)S(1)} %add_convert_fusion.10.rest_0_), custom_call_target="tpu_custom_call" | custom-call | bytes 4194304 | tf_op jit(solution)/shard_map/pallas_call | solution.py:83
  77.5 3.4 %collective-permute-start.27 = (bf16[4,198,256]{2,1,0:T(8,128)(2,1)S(1)}, bf16[4,198,256]{2,1,0:T(8,128)(2,1)S(1)}, u32[]{:S(2)}, u32[]{:S(2)}) collective-permute-start(bf16[4,198,256]{2,1,0:T(8,128)(2,1)S(1)} %get-tuple-element.58), channel_id=1, source_target_pairs={{0,4},{4,0},{1,5},{5,1},{2,6},{6,2},{3,7},{7,3},{8,12},{12,8},{9,1... | collective-permute-start | bytes 1216520 | tf_op jit(solution)/shard_map/ppermute | solution.py:56
  86.0 5.5 %collective-permute-done.28 = bf16[4,198,256]{2,1,0:T(8,128)(2,1)S(1)} collective-permute-done((bf16[4,198,256]{2,1,0:T(8,128)(2,1)S(1)}, bf16[4,198,256]{2,1,0:T(8,128)(2,1)S(1)}, u32[]{:S(2)}, u32[]{:S(2)}) %collective-permute-start.28) | collective-permute-done | bytes 405536 | tf_op jit(solution)/shard_map/ppermute | solution.py:167
  91.5 4.3 %collective-permute-done.30 = bf16[4,198,256]{2,1,0:T(8,128)(2,1)S(1)} collective-permute-done((bf16[4,198,256]{2,1,0:T(8,128)(2,1)S(1)}, bf16[4,198,256]{2,1,0:T(8,128)(2,1)S(1)}, u32[]{:S(2)}, u32[]{:S(2)}) %collective-permute-start.30) | collective-permute-done | bytes 405536 | tf_op jit(solution)/shard_map/ppermute | solution.py:167
  106.1 2.2 %shard_map.78.refs_6_.refs_1_ = bf16[256,8192]{1,0:T(8,128)(2,1)S(1)} custom-call(bf16[512,8192]{1,0:T(8,128)(2,1)} %bitcast.60, bf16[4,198,256]{2,1,0:T(8,128)(2,1)S(1)} %add_convert_fusion.5.rest_0_), custom_call_target="tpu_custom_call" | custom-call | bytes 4194304 | tf_op jit(solution)/shard_map/pallas_call | solution.py:83
  110.3 2.5 %collective-permute-done.36.refs_1_ = bf16[198,256]{1,0:T(8,128)(2,1)S(1)} collective-permute-done((bf16[198,256]{1,0:T(8,128)(2,1)S(1)}, bf16[198,256]{1,0:T(8,128)(2,1)S(1)}, u32[]{:S(2)}, u32[]{:S(2)}) %collective-permute-start.36) | collective-permute-done | bytes 101408 | tf_op jit(solution)/shard_map/ppermute | solution.py:177
  120.5 2.2 %collective-permute-done.49 = bf16[198,198]{1,0:T(8,128)(2,1)S(1)} collective-permute-done((bf16[198,198]{1,0:T(8,128)(2,1)S(1)}, bf16[198,198]{1,0:T(8,128)(2,1)S(1)}, u32[]{:S(2)}, u32[]{:S(2)}) %collective-permute-start.49) | collective-permute-done | bytes 78440 | tf_op jit(solution)/shard_map/ppermute | solution.py:177
  125.5 2.2 %collective-permute-done.47 = bf16[198,198]{1,0:T(8,128)(2,1)S(1)} collective-permute-done((bf16[198,198]{1,0:T(8,128)(2,1)S(1)}, bf16[198,198]{1,0:T(8,128)(2,1)S(1)}, u32[]{:S(2)}, u32[]{:S(2)}) %collective-permute-start.47) | collective-permute-done | bytes 78440 | tf_op jit(solution)/shard_map/ppermute | solution.py:177
  129.0 4.3 %collective-permute-done.43 = bf16[4,198,256]{2,1,0:T(8,128)(2,1)S(1)} collective-permute-done((bf16[4,198,256]{2,1,0:T(8,128)(2,1)S(1)}, bf16[4,198,256]{2,1,0:T(8,128)(2,1)S(1)}, u32[]{:S(2)}, u32[]{:S(2)}) %collective-permute-start.43) | collective-permute-done | bytes 405536 | tf_op jit(solution)/shard_map/ppermute | solution.py:167
  137.1 2.8 %collective-permute-done.50 = bf16[2,198,256]{2,1,0:T(8,128)(2,1)S(1)} collective-permute-done((bf16[2,198,256]{2,1,0:T(8,128)(2,1)S(1)}, bf16[2,198,256]{2,1,0:T(8,128)(2,1)S(1)}, u32[]{:S(2)}, u32[]{:S(2)}) %collective-permute-start.50) | collective-permute-done | bytes 202784 | tf_op jit(solution)/shard_map/ppermute | solution.py:172
  140.0 2.4 %collective-permute-done.51 = bf16[2,198,256]{2,1,0:T(8,128)(2,1)S(1)} collective-permute-done((bf16[2,198,256]{2,1,0:T(8,128)(2,1)S(1)}, bf16[2,198,256]{2,1,0:T(8,128)(2,1)S(1)}, u32[]{:S(2)}, u32[]{:S(2)}) %collective-permute-start.51) | collective-permute-done | bytes 202784 | tf_op jit(solution)/shard_map/ppermute | solution.py:172
  150.2 4.9 %collective-permute-start.59 = (f32[198,198]{1,0:T(8,128)S(1)}, f32[198,198]{1,0:T(8,128)S(1)}, u32[]{:S(2)}, u32[]{:S(2)}) collective-permute-start(f32[198,198]{1,0:T(8,128)S(1)} %convert_add_fusion.3.own), channel_id=1, source_target_pairs={{0,4},{4,0},{1,5},{5,1},{2,6},{6,2},{3,7},{7,3},{8,12},{12,8},{9,1... | collective-permute-start | bytes 470456 | tf_op jit(solution)/shard_map/ppermute | solution.py:56
  (161 shorter events, 77.9 us)
Async XLA Ops:
  6.6 10.9 %collective-permute-start = (bf16[4,198,256]{2,1,0:T(8,128)(2,1)S(1)}, bf16[4,198,256]{2,1,0:T(8,128)(2,1)S(1)}, u32[]{:S(2)}, u32[]{:S(2)}) collective-permute-start(bf16[4,198,256]{2,1,0:T(8,128)(2,1)S(1)} %get-tuple-element.38), channel_id=1, source_target_pairs={{0,4},{4,0},{1,5},{5,1},{2,6},{6,2},{3,7},{7,3},{8,12},{12,8},{9,1... | collective-permute-start | bytes 1216520 | tf_op jit(solution)/shard_map/ppermute | solution.py:56
  8.0 9.5 %collective-permute-start.2 = (bf16[4,198,256]{2,1,0:T(8,128)(2,1)S(1)}, bf16[4,198,256]{2,1,0:T(8,128)(2,1)S(1)}, u32[]{:S(2)}, u32[]{:S(2)}) collective-permute-start(bf16[4,198,256]{2,1,0:T(8,128)(2,1)S(1)} %add_convert_fusion.18), channel_id=1, source_target_pairs={{0,16},{4,68},{8,24},{12,76},{16,0},{20,84},{24,8},{28,92},{32,48}... | collective-permute-start | bytes 1216520 | tf_op jit(solution)/shard_map/ppermute | solution.py:167
  11.2 9.9 %collective-permute-start.4 = (bf16[4,198,256]{2,1,0:T(8,128)(2,1)S(1)}, bf16[4,198,256]{2,1,0:T(8,128)(2,1)S(1)}, u32[]{:S(2)}, u32[]{:S(2)}) collective-permute-start(bf16[4,198,256]{2,1,0:T(8,128)(2,1)S(1)} %add_convert_fusion.17), channel_id=1, source_target_pairs={{0,8},{4,36},{8,16},{12,44},{16,24},{20,52},{24,0},{28,60},{32,40}... | collective-permute-start | bytes 1216520 | tf_op jit(solution)/shard_map/ppermute | solution.py:167
  11.8 9.7 %collective-permute-start.6 = (bf16[4,198,256]{2,1,0:T(8,128)(2,1)S(1)}, bf16[4,198,256]{2,1,0:T(8,128)(2,1)S(1)}, u32[]{:S(2)}, u32[]{:S(2)}) collective-permute-start(bf16[4,198,256]{2,1,0:T(8,128)(2,1)S(1)} %add_convert_fusion.16.near), channel_id=1, source_target_pairs={{0,24},{4,100},{8,0},{12,108},{16,8},{20,116},{24,16},{28,124},{32... | collective-permute-start | bytes 1216520 | tf_op jit(solution)/shard_map/ppermute | solution.py:167
  30.3 6.7 %collective-permute-start.12 = (bf16[198,256]{1,0:T(8,128)(2,1)S(1)}, bf16[198,256]{1,0:T(8,128)(2,1)S(1)}, u32[]{:S(2)}, u32[]{:S(2)}) collective-permute-start(bf16[198,256]{1,0:T(8,128)(2,1)S(1)} %fusion.8.refs_0_), channel_id=1, source_target_pairs={{0,3},{1,0},{2,1},{3,2},{4,7},{5,4},{6,5},{7,6},{8,11},{9,8},{10,9... | collective-permute-start | bytes 304136 | tf_op jit(solution)/shard_map/ppermute | solution.py:177
  47.7 8.9 %collective-permute-start.15 = (bf16[4,198,256]{2,1,0:T(8,128)(2,1)S(1)}, bf16[4,198,256]{2,1,0:T(8,128)(2,1)S(1)}, u32[]{:S(2)}, u32[]{:S(2)}) collective-permute-start(bf16[4,198,256]{2,1,0:T(8,128)(2,1)S(1)} %add_convert_fusion.13), channel_id=1, source_target_pairs={{0,16},{4,68},{8,24},{12,76},{16,0},{20,84},{24,8},{28,92},{32,48}... | collective-permute-start | bytes 1216520 | tf_op jit(solution)/shard_map/ppermute | solution.py:167
  48.8 12.2 %collective-permute-start.17 = (bf16[4,198,256]{2,1,0:T(8,128)(2,1)S(1)}, bf16[4,198,256]{2,1,0:T(8,128)(2,1)S(1)}, u32[]{:S(2)}, u32[]{:S(2)}) collective-permute-start(bf16[4,198,256]{2,1,0:T(8,128)(2,1)S(1)} %add_convert_fusion.12), channel_id=1, source_target_pairs={{0,8},{4,36},{8,16},{12,44},{16,24},{20,52},{24,0},{28,60},{32,40}... | collective-permute-start | bytes 1216520 | tf_op jit(solution)/shard_map/ppermute | solution.py:167
  49.8 11.2 %collective-permute-start.19 = (bf16[4,198,256]{2,1,0:T(8,128)(2,1)S(1)}, bf16[4,198,256]{2,1,0:T(8,128)(2,1)S(1)}, u32[]{:S(2)}, u32[]{:S(2)}) collective-permute-start(bf16[4,198,256]{2,1,0:T(8,128)(2,1)S(1)} %add_convert_fusion.11), channel_id=1, source_target_pairs={{0,24},{4,100},{8,0},{12,108},{16,8},{20,116},{24,16},{28,124},{32... | collective-permute-start | bytes 1216520 | tf_op jit(solution)/shard_map/ppermute | solution.py:167
  82.7 8.7 %collective-permute-start.28 = (bf16[4,198,256]{2,1,0:T(8,128)(2,1)S(1)}, bf16[4,198,256]{2,1,0:T(8,128)(2,1)S(1)}, u32[]{:S(2)}, u32[]{:S(2)}) collective-permute-start(bf16[4,198,256]{2,1,0:T(8,128)(2,1)S(1)} %add_convert_fusion.8), channel_id=1, source_target_pairs={{0,16},{4,68},{8,24},{12,76},{16,0},{20,84},{24,8},{28,92},{32,48}... | collective-permute-start | bytes 1216520 | tf_op jit(solution)/shard_map/ppermute | solution.py:167
  83.0 12.8 %collective-permute-start.30 = (bf16[4,198,256]{2,1,0:T(8,128)(2,1)S(1)}, bf16[4,198,256]{2,1,0:T(8,128)(2,1)S(1)}, u32[]{:S(2)}, u32[]{:S(2)}) collective-permute-start(bf16[4,198,256]{2,1,0:T(8,128)(2,1)S(1)} %add_convert_fusion.7), channel_id=1, source_target_pairs={{0,8},{4,36},{8,16},{12,44},{16,24},{20,52},{24,0},{28,60},{32,40}... | collective-permute-start | bytes 1216520 | tf_op jit(solution)/shard_map/ppermute | solution.py:167
  84.2 11.6 %collective-permute-start.32 = (bf16[4,198,256]{2,1,0:T(8,128)(2,1)S(1)}, bf16[4,198,256]{2,1,0:T(8,128)(2,1)S(1)}, u32[]{:S(2)}, u32[]{:S(2)}) collective-permute-start(bf16[4,198,256]{2,1,0:T(8,128)(2,1)S(1)} %add_convert_fusion.6), channel_id=1, source_target_pairs={{0,24},{4,100},{8,0},{12,108},{16,8},{20,116},{24,16},{28,124},{32... | collective-permute-start | bytes 1216520 | tf_op jit(solution)/shard_map/ppermute | solution.py:167
  105.8 7.0 %collective-permute-start.36 = (bf16[198,256]{1,0:T(8,128)(2,1)S(1)}, bf16[198,256]{1,0:T(8,128)(2,1)S(1)}, u32[]{:S(2)}, u32[]{:S(2)}) collective-permute-start(bf16[198,256]{1,0:T(8,128)(2,1)S(1)} %fusion.2.refs_0_), channel_id=1, source_target_pairs={{0,1},{1,2},{2,3},{3,0},{4,5},{5,6},{6,7},{7,4},{8,9},{9,10},{10,1... | collective-permute-start | bytes 304136 | tf_op jit(solution)/shard_map/ppermute | solution.py:177
  116.1 11.6 %collective-permute-start.39 = (bf16[4,198,256]{2,1,0:T(8,128)(2,1)S(1)}, bf16[4,198,256]{2,1,0:T(8,128)(2,1)S(1)}, u32[]{:S(2)}, u32[]{:S(2)}) collective-permute-start(bf16[4,198,256]{2,1,0:T(8,128)(2,1)S(1)} %get-tuple-element.65), channel_id=1, source_target_pairs={{0,4},{4,0},{1,5},{5,1},{2,6},{6,2},{3,7},{7,3},{8,12},{12,8},{9,1... | collective-permute-start | bytes 1216520 | tf_op jit(solution)/shard_map/ppermute | solution.py:56
  119.9 7.8 %collective-permute-start.47 = (bf16[198,198]{1,0:T(8,128)(2,1)S(1)}, bf16[198,198]{1,0:T(8,128)(2,1)S(1)}, u32[]{:S(2)}, u32[]{:S(2)}) collective-permute-start(bf16[198,198]{1,0:T(8,128)(2,1)S(1)} %add_convert_fusion.23), channel_id=1, source_target_pairs={{0,1},{1,2},{2,3},{3,0},{4,5},{5,6},{6,7},{7,4},{8,9},{9,10},{10,1... | collective-permute-start | bytes 235232 | tf_op jit(solution)/shard_map/ppermute | solution.py:177
  120.2 8.7 %collective-permute-start.41 = (bf16[4,198,256]{2,1,0:T(8,128)(2,1)S(1)}, bf16[4,198,256]{2,1,0:T(8,128)(2,1)S(1)}, u32[]{:S(2)}, u32[]{:S(2)}) collective-permute-start(bf16[4,198,256]{2,1,0:T(8,128)(2,1)S(1)} %add_convert_fusion.3), channel_id=1, source_target_pairs={{0,16},{4,68},{8,24},{12,76},{16,0},{20,84},{24,8},{28,92},{32,48}... | collective-permute-start | bytes 1216520 | tf_op jit(solution)/shard_map/ppermute | solution.py:167
  122.8 10.5 %collective-permute-start.43 = (bf16[4,198,256]{2,1,0:T(8,128)(2,1)S(1)}, bf16[4,198,256]{2,1,0:T(8,128)(2,1)S(1)}, u32[]{:S(2)}, u32[]{:S(2)}) collective-permute-start(bf16[4,198,256]{2,1,0:T(8,128)(2,1)S(1)} %add_convert_fusion.2), channel_id=1, source_target_pairs={{0,8},{4,36},{8,16},{12,44},{16,24},{20,52},{24,0},{28,60},{32,40}... | collective-permute-start | bytes 1216520 | tf_op jit(solution)/shard_map/ppermute | solution.py:167
  124.7 8.6 %collective-permute-start.45 = (bf16[4,198,256]{2,1,0:T(8,128)(2,1)S(1)}, bf16[4,198,256]{2,1,0:T(8,128)(2,1)S(1)}, u32[]{:S(2)}, u32[]{:S(2)}) collective-permute-start(bf16[4,198,256]{2,1,0:T(8,128)(2,1)S(1)} %add_convert_fusion.1), channel_id=1, source_target_pairs={{0,24},{4,100},{8,0},{12,108},{16,8},{20,116},{24,16},{28,124},{32... | collective-permute-start | bytes 1216520 | tf_op jit(solution)/shard_map/ppermute | solution.py:167
  133.7 6.3 %collective-permute-start.50 = (bf16[2,198,256]{2,1,0:T(8,128)(2,1)S(1)}, bf16[2,198,256]{2,1,0:T(8,128)(2,1)S(1)}, u32[]{:S(2)}, u32[]{:S(2)}) collective-permute-start(bf16[2,198,256]{2,1,0:T(8,128)(2,1)S(1)} %get-tuple-element.89), channel_id=1, source_target_pairs={{4,20},{0,64},{12,28},{8,72},{20,4},{16,80},{28,12},{24,88},{36,52... | collective-permute-start | bytes 608264 | tf_op jit(solution)/shard_map/ppermute | solution.py:172
  134.5 7.9 %collective-permute-start.51 = (bf16[2,198,256]{2,1,0:T(8,128)(2,1)S(1)}, bf16[2,198,256]{2,1,0:T(8,128)(2,1)S(1)}, u32[]{:S(2)}, u32[]{:S(2)}) collective-permute-start(bf16[2,198,256]{2,1,0:T(8,128)(2,1)S(1)} %get-tuple-element.90), channel_id=1, source_target_pairs={{4,12},{0,32},{12,20},{8,40},{20,28},{16,48},{28,4},{24,56},{36,44... | collective-permute-start | bytes 608264 | tf_op jit(solution)/shard_map/ppermute | solution.py:172
  135.7 6.6 %collective-permute-start.52 = (bf16[2,198,256]{2,1,0:T(8,128)(2,1)S(1)}, bf16[2,198,256]{2,1,0:T(8,128)(2,1)S(1)}, u32[]{:S(2)}, u32[]{:S(2)}) collective-permute-start(bf16[2,198,256]{2,1,0:T(8,128)(2,1)S(1)} %get-tuple-element.91), channel_id=1, source_target_pairs={{4,28},{0,96},{12,4},{8,104},{20,12},{16,112},{28,20},{24,120},{36... | collective-permute-start | bytes 608264 | tf_op jit(solution)/shard_map/ppermute | solution.py:172
  143.1 7.1 %collective-permute-start.57 = (bf16[198,256]{1,0:T(8,128)(2,1)S(1)}, bf16[198,256]{1,0:T(8,128)(2,1)S(1)}, u32[]{:S(2)}, u32[]{:S(2)}) collective-permute-start(bf16[198,256]{1,0:T(8,128)(2,1)S(1)} %get-tuple-element.87), channel_id=1, source_target_pairs={{0,8},{4,36},{8,16},{12,44},{16,24},{20,52},{24,0},{28,60},{32,40}... | collective-permute-start | bytes 304136 | tf_op jit(solution)/shard_map/ppermute | solution.py:321
  144.3 10.8 %collective-permute-start.54 = (bf16[198,256]{1,0:T(8,128)(2,1)S(1)}, bf16[198,256]{1,0:T(8,128)(2,1)S(1)}, u32[]{:S(2)}, u32[]{:S(2)}) collective-permute-start(bf16[198,256]{1,0:T(8,128)(2,1)S(1)} %get-tuple-element.88), channel_id=1, source_target_pairs={{0,1},{1,2},{2,3},{3,0},{4,5},{5,6},{6,7},{7,4},{8,9},{9,10},{10,1... | collective-permute-start | bytes 304136 | tf_op jit(solution)/shard_map/ppermute | solution.py:323
  146.1 9.1 %collective-permute-start.53 = (bf16[198,256]{1,0:T(8,128)(2,1)S(1)}, bf16[198,256]{1,0:T(8,128)(2,1)S(1)}, u32[]{:S(2)}, u32[]{:S(2)}) collective-permute-start(bf16[198,256]{1,0:T(8,128)(2,1)S(1)} %get-tuple-element.88), channel_id=1, source_target_pairs={{0,2},{1,3},{2,0},{3,1},{4,6},{5,7},{6,4},{7,5},{8,10},{9,11},{10,... | collective-permute-start | bytes 304136 | tf_op jit(solution)/shard_map/ppermute | solution.py:323
  148.1 7.0 %collective-permute-start.55 = (bf16[198,256]{1,0:T(8,128)(2,1)S(1)}, bf16[198,256]{1,0:T(8,128)(2,1)S(1)}, u32[]{:S(2)}, u32[]{:S(2)}) collective-permute-start(bf16[198,256]{1,0:T(8,128)(2,1)S(1)} %get-tuple-element.88), channel_id=1, source_target_pairs={{0,3},{1,0},{2,1},{3,2},{4,7},{5,4},{6,5},{7,6},{8,11},{9,8},{10,9... | collective-permute-start | bytes 304136 | tf_op jit(solution)/shard_map/ppermute | solution.py:323
  (39 other events, 189.8 us)

commit v7 on v6

--- a/solution.py
+++ b/solution.py
@@ -265,22 +265,41 @@
     return jnp.pad(whole, ((0, 0), (0, BLOCK - ROWS)))
 
 
-def finish_kernel(core, own, other, grams):
+def finish_kernel(core, own, other, grams, done):
+    done[...] = jnp.zeros_like(done)
     mine, theirs = own[...], other[...]
     first = core[0] == 0
     grams[:, 0, :] = jnp.where(first, mine, theirs)
     grams[:, 1, :] = jnp.where(first, theirs, mine)
 
 
+def state_kernel(after, a, b, c, d, state):
+    state[...] = total(a, b, c, d).astype(BF16)
+
+
+def last_state(parts, after):
+    return pl.pallas_call(
+        state_kernel,
+        out_shape=jax.ShapeDtypeStruct((ROWS, BLOCK), BF16),
+        in_specs=[pl.BlockSpec(memory_space=pl.ANY)] + [VMEM] * 4,
+        out_specs=VMEM,
+        compiler_params=pltpu.CompilerParams(vmem_limit_bytes=GRANT),
+        cost_estimate=pl.CostEstimate(flops=10**5, bytes_accessed=10**5, transcendentals=0),
+    )(after, *parts)
+
+
 def both_grams(own):
-    grams = pl.pallas_call(
+    other = swap_cores(own)
+    return pl.pallas_call(
         finish_kernel,
-        out_shape=jax.ShapeDtypeStruct((ROWS, SITE_COUNT, ROWS), F32),
+        out_shape=[
+            jax.ShapeDtypeStruct((ROWS, SITE_COUNT, ROWS), F32),
+            jax.ShapeDtypeStruct((8, 128), F32),
+        ],
         in_specs=[pl.BlockSpec(memory_space=pltpu.SMEM)] + [VMEM] * 2,
-        out_specs=VMEM,
-        compiler_params=pltpu.CompilerParams(vmem_limit_bytes=GRANT),
-    )(lax.axis_index("core").astype(jnp.int32)[None], own, swap_cores(own))
-    return jnp.swapaxes(grams, 0, 1)
+        out_specs=[VMEM] * 2,
+        compiler_params=pltpu.CompilerParams(vmem_limit_bytes=GRANT),
+    )(lax.axis_index("core").astype(jnp.int32)[None], own, other)
 
 
 def on_device(carried, site_tensors, operator_tensors, rotation, kept_columns):
@@ -321,8 +340,8 @@
                 got.append(lax.ppermute(both[1], BOND, shifts(d, 0)))
             for d in (2, 1, 3):
                 parts.append(lax.ppermute(both[0], "z", ring_shift(d)))
-            grams = both_grams(summed([both[1], *got])[:, :ROWS])
-            return summed(parts).astype(BF16), grams
+            grams, done = both_grams(summed([both[1], *got])[:, :ROWS])
+            return last_state(parts, done), jnp.swapaxes(grams, 0, 1)
         parts = along_z(along_second(pieces))
 
 

time: 159 us -> 165 us (1.038)
  waiting for transfers between devices: 63.6 us -> 71.9 us
    ppermute x3, waiting for transfers between devices: 0.01 us -> 4.76 us  [on_device(): got.append(lax.ppermute(both[1], BOND, shifts(d, 0)))]
    ppermute x3, waiting for transfers between devices: 0.01 us -> 3.92 us  [on_device(): parts.append(lax.ppermute(both[0], 'z', ring_shift(d)))]
  transfers between devices with their start and end apart: 60 -> 60, of which waited for: 29 -> 33; matrix products, arithmetic and copies ran while one was open for 1% -> 1% of each run, Pallas kernels for 10% -> 10%
where the time goes in v7:
time: 165 us
  waiting for transfers between devices  71.9 us (44%)
  starting transfers between devices  62.9 us (38%)
  Pallas kernels  25 us (15%)
  other arithmetic  3.07 us (2%)
    ppermute x12, waiting for transfers between devices, along_first(): got = [lax.ppermute(mine[d], BOND, shifts(d, 0)) for d in (2, 1, 3)]  28.7 us
    ppermute x18, starting transfers between devices, swap_cores(): return lax.ppermute(array, 'core', [(0, 1), (1, 0)])  18.8 us
    ppermute x12, waiting for transfers between devices, along_second(): got = [lax.ppermute(pieces[e], BOND, shifts(e, 1)) for e in (2, 1, 3)]  17.6 us
    ppermute x12, waiting for transfers between devices, along_z(): lax.ppermute(array, 'z', ring_shift(d))  16.1 us
    ppermute x12, starting transfers between devices, along_second(): got = [lax.ppermute(pieces[e], BOND, shifts(e, 1)) for e in (2, 1, 3)]  13.9 us
    ppermute x12, starting transfers between devices, along_first(): got = [lax.ppermute(mine[d], BOND, shifts(d, 0)) for d in (2, 1, 3)]  13.6 us
    ppermute x12, starting transfers between devices, along_z(): lax.ppermute(array, 'z', ring_shift(d))  10.3 us
    pallas_call x7, Pallas kernels, multiply(): pl.pallas_call(functools.partial(multiply_kernel, prepare, len(operands))...  9.47 us
  transfers between devices with their start and end apart: 60, of which 33 were waited for; matrix products, arithmetic and copies ran while one was open for 1% of the time, Pallas kernels for 10%

profile of v7, /device:TPU:1, one launch (start us, length us, event | category | flops | bytes accessed | tf_op | source)
XLA Modules:
  0.0 164.5 jit_solution(10044143216293480634)
XLA Ops:
  1.1 2.2 %shard_map.68.refs_1_ = bf16[256,8192]{1,0:T(8,128)(2,1)S(1)} custom-call(bf16[512,8192]{1,0:T(8,128)(2,1)} %bitcast.55, s32[34]{0:T(128)S(1)} %pad_add_fusion.rest_0_.order.place), custom_call_target="tpu_custom_call" | custom-call | bytes 4194304 | tf_op jit(solution)/shard_map/pallas_call | solution.py:83
  8.0 3.1 %collective-permute-start.2 = (bf16[4,198,256]{2,1,0:T(8,128)(2,1)S(1)}, bf16[4,198,256]{2,1,0:T(8,128)(2,1)S(1)}, u32[]{:S(2)}, u32[]{:S(2)}) collective-permute-start(bf16[4,198,256]{2,1,0:T(8,128)(2,1)S(1)} %add_convert_fusion.18), channel_id=1, source_target_pairs={{0,16},{4,68},{8,24},{12,76},{16,0},{20,84},{24,8},{28,92},{32,48}... | collective-permute-start | bytes 1216520 | tf_op jit(solution)/shard_map/ppermute | solution.py:167
  11.8 2.3 %collective-permute-start.6 = (bf16[4,198,256]{2,1,0:T(8,128)(2,1)S(1)}, bf16[4,198,256]{2,1,0:T(8,128)(2,1)S(1)}, u32[]{:S(2)}, u32[]{:S(2)}) collective-permute-start(bf16[4,198,256]{2,1,0:T(8,128)(2,1)S(1)} %add_convert_fusion.16.near), channel_id=1, source_target_pairs={{0,24},{4,100},{8,0},{12,108},{16,8},{20,116},{24,16},{28,124},{32... | collective-permute-start | bytes 1216520 | tf_op jit(solution)/shard_map/ppermute | solution.py:167
  14.2 3.3 %shard_map.70 = bf16[2,4,198,198]{3,2,1,0:T(8,128)(2,1)S(1)} custom-call(s32[34]{0:T(128)S(1)} %pad_add_fusion.rest_0_.order.place, bf16[4,198,256]{2,1,0:T(8,128)(2,1)S(1)} %add_convert_fusion.16.near, bf16[2,66,4,264]{3,2,1,0:T(4,128)(2,1)S(1)} %bitcast.54), custom_call_target="tpu_custom_call" | custom-call | flops 1000000000 | bytes 1000000 | tf_op jit(solution)/shard_map/pallas_call | solution.py:207
  17.5 3.6 %collective-permute-done.4 = bf16[4,198,256]{2,1,0:T(8,128)(2,1)S(1)} collective-permute-done((bf16[4,198,256]{2,1,0:T(8,128)(2,1)S(1)}, bf16[4,198,256]{2,1,0:T(8,128)(2,1)S(1)}, u32[]{:S(2)}, u32[]{:S(2)}) %collective-permute-start.4) | collective-permute-done | bytes 405536 | tf_op jit(solution)/shard_map/ppermute | solution.py:167
  21.8 2.6 %collective-permute-start.7 = (bf16[198,256]{1,0:T(8,128)(2,1)S(1)}, bf16[198,256]{1,0:T(8,128)(2,1)S(1)}, u32[]{:S(2)}, u32[]{:S(2)}) collective-permute-start(bf16[198,256]{1,0:T(8,128)(2,1)S(1)} %get-tuple-element.88), channel_id=1, source_target_pairs={{4,20},{0,64},{12,28},{8,72},{20,4},{16,80},{28,12},{24,88},{36,52... | collective-permute-start | bytes 304136 | tf_op jit(solution)/shard_map/ppermute | solution.py:172
  30.3 3.8 %collective-permute-start.12 = (bf16[198,256]{1,0:T(8,128)(2,1)S(1)}, bf16[198,256]{1,0:T(8,128)(2,1)S(1)}, u32[]{:S(2)}, u32[]{:S(2)}) collective-permute-start(bf16[198,256]{1,0:T(8,128)(2,1)S(1)} %fusion.8.refs_0_), channel_id=1, source_target_pairs={{0,3},{1,0},{2,1},{3,2},{4,7},{5,4},{6,5},{7,6},{8,11},{9,8},{10,9... | collective-permute-start | bytes 304136 | tf_op jit(solution)/shard_map/ppermute | solution.py:177
  34.8 2.2 %shard_map.72.refs_6_.refs_1_ = bf16[256,8192]{1,0:T(8,128)(2,1)S(1)} custom-call(bf16[512,8192]{1,0:T(8,128)(2,1)} %bitcast.57, bf16[4,198,256]{2,1,0:T(8,128)(2,1)S(1)} %add_convert_fusion.15.near.rest_0_), custom_call_target="tpu_custom_call" | custom-call | bytes 4194304 | tf_op jit(solution)/shard_map/pallas_call | solution.py:83
  37.1 2.2 %collective-permute-done.11.refs_2_ = bf16[198,256]{1,0:T(8,128)(2,1)S(1)} collective-permute-done((bf16[198,256]{1,0:T(8,128)(2,1)S(1)}, bf16[198,256]{1,0:T(8,128)(2,1)S(1)}, u32[]{:S(2)}, u32[]{:S(2)}) %collective-permute-start.11) | collective-permute-done | bytes 101408 | tf_op jit(solution)/shard_map/ppermute | solution.py:177
  41.5 4.3 %collective-permute-start.14 = (bf16[4,198,256]{2,1,0:T(8,128)(2,1)S(1)}, bf16[4,198,256]{2,1,0:T(8,128)(2,1)S(1)}, u32[]{:S(2)}, u32[]{:S(2)}) collective-permute-start(bf16[4,198,256]{2,1,0:T(8,128)(2,1)S(1)} %get-tuple-element.51), channel_id=1, source_target_pairs={{0,4},{4,0},{1,5},{5,1},{2,6},{6,2},{3,7},{7,3},{8,12},{12,8},{9,1... | collective-permute-start | bytes 1216520 | tf_op jit(solution)/shard_map/ppermute | solution.py:56
  51.7 4.9 %collective-permute-done.15 = bf16[4,198,256]{2,1,0:T(8,128)(2,1)S(1)} collective-permute-done((bf16[4,198,256]{2,1,0:T(8,128)(2,1)S(1)}, bf16[4,198,256]{2,1,0:T(8,128)(2,1)S(1)}, u32[]{:S(2)}, u32[]{:S(2)}) %collective-permute-start.15) | collective-permute-done | bytes 405536 | tf_op jit(solution)/shard_map/ppermute | solution.py:167
  56.6 4.3 %collective-permute-done.17 = bf16[4,198,256]{2,1,0:T(8,128)(2,1)S(1)} collective-permute-done((bf16[4,198,256]{2,1,0:T(8,128)(2,1)S(1)}, bf16[4,198,256]{2,1,0:T(8,128)(2,1)S(1)}, u32[]{:S(2)}, u32[]{:S(2)}) %collective-permute-start.17) | collective-permute-done | bytes 405536 | tf_op jit(solution)/shard_map/ppermute | solution.py:167
  71.6 2.2 %shard_map.75.refs_4_.refs_1_ = bf16[256,8192]{1,0:T(8,128)(2,1)S(1)} custom-call(bf16[512,8192]{1,0:T(8,128)(2,1)} %bitcast.56, bf16[4,198,256]{2,1,0:T(8,128)(2,1)S(1)} %add_convert_fusion.10.rest_0_), custom_call_target="tpu_custom_call" | custom-call | bytes 4194304 | tf_op jit(solution)/shard_map/pallas_call | solution.py:83
  77.5 3.4 %collective-permute-start.27 = (bf16[4,198,256]{2,1,0:T(8,128)(2,1)S(1)}, bf16[4,198,256]{2,1,0:T(8,128)(2,1)S(1)}, u32[]{:S(2)}, u32[]{:S(2)}) collective-permute-start(bf16[4,198,256]{2,1,0:T(8,128)(2,1)S(1)} %get-tuple-element.60), channel_id=1, source_target_pairs={{0,4},{4,0},{1,5},{5,1},{2,6},{6,2},{3,7},{7,3},{8,12},{12,8},{9,1... | collective-permute-start | bytes 1216520 | tf_op jit(solution)/shard_map/ppermute | solution.py:56
  86.0 5.5 %collective-permute-done.28 = bf16[4,198,256]{2,1,0:T(8,128)(2,1)S(1)} collective-permute-done((bf16[4,198,256]{2,1,0:T(8,128)(2,1)S(1)}, bf16[4,198,256]{2,1,0:T(8,128)(2,1)S(1)}, u32[]{:S(2)}, u32[]{:S(2)}) %collective-permute-start.28) | collective-permute-done | bytes 405536 | tf_op jit(solution)/shard_map/ppermute | solution.py:167
  91.5 4.3 %collective-permute-done.30 = bf16[4,198,256]{2,1,0:T(8,128)(2,1)S(1)} collective-permute-done((bf16[4,198,256]{2,1,0:T(8,128)(2,1)S(1)}, bf16[4,198,256]{2,1,0:T(8,128)(2,1)S(1)}, u32[]{:S(2)}, u32[]{:S(2)}) %collective-permute-start.30) | collective-permute-done | bytes 405536 | tf_op jit(solution)/shard_map/ppermute | solution.py:167
  106.1 2.2 %shard_map.78.refs_6_.refs_1_ = bf16[256,8192]{1,0:T(8,128)(2,1)S(1)} custom-call(bf16[512,8192]{1,0:T(8,128)(2,1)} %bitcast.58, bf16[4,198,256]{2,1,0:T(8,128)(2,1)S(1)} %add_convert_fusion.5.rest_0_), custom_call_target="tpu_custom_call" | custom-call | bytes 4194304 | tf_op jit(solution)/shard_map/pallas_call | solution.py:83
  110.3 2.5 %collective-permute-done.36.refs_1_ = bf16[198,256]{1,0:T(8,128)(2,1)S(1)} collective-permute-done((bf16[198,256]{1,0:T(8,128)(2,1)S(1)}, bf16[198,256]{1,0:T(8,128)(2,1)S(1)}, u32[]{:S(2)}, u32[]{:S(2)}) %collective-permute-start.36) | collective-permute-done | bytes 101408 | tf_op jit(solution)/shard_map/ppermute | solution.py:177
  120.5 2.2 %collective-permute-done.49 = bf16[198,198]{1,0:T(8,128)(2,1)S(1)} collective-permute-done((bf16[198,198]{1,0:T(8,128)(2,1)S(1)}, bf16[198,198]{1,0:T(8,128)(2,1)S(1)}, u32[]{:S(2)}, u32[]{:S(2)}) %collective-permute-start.49) | collective-permute-done | bytes 78440 | tf_op jit(solution)/shard_map/ppermute | solution.py:177
  129.0 4.3 %collective-permute-done.43 = bf16[4,198,256]{2,1,0:T(8,128)(2,1)S(1)} collective-permute-done((bf16[4,198,256]{2,1,0:T(8,128)(2,1)S(1)}, bf16[4,198,256]{2,1,0:T(8,128)(2,1)S(1)}, u32[]{:S(2)}, u32[]{:S(2)}) %collective-permute-start.43) | collective-permute-done | bytes 405536 | tf_op jit(solution)/shard_map/ppermute | solution.py:167
  137.1 2.8 %collective-permute-done.50 = bf16[2,198,256]{2,1,0:T(8,128)(2,1)S(1)} collective-permute-done((bf16[2,198,256]{2,1,0:T(8,128)(2,1)S(1)}, bf16[2,198,256]{2,1,0:T(8,128)(2,1)S(1)}, u32[]{:S(2)}, u32[]{:S(2)}) %collective-permute-start.50) | collective-permute-done | bytes 202784 | tf_op jit(solution)/shard_map/ppermute | solution.py:172
  140.0 2.4 %collective-permute-done.51 = bf16[2,198,256]{2,1,0:T(8,128)(2,1)S(1)} collective-permute-done((bf16[2,198,256]{2,1,0:T(8,128)(2,1)S(1)}, bf16[2,198,256]{2,1,0:T(8,128)(2,1)S(1)}, u32[]{:S(2)}, u32[]{:S(2)}) %collective-permute-start.51) | collective-permute-done | bytes 202784 | tf_op jit(solution)/shard_map/ppermute | solution.py:172
  149.1 5.3 %collective-permute-start.56 = (f32[198,198]{1,0:T(8,128)S(1)}, f32[198,198]{1,0:T(8,128)S(1)}, u32[]{:S(2)}, u32[]{:S(2)}) collective-permute-start(f32[198,198]{1,0:T(8,128)S(1)} %convert_add_fusion.3.own), channel_id=1, source_target_pairs={{0,4},{4,0},{1,5},{5,1},{2,6},{6,2},{3,7},{7,3},{8,12},{12,8},{9,1... | collective-permute-start | bytes 470456 | tf_op jit(solution)/shard_map/ppermute | solution.py:56
  156.4 2.6 %collective-permute-start.57 = (bf16[198,256]{1,0:T(8,128)(2,1)S(1)}, bf16[198,256]{1,0:T(8,128)(2,1)S(1)}, u32[]{:S(2)}, u32[]{:S(2)}) collective-permute-start(bf16[198,256]{1,0:T(8,128)(2,1)S(1)} %get-tuple-element.91.a), channel_id=1, source_target_pairs={{0,2},{1,3},{2,0},{3,1},{4,6},{5,7},{6,4},{7,5},{8,10},{9,11},{10,... | collective-permute-start | bytes 304136 | tf_op jit(solution)/shard_map/ppermute | solution.py:342
  (161 shorter events, 84.5 us)
Async XLA Ops:
  6.6 10.9 %collective-permute-start = (bf16[4,198,256]{2,1,0:T(8,128)(2,1)S(1)}, bf16[4,198,256]{2,1,0:T(8,128)(2,1)S(1)}, u32[]{:S(2)}, u32[]{:S(2)}) collective-permute-start(bf16[4,198,256]{2,1,0:T(8,128)(2,1)S(1)} %get-tuple-element.40), channel_id=1, source_target_pairs={{0,4},{4,0},{1,5},{5,1},{2,6},{6,2},{3,7},{7,3},{8,12},{12,8},{9,1... | collective-permute-start | bytes 1216520 | tf_op jit(solution)/shard_map/ppermute | solution.py:56
  8.0 9.5 %collective-permute-start.2 = (bf16[4,198,256]{2,1,0:T(8,128)(2,1)S(1)}, bf16[4,198,256]{2,1,0:T(8,128)(2,1)S(1)}, u32[]{:S(2)}, u32[]{:S(2)}) collective-permute-start(bf16[4,198,256]{2,1,0:T(8,128)(2,1)S(1)} %add_convert_fusion.18), channel_id=1, source_target_pairs={{0,16},{4,68},{8,24},{12,76},{16,0},{20,84},{24,8},{28,92},{32,48}... | collective-permute-start | bytes 1216520 | tf_op jit(solution)/shard_map/ppermute | solution.py:167
  11.2 9.9 %collective-permute-start.4 = (bf16[4,198,256]{2,1,0:T(8,128)(2,1)S(1)}, bf16[4,198,256]{2,1,0:T(8,128)(2,1)S(1)}, u32[]{:S(2)}, u32[]{:S(2)}) collective-permute-start(bf16[4,198,256]{2,1,0:T(8,128)(2,1)S(1)} %add_convert_fusion.17), channel_id=1, source_target_pairs={{0,8},{4,36},{8,16},{12,44},{16,24},{20,52},{24,0},{28,60},{32,40}... | collective-permute-start | bytes 1216520 | tf_op jit(solution)/shard_map/ppermute | solution.py:167
  11.8 9.7 %collective-permute-start.6 = (bf16[4,198,256]{2,1,0:T(8,128)(2,1)S(1)}, bf16[4,198,256]{2,1,0:T(8,128)(2,1)S(1)}, u32[]{:S(2)}, u32[]{:S(2)}) collective-permute-start(bf16[4,198,256]{2,1,0:T(8,128)(2,1)S(1)} %add_convert_fusion.16.near), channel_id=1, source_target_pairs={{0,24},{4,100},{8,0},{12,108},{16,8},{20,116},{24,16},{28,124},{32... | collective-permute-start | bytes 1216520 | tf_op jit(solution)/shard_map/ppermute | solution.py:167
  30.3 6.7 %collective-permute-start.12 = (bf16[198,256]{1,0:T(8,128)(2,1)S(1)}, bf16[198,256]{1,0:T(8,128)(2,1)S(1)}, u32[]{:S(2)}, u32[]{:S(2)}) collective-permute-start(bf16[198,256]{1,0:T(8,128)(2,1)S(1)} %fusion.8.refs_0_), channel_id=1, source_target_pairs={{0,3},{1,0},{2,1},{3,2},{4,7},{5,4},{6,5},{7,6},{8,11},{9,8},{10,9... | collective-permute-start | bytes 304136 | tf_op jit(solution)/shard_map/ppermute | solution.py:177
  34.1 5.8 %collective-permute-start.10 = (bf16[198,256]{1,0:T(8,128)(2,1)S(1)}, bf16[198,256]{1,0:T(8,128)(2,1)S(1)}, u32[]{:S(2)}, u32[]{:S(2)}) collective-permute-start(bf16[198,256]{1,0:T(8,128)(2,1)S(1)} %fusion.8.refs_0_), channel_id=1, source_target_pairs={{0,1},{1,2},{2,3},{3,0},{4,5},{5,6},{6,7},{7,4},{8,9},{9,10},{10,1... | collective-permute-start | bytes 304136 | tf_op jit(solution)/shard_map/ppermute | solution.py:177
  41.5 6.1 %collective-permute-start.14 = (bf16[4,198,256]{2,1,0:T(8,128)(2,1)S(1)}, bf16[4,198,256]{2,1,0:T(8,128)(2,1)S(1)}, u32[]{:S(2)}, u32[]{:S(2)}) collective-permute-start(bf16[4,198,256]{2,1,0:T(8,128)(2,1)S(1)} %get-tuple-element.51), channel_id=1, source_target_pairs={{0,4},{4,0},{1,5},{5,1},{2,6},{6,2},{3,7},{7,3},{8,12},{12,8},{9,1... | collective-permute-start | bytes 1216520 | tf_op jit(solution)/shard_map/ppermute | solution.py:56
  47.7 8.9 %collective-permute-start.15 = (bf16[4,198,256]{2,1,0:T(8,128)(2,1)S(1)}, bf16[4,198,256]{2,1,0:T(8,128)(2,1)S(1)}, u32[]{:S(2)}, u32[]{:S(2)}) collective-permute-start(bf16[4,198,256]{2,1,0:T(8,128)(2,1)S(1)} %add_convert_fusion.13), channel_id=1, source_target_pairs={{0,16},{4,68},{8,24},{12,76},{16,0},{20,84},{24,8},{28,92},{32,48}... | collective-permute-start | bytes 1216520 | tf_op jit(solution)/shard_map/ppermute | solution.py:167
  48.8 12.2 %collective-permute-start.17 = (bf16[4,198,256]{2,1,0:T(8,128)(2,1)S(1)}, bf16[4,198,256]{2,1,0:T(8,128)(2,1)S(1)}, u32[]{:S(2)}, u32[]{:S(2)}) collective-permute-start(bf16[4,198,256]{2,1,0:T(8,128)(2,1)S(1)} %add_convert_fusion.12), channel_id=1, source_target_pairs={{0,8},{4,36},{8,16},{12,44},{16,24},{20,52},{24,0},{28,60},{32,40}... | collective-permute-start | bytes 1216520 | tf_op jit(solution)/shard_map/ppermute | solution.py:167
  49.8 11.2 %collective-permute-start.19 = (bf16[4,198,256]{2,1,0:T(8,128)(2,1)S(1)}, bf16[4,198,256]{2,1,0:T(8,128)(2,1)S(1)}, u32[]{:S(2)}, u32[]{:S(2)}) collective-permute-start(bf16[4,198,256]{2,1,0:T(8,128)(2,1)S(1)} %add_convert_fusion.11), channel_id=1, source_target_pairs={{0,24},{4,100},{8,0},{12,108},{16,8},{20,116},{24,16},{28,124},{32... | collective-permute-start | bytes 1216520 | tf_op jit(solution)/shard_map/ppermute | solution.py:167
  82.7 8.7 %collective-permute-start.28 = (bf16[4,198,256]{2,1,0:T(8,128)(2,1)S(1)}, bf16[4,198,256]{2,1,0:T(8,128)(2,1)S(1)}, u32[]{:S(2)}, u32[]{:S(2)}) collective-permute-start(bf16[4,198,256]{2,1,0:T(8,128)(2,1)S(1)} %add_convert_fusion.8), channel_id=1, source_target_pairs={{0,16},{4,68},{8,24},{12,76},{16,0},{20,84},{24,8},{28,92},{32,48}... | collective-permute-start | bytes 1216520 | tf_op jit(solution)/shard_map/ppermute | solution.py:167
  83.0 12.8 %collective-permute-start.30 = (bf16[4,198,256]{2,1,0:T(8,128)(2,1)S(1)}, bf16[4,198,256]{2,1,0:T(8,128)(2,1)S(1)}, u32[]{:S(2)}, u32[]{:S(2)}) collective-permute-start(bf16[4,198,256]{2,1,0:T(8,128)(2,1)S(1)} %add_convert_fusion.7), channel_id=1, source_target_pairs={{0,8},{4,36},{8,16},{12,44},{16,24},{20,52},{24,0},{28,60},{32,40}... | collective-permute-start | bytes 1216520 | tf_op jit(solution)/shard_map/ppermute | solution.py:167
  84.2 11.6 %collective-permute-start.32 = (bf16[4,198,256]{2,1,0:T(8,128)(2,1)S(1)}, bf16[4,198,256]{2,1,0:T(8,128)(2,1)S(1)}, u32[]{:S(2)}, u32[]{:S(2)}) collective-permute-start(bf16[4,198,256]{2,1,0:T(8,128)(2,1)S(1)} %add_convert_fusion.6), channel_id=1, source_target_pairs={{0,24},{4,100},{8,0},{12,108},{16,8},{20,116},{24,16},{28,124},{32... | collective-permute-start | bytes 1216520 | tf_op jit(solution)/shard_map/ppermute | solution.py:167
  105.8 7.0 %collective-permute-start.36 = (bf16[198,256]{1,0:T(8,128)(2,1)S(1)}, bf16[198,256]{1,0:T(8,128)(2,1)S(1)}, u32[]{:S(2)}, u32[]{:S(2)}) collective-permute-start(bf16[198,256]{1,0:T(8,128)(2,1)S(1)} %fusion.2.refs_0_), channel_id=1, source_target_pairs={{0,1},{1,2},{2,3},{3,0},{4,5},{5,6},{6,7},{7,4},{8,9},{9,10},{10,1... | collective-permute-start | bytes 304136 | tf_op jit(solution)/shard_map/ppermute | solution.py:177
  116.1 11.6 %collective-permute-start.39 = (bf16[4,198,256]{2,1,0:T(8,128)(2,1)S(1)}, bf16[4,198,256]{2,1,0:T(8,128)(2,1)S(1)}, u32[]{:S(2)}, u32[]{:S(2)}) collective-permute-start(bf16[4,198,256]{2,1,0:T(8,128)(2,1)S(1)} %get-tuple-element.67), channel_id=1, source_target_pairs={{0,4},{4,0},{1,5},{5,1},{2,6},{6,2},{3,7},{7,3},{8,12},{12,8},{9,1... | collective-permute-start | bytes 1216520 | tf_op jit(solution)/shard_map/ppermute | solution.py:56
  119.9 7.8 %collective-permute-start.47 = (bf16[198,198]{1,0:T(8,128)(2,1)S(1)}, bf16[198,198]{1,0:T(8,128)(2,1)S(1)}, u32[]{:S(2)}, u32[]{:S(2)}) collective-permute-start(bf16[198,198]{1,0:T(8,128)(2,1)S(1)} %add_convert_fusion.22), channel_id=1, source_target_pairs={{0,1},{1,2},{2,3},{3,0},{4,5},{5,6},{6,7},{7,4},{8,9},{9,10},{10,1... | collective-permute-start | bytes 235232 | tf_op jit(solution)/shard_map/ppermute | solution.py:177
  120.2 8.7 %collective-permute-start.41 = (bf16[4,198,256]{2,1,0:T(8,128)(2,1)S(1)}, bf16[4,198,256]{2,1,0:T(8,128)(2,1)S(1)}, u32[]{:S(2)}, u32[]{:S(2)}) collective-permute-start(bf16[4,198,256]{2,1,0:T(8,128)(2,1)S(1)} %add_convert_fusion.3), channel_id=1, source_target_pairs={{0,16},{4,68},{8,24},{12,76},{16,0},{20,84},{24,8},{28,92},{32,48}... | collective-permute-start | bytes 1216520 | tf_op jit(solution)/shard_map/ppermute | solution.py:167
  122.8 10.5 %collective-permute-start.43 = (bf16[4,198,256]{2,1,0:T(8,128)(2,1)S(1)}, bf16[4,198,256]{2,1,0:T(8,128)(2,1)S(1)}, u32[]{:S(2)}, u32[]{:S(2)}) collective-permute-start(bf16[4,198,256]{2,1,0:T(8,128)(2,1)S(1)} %add_convert_fusion.2), channel_id=1, source_target_pairs={{0,8},{4,36},{8,16},{12,44},{16,24},{20,52},{24,0},{28,60},{32,40}... | collective-permute-start | bytes 1216520 | tf_op jit(solution)/shard_map/ppermute | solution.py:167
  124.7 8.6 %collective-permute-start.45 = (bf16[4,198,256]{2,1,0:T(8,128)(2,1)S(1)}, bf16[4,198,256]{2,1,0:T(8,128)(2,1)S(1)}, u32[]{:S(2)}, u32[]{:S(2)}) collective-permute-start(bf16[4,198,256]{2,1,0:T(8,128)(2,1)S(1)} %add_convert_fusion.1), channel_id=1, source_target_pairs={{0,24},{4,100},{8,0},{12,108},{16,8},{20,116},{24,16},{28,124},{32... | collective-permute-start | bytes 1216520 | tf_op jit(solution)/shard_map/ppermute | solution.py:167
  133.7 6.3 %collective-permute-start.50 = (bf16[2,198,256]{2,1,0:T(8,128)(2,1)S(1)}, bf16[2,198,256]{2,1,0:T(8,128)(2,1)S(1)}, u32[]{:S(2)}, u32[]{:S(2)}) collective-permute-start(bf16[2,198,256]{2,1,0:T(8,128)(2,1)S(1)} %get-tuple-element.93), channel_id=1, source_target_pairs={{4,20},{0,64},{12,28},{8,72},{20,4},{16,80},{28,12},{24,88},{36,52... | collective-permute-start | bytes 608264 | tf_op jit(solution)/shard_map/ppermute | solution.py:172
  134.5 7.9 %collective-permute-start.51 = (bf16[2,198,256]{2,1,0:T(8,128)(2,1)S(1)}, bf16[2,198,256]{2,1,0:T(8,128)(2,1)S(1)}, u32[]{:S(2)}, u32[]{:S(2)}) collective-permute-start(bf16[2,198,256]{2,1,0:T(8,128)(2,1)S(1)} %get-tuple-element.94), channel_id=1, source_target_pairs={{4,12},{0,32},{12,20},{8,40},{20,28},{16,48},{28,4},{24,56},{36,44... | collective-permute-start | bytes 608264 | tf_op jit(solution)/shard_map/ppermute | solution.py:172
  135.7 6.6 %collective-permute-start.52 = (bf16[2,198,256]{2,1,0:T(8,128)(2,1)S(1)}, bf16[2,198,256]{2,1,0:T(8,128)(2,1)S(1)}, u32[]{:S(2)}, u32[]{:S(2)}) collective-permute-start(bf16[2,198,256]{2,1,0:T(8,128)(2,1)S(1)} %get-tuple-element.95), channel_id=1, source_target_pairs={{4,28},{0,96},{12,4},{8,104},{20,12},{16,112},{28,20},{24,120},{36... | collective-permute-start | bytes 608264 | tf_op jit(solution)/shard_map/ppermute | solution.py:172
  149.1 9.9 %collective-permute-start.56 = (f32[198,198]{1,0:T(8,128)S(1)}, f32[198,198]{1,0:T(8,128)S(1)}, u32[]{:S(2)}, u32[]{:S(2)}) collective-permute-start(f32[198,198]{1,0:T(8,128)S(1)} %convert_add_fusion.3.own), channel_id=1, source_target_pairs={{0,4},{4,0},{1,5},{5,1},{2,6},{6,2},{3,7},{7,3},{8,12},{12,8},{9,1... | collective-permute-start | bytes 470456 | tf_op jit(solution)/shard_map/ppermute | solution.py:56
  156.4 7.4 %collective-permute-start.57 = (bf16[198,256]{1,0:T(8,128)(2,1)S(1)}, bf16[198,256]{1,0:T(8,128)(2,1)S(1)}, u32[]{:S(2)}, u32[]{:S(2)}) collective-permute-start(bf16[198,256]{1,0:T(8,128)(2,1)S(1)} %get-tuple-element.91.a), channel_id=1, source_target_pairs={{0,2},{1,3},{2,0},{3,1},{4,6},{5,7},{6,4},{7,5},{8,10},{9,11},{10,... | collective-permute-start | bytes 304136 | tf_op jit(solution)/shard_map/ppermute | solution.py:342
  (39 other events, 184.4 us)
